TPU v7x, 32 devices: a whole 2x2x4 slice. The times are simulated.
32 devices in a mesh: seq: 8 (over z, x), ch: 4 (over y, core).
Axes of the slice: x: 2, y: 2, z: 4, core: 2. Of those that a mesh axis runs over, the one named last changes fastest.
Arguments:
- features: float32 [1536, 4096], P('ch', 'seq'), may hold values from -6 to 6
- gain_one: float32 [1536], P('ch'), may hold values from 0.5 to 2
- shift_one: float32 [1536], P('ch'), may hold values from -1 to 1
- wide_one: float32 [5, 1536, 1536], P(None, 'ch'), may hold values from -0.0625 to 0.0625
- gain_two: float32 [1536], P('ch'), may hold values from 0.5 to 2
- shift_two: float32 [1536], P('ch'), may hold values from -1 to 1
- wide_two: float32 [5, 1536, 1536], P(None, 'ch'), may hold values from -0.0625 to 0.0625
Outputs:
- regrouped: float32 [8, 384, 512], P('seq', 'ch')
All inputs are finite; a program needn't handle non-finite values.
Results may differ from a plain program's by a relative error of at most 0.0001.
Values sent between devices are 32-bit elements; how exact they have to be, the bound alone decides.
No kernel may reach another device: no remote copies, remote signals or barrier semaphores. Data moves between devices by JAX's collectives and lax.ppermute only.
A program may use at most 128 MiB of HBM per device.

v0:
```python
import jax
import jax.numpy as jnp
from jax import lax
from jax.sharding import PartitionSpec as P

KW = 5
GROUP = 4


def extended_2(cells, sides, width):
    for axis, dim in sides:
        count = lax.axis_size(axis)
        ends = count - 1
        head = lax.slice_in_dim(cells, 0, width, axis=dim)
        tail = lax.slice_in_dim(cells, cells.shape[dim] - width, cells.shape[dim], axis=dim)
        cells = jnp.concatenate(
            [
                lax.ppermute(tail, axis, [(i, (i + 1) % count) for i in range(ends)]),
                cells,
                lax.ppermute(head, axis, [((i + 1) % count, i) for i in range(ends)]),
            ],
            axis=dim,
        )
    return cells


def partner(block, axis, apart):
    count = lax.axis_size(axis)
    route = []
    for low in range(count):
        high = low | 1 << apart
        if high != low and high < count:
            route += [(low, high), (high, low)]
    return lax.ppermute(block, axis, route)


def activate(values, gain, offset):
    return jax.nn.gelu(values * gain[:, None] + offset[:, None], approximate=False)


def pool_pairs(values):
    return jnp.max(values.reshape(values.shape[0], values.shape[1] // 2, 2), axis=2)


def tap_stack(extended):
    length = extended.shape[1] - (KW - 1)
    return jnp.stack([extended[:, kernel_tap : kernel_tap + length] for kernel_tap in range(KW)])


def make_term(stacked, weight):
    return lax.dot_general(
        weight,
        stacked,
        (((0, 1), (0, 1)), ((), ())),
        precision=lax.Precision.HIGHEST,
        preferred_element_type=jnp.float32,
    )


def body(features, gain_one, shift_one, wide_one, gain_two, shift_two, wide_two):
    seq_pos = lax.axis_index("seq")
    active_one = activate(features, gain_one, shift_one)
    extended = extended_2(active_one, (("seq", 1),), 2)
    conv_one = lax.psum_scatter(
        make_term(tap_stack(extended), wide_one), "ch", scatter_dimension=0, tiled=True
    )
    pooled_one = pool_pairs(conv_one)
    active_two = activate(pooled_one, gain_two, shift_two)
    second_ext = extended_2(active_two, (("seq", 1),), 2)
    conv_two = lax.psum_scatter(
        make_term(tap_stack(second_ext), wide_two), "ch", scatter_dimension=0, tiled=True
    )
    pooled_two = pool_pairs(conv_two)
    local_chan = pooled_two.shape[0]
    part_chan = local_chan // GROUP
    quarter = pooled_two.shape[1]
    pieces = pooled_two.reshape(GROUP, part_chan, quarter)
    member = seq_pos % GROUP
    bit_total = GROUP.bit_length() - 1
    bit_order = list(range(bit_total))
    buffer = pieces
    for bit_pos in bit_order:
        low = 1 << bit_pos
        viewed = buffer.reshape(GROUP // (2 * low), 2, low, part_chan, quarter)
        lower_half = viewed[:, 0]
        upper_half = viewed[:, 1]
        my_bit = member // low % 2
        outgoing = jnp.where(my_bit == 0, upper_half, lower_half)
        arrived = partner(outgoing, "seq", bit_pos)
        new_lower = jnp.where(my_bit == 0, lower_half, arrived)
        new_upper = jnp.where(my_bit == 0, arrived, upper_half)
        buffer = jnp.stack([new_lower, new_upper], axis=1).reshape(GROUP, part_chan, quarter)
    result = jnp.transpose(buffer, (1, 0, 2)).reshape(part_chan, GROUP * quarter)
    return result[None]


def solution(mesh):
    return jax.shard_map(
        body,
        mesh=mesh,
        in_specs=(
            P("ch", "seq"),
            P("ch"),
            P("ch"),
            P(None, "ch", None),
            P("ch"),
            P("ch"),
            P(None, "ch", None),
        ),
        out_specs=P("seq", "ch", None),
        check_vma=False,
    )
```

profile of v0, /device:TPU:0, one launch (start us, length us, event | category | flops | bytes accessed | tf_op | source)
XLA Modules:
  0.0 157.5 jit_solution(14076554023783912147)
XLA Ops:
  6.5 1.4 copy.15
  8.0 2.4 %fusion.7 = f32[384,512]{0,1:T(8,128)S(1)} fusion(f32[384,512]{0,1:T(8,128)S(1)} %copy.15, f32[384]{0:T(512)} %param.9, f32[384]{0:T(512)} %param.8), kind=kLoop, calls=%fused_computation.14 | loop fusion | flops 12976128 | bytes 1575936 | tf_op jit(solution)/shard_map/mul | solution.py:38
  10.4 4.8 %collective-permute-start = (f32[384,2]{0,1:T(2,128)S(1)}, f32[384,2]{0,1:T(2,128)S(1)}, u32[]{:S(2)}, u32[]{:S(2)}) collective-permute-start(f32[384,2]{0,1:T(2,128)S(1)} %get-tuple-element.6), channel_id=1, source_target_pairs={{0,4},{4,8},{8,12},{12,16},{16,20},{20,24},{24,28},{1,5},{5,9},{9,... | collective-permute-start | bytes 9224 | tf_op jit(solution)/shard_map/ppermute | solution.py:18
  15.2 1.3 collective-permute-start.1
  16.7 1.7 %bitcast_dynamic-update-slice_fusion = f32[5,384,512]{1,2,0:T(8,128)S(1)} fusion(f32[5,384,512]{1,2,0:T(8,128)S(1)} %fusion.11, f32[384]{0:T(512)S(1)} %copy-done, f32[384,512]{0,1:T(8,128)S(1)} %copy.15, f32[384]{0:T(512)S(1)} %copy-done.1), kind=kLoop, calls=%fused_computation.21 | loop fusion | flops 12976128 | bytes 1576960
  18.4 2.3 %collective-permute-done.1 = f32[384,2]{0,1:T(2,128)S(1)} collective-permute-done((f32[384,2]{0,1:T(2,128)S(1)}, f32[384,2]{0,1:T(2,128)S(1)}, u32[]{:S(2)}, u32[]{:S(2)}) %collective-permute-start.1) | collective-permute-done | bytes 3104 | tf_op jit(solution)/shard_map/ppermute | solution.py:20
  20.9 23.6 %convolution_bitcast_fusion = f32[1536,512]{0,1:T(8,128)} fusion(f32[5,384,512]{1,2,0:T(8,128)S(1)} %fusion.9, f32[5,384,1536]{2,1,0:T(8,128)} %param.10), kind=kOutput, calls=%fused_computation | convolution fusion | flops 18119393280 | bytes 18874368 | tf_op jit(solution)/shard_map/dot_general | solution.py:51
  44.7 39.1 %reduce-scatter.3.cloned.1.call-done = f32[384,512]{0,1:T(8,128)} async-done(((f32[1536,512]{0,1:T(8,128)}), f32[384,512]{0,1:T(8,128)}) %reduce-scatter.3.cloned.1.call-update) | async-done | bytes 786448 | tf_op jit(solution)/shard_map/reduce_scatter | solution.py:64
  83.8 1.6 %reshape.290 = f32[384,256,2]{0,2,1:T(2,128)S(1)} reshape(f32[384,512]{0,1:T(8,128)} %reduce-scatter.3.cloned.1.call-done) | data formatting | bytes 1572864 | tf_op jit(solution)/shard_map/reshape | solution.py:42
  85.4 0.9 reduce_max.20
  86.3 0.9 fusion.26
  87.2 3.4 %collective-permute-start.2 = (f32[384,2]{0,1:T(2,128)S(1)}, f32[384,2]{0,1:T(2,128)S(1)}, u32[]{:S(2)}, u32[]{:S(2)}) collective-permute-start(f32[384,2]{0,1:T(2,128)S(1)} %get-tuple-element.8), channel_id=1, source_target_pairs={{0,4},{4,8},{8,12},{12,16},{16,20},{20,24},{24,28},{1,5},{5,9},{9,... | collective-permute-start | bytes 9224 | tf_op jit(solution)/shard_map/ppermute | solution.py:18
  90.6 1.3 collective-permute-start.3
  92.0 0.9 fusion.29
  92.9 3.2 %collective-permute-done.3 = f32[384,2]{0,1:T(2,128)S(1)} collective-permute-done((f32[384,2]{0,1:T(2,128)S(1)}, f32[384,2]{0,1:T(2,128)S(1)}, u32[]{:S(2)}, u32[]{:S(2)}) %collective-permute-start.3) | collective-permute-done | bytes 3104 | tf_op jit(solution)/shard_map/ppermute | solution.py:20
  96.2 13.9 %convolution_bitcast_fusion.1 = f32[1536,256]{0,1:T(8,128)} fusion(f32[5,384,256]{1,2,0:T(8,128)S(1)} %fusion.31, f32[5,384,1536]{2,1,0:T(8,128)} %param.13), kind=kOutput, calls=%fused_computation.1 | convolution fusion | flops 9059696640 | bytes 15335424 | tf_op jit(solution)/shard_map/dot_general | solution.py:51
  110.2 28.3 %reduce-scatter.5.cloned.1.call-done = f32[384,256]{0,1:T(8,128)} async-done(((f32[1536,256]{0,1:T(8,128)}), f32[384,256]{0,1:T(8,128)}) %reduce-scatter.5.cloned.1.call-update) | async-done | bytes 393232 | tf_op jit(solution)/shard_map/reduce_scatter | solution.py:70
  138.5 1.2 reshape.291
  139.7 0.5 reduce_max.22
  140.3 1.5 collective-permute-start.4
  141.8 3.1 %collective-permute-done.4 = f32[2,1,96,128]{3,2,0,1:T(8,128)S(1)} collective-permute-done((f32[2,1,96,128]{3,2,0,1:T(8,128)S(1)}, f32[2,1,96,128]{3,2,0,1:T(8,128)S(1)}, u32[]{:S(2)}, u32[]{:S(2)}) %collective-permute-start.4) | collective-permute-done | bytes 98336 | tf_op jit(solution)/shard_map/ppermute | solution.py:34
  145.1 1.5 collective-permute-start.5
  146.6 3.1 %collective-permute-done.5 = f32[1,2,96,128]{3,2,1,0:T(8,128)S(1)} collective-permute-done((f32[1,2,96,128]{3,2,1,0:T(8,128)S(1)}, f32[1,2,96,128]{3,2,1,0:T(8,128)S(1)}, u32[]{:S(2)}, u32[]{:S(2)}) %collective-permute-start.5) | collective-permute-done | bytes 98336 | tf_op jit(solution)/shard_map/ppermute | solution.py:34
  149.9 0.8 broadcast_in_dim_reshape.3
  (32 shorter events, 1.0 us)
Async XLA Ops:
  6.5 10.1 %copy-start = (f32[384]{0:T(512)S(1)}, f32[384]{0:T(512)}, u32[]{:S(2)}) copy-start(f32[384]{0:T(512)} %param.9) | copy-start | bytes 4612
  6.5 10.2 %copy-start.1 = (f32[384]{0:T(512)S(1)}, f32[384]{0:T(512)}, u32[]{:S(2)}) copy-start(f32[384]{0:T(512)} %param.8) | copy-start | bytes 4612
  6.5 77.3 %reduce-scatter.3.cloned.1.call-start = ((), (), s32[]{:S(2)}) async-start(), calls=%async_computation.2 | async-start | bytes 3932160 | tf_op jit(solution)/shard_map/reduce_scatter | solution.py:64
  10.4 6.2 %collective-permute-start = (f32[384,2]{0,1:T(2,128)S(1)}, f32[384,2]{0,1:T(2,128)S(1)}, u32[]{:S(2)}, u32[]{:S(2)}) collective-permute-start(f32[384,2]{0,1:T(2,128)S(1)} %get-tuple-element.6), channel_id=1, source_target_pairs={{0,4},{4,8},{8,12},{12,16},{16,20},{20,24},{24,28},{1,5},{5,9},{9,... | collective-permute-start | bytes 9224 | tf_op jit(solution)/shard_map/ppermute | solution.py:18
  15.2 5.5 %collective-permute-start.1 = (f32[384,2]{0,1:T(2,128)S(1)}, f32[384,2]{0,1:T(2,128)S(1)}, u32[]{:S(2)}, u32[]{:S(2)}) collective-permute-start(f32[384,2]{0,1:T(2,128)S(1)} %get-tuple-element.5), channel_id=1, source_target_pairs={{4,0},{8,4},{12,8},{16,12},{20,16},{24,20},{28,24},{5,1},{9,5},{13... | collective-permute-start | bytes 9224 | tf_op jit(solution)/shard_map/ppermute | solution.py:20
  44.5 41.9 %copy-start.2 = (f32[384]{0:T(512)S(1)}, f32[384]{0:T(512)}, u32[]{:S(2)}) copy-start(f32[384]{0:T(512)} %param.12) | copy-start | bytes 4612
  44.5 41.9 %copy-start.3 = (f32[384]{0:T(512)S(1)}, f32[384]{0:T(512)}, u32[]{:S(2)}) copy-start(f32[384]{0:T(512)} %param.11) | copy-start | bytes 4612
  44.5 94.0 %reduce-scatter.5.cloned.1.call-start = ((), (), s32[]{:S(2)}) async-start(), calls=%async_computation.3 | async-start | bytes 1966080 | tf_op jit(solution)/shard_map/reduce_scatter | solution.py:70
  87.2 4.7 %collective-permute-start.2 = (f32[384,2]{0,1:T(2,128)S(1)}, f32[384,2]{0,1:T(2,128)S(1)}, u32[]{:S(2)}, u32[]{:S(2)}) collective-permute-start(f32[384,2]{0,1:T(2,128)S(1)} %get-tuple-element.8), channel_id=1, source_target_pairs={{0,4},{4,8},{8,12},{12,16},{16,20},{20,24},{24,28},{1,5},{5,9},{9,... | collective-permute-start | bytes 9224 | tf_op jit(solution)/shard_map/ppermute | solution.py:18
  90.6 5.5 %collective-permute-start.3 = (f32[384,2]{0,1:T(2,128)S(1)}, f32[384,2]{0,1:T(2,128)S(1)}, u32[]{:S(2)}, u32[]{:S(2)}) collective-permute-start(f32[384,2]{0,1:T(2,128)S(1)} %get-tuple-element.7), channel_id=1, source_target_pairs={{4,0},{8,4},{12,8},{16,12},{20,16},{24,20},{28,24},{5,1},{9,5},{13... | collective-permute-start | bytes 9224 | tf_op jit(solution)/shard_map/ppermute | solution.py:20
  140.3 4.7 %collective-permute-start.4 = (f32[2,1,96,128]{3,2,0,1:T(8,128)S(1)}, f32[2,1,96,128]{3,2,0,1:T(8,128)S(1)}, u32[]{:S(2)}, u32[]{:S(2)}) collective-permute-start(f32[2,1,96,128]{3,2,0,1:T(8,128)S(1)} %fusion.49), channel_id=1, source_target_pairs={{0,4},{4,0},{8,12},{12,8},{16,20},{20,16},{24,28},{28,24},{1,5},{5... | collective-permute-start | bytes 294920 | tf_op jit(solution)/shard_map/ppermute | solution.py:34
  145.1 4.7 %collective-permute-start.5 = (f32[1,2,96,128]{3,2,1,0:T(8,128)S(1)}, f32[1,2,96,128]{3,2,1,0:T(8,128)S(1)}, u32[]{:S(2)}, u32[]{:S(2)}) collective-permute-start(f32[1,2,96,128]{3,2,1,0:T(8,128)S(1)} %fusion.50), channel_id=1, source_target_pairs={{0,8},{8,0},{4,12},{12,4},{16,24},{24,16},{20,28},{28,20},{1,9},{9... | collective-permute-start | bytes 294920 | tf_op jit(solution)/shard_map/ppermute | solution.py:34
Sparse Core Ops, SparseCore 0:
  44.6 39.1 reduce-scatter.2
  110.3 28.1 reduce-scatter.4
where the time goes:
time: 158 us
  waiting for transfers between devices  79.2 us (50%)
  matrix products  37.6 us (24%)
  starting transfers between devices  14.1 us (9%)
  between operations  13.7 us (9%)
  other arithmetic  7.67 us (5%)
  local copies, waits for them, and re-layouts  5.27 us (3%)
    reduce_scatter x1, waiting for transfers between devices, body(): lax.psum_scatter(make_term(tap_stack(extended), wide_one), 'ch', scatter_...  39.1 us
    dot_general x2, matrix products, make_term(): lax.dot_general(weight, stacked, (((0, 1), (0, 1)), ((), ())), precision=...  37.6 us
    reduce_scatter x1, waiting for transfers between devices, body(): lax.psum_scatter(make_term(tap_stack(second_ext), wide_two), 'ch', scatte...  28.3 us
    ppermute x2, starting transfers between devices, extended_2(): lax.ppermute(tail, axis, [(i, (i + 1) % count) for i in range(ends)])  8.22 us
    ppermute x2, waiting for transfers between devices, partner(): return lax.ppermute(block, axis, route)  6.3 us
    ppermute x2, waiting for transfers between devices, extended_2(): lax.ppermute(head, axis, [((i + 1) % count, i) for i in range(ends)])  5.55 us
    mul x2, other arithmetic, activate(): jax.nn.gelu(values * gain[:, None] + offset[:, None], approximate=False)  3.26 us
  transfers between devices with their start and end apart: 8, of which 6 were waited for; matrix products, arithmetic and copies ran while one was open for 2% of the time, Pallas kernels for 0%

commit v1 on v0

v1 whole, which is shorter than its diff:
```python
import functools

import jax
import jax.numpy as jnp
from jax import lax
from jax.experimental import pallas as pl
from jax.experimental.pallas import tpu as pltpu
from jax.sharding import PartitionSpec as P

KW = 5
GROUP = 4
EDGE = 8
CHUNK = 264
LANES = 128
VMEM_LIMIT = 2 * 1024 * 1024
VECTORS = pl.BlockSpec(memory_space=pltpu.VMEM)
SCALARS = pl.BlockSpec(memory_space=pltpu.SMEM)
IN_HBM = pl.BlockSpec(memory_space=pltpu.HBM)
LIGHT = 10_000_000_000


def f32(*shape):
    return jax.ShapeDtypeStruct(shape, jnp.float32)


def bf16(*shape):
    return jax.ShapeDtypeStruct(shape, jnp.bfloat16)


def in_hbm(array):
    return pltpu.with_memory_space_constraint(array, pltpu.HBM)


def cost(flops):
    return pl.CostEstimate(flops=flops, transcendentals=0, bytes_accessed=0)


def call(kernel, name, where, args, outs, scratch=(), flops=LIGHT):
    return pl.pallas_call(
        kernel,
        in_specs=[SCALARS] + [VECTORS] * len(args),
        out_specs=[VECTORS] * len(outs),
        out_shape=list(outs),
        scratch_shapes=[pltpu.VMEM(shape, jnp.float32) for shape in scratch],
        compiler_params=pltpu.CompilerParams(vmem_limit_bytes=VMEM_LIMIT),
        cost_estimate=cost(flops),
        name=name,
    )(where, *args)


def swapped(block, axis, bit):
    count = lax.axis_size(axis)
    return lax.ppermute(block, axis, [(i, i ^ bit) for i in range(count)])


def gelu(values):
    return 0.5 * values * (1.0 + lax.erf(values * (0.5**0.5)))


def store_taps(hi_ref, lo_ref, act_ref, start):
    rows, channels = hi_ref.shape[0], act_ref.shape[1]
    for tap in range(KW):
        values = act_ref[pl.ds(start + tap, rows)]
        hi = values.astype(jnp.bfloat16)
        cols = slice(tap * channels, (tap + 1) * channels)
        hi_ref[:, cols] = hi
        lo_ref[:, cols] = (values - hi.astype(jnp.float32)).astype(jnp.bfloat16)


def row_plan(length, chunk):
    return chunk, length - chunk + 16, chunk // 2 - 4, (length - chunk) // 2 + 12


def padded(rows):
    return -(-rows // 16) * 16


def split_tap(where_ref, tap, w_ref, outs, far):
    channels, owned = w_ref.shape[0], w_ref.shape[1] // 4
    hi_ref, lo_ref = outs
    high = 1 - where_ref[0] if far else where_ref[0]
    core = where_ref[1]
    for half, owner in enumerate((2 * high + 1 - core, 2 * high + core)):
        weight = w_ref[:, pl.ds(pl.multiple_of(owner * owned, LANES), owned)]
        hi = weight.astype(jnp.bfloat16)
        place = (slice(tap * channels, (tap + 1) * channels), slice(half * owned, (half + 1) * owned))
        hi_ref[place] = hi
        lo_ref[place] = (weight - hi.astype(jnp.float32)).astype(jnp.bfloat16)


def opening_kernel(where_ref, gain_hbm, shift_hbm, x_hbm, w_hbm, hi_ref, lo_ref, edge_ref, far_hi, far_lo, own_hi, own_lo,
                   x_ref, gain_ref, shift_ref, act_ref, w_ref, x_sem, w_sem):
    length = x_ref.shape[1]
    gets = [
        pltpu.make_async_copy(src, dst, x_sem.at[i])
        for i, (src, dst) in enumerate(((gain_hbm, gain_ref), (shift_hbm, shift_ref), (x_hbm, x_ref)))
    ]
    copies = [pltpu.make_async_copy(w_hbm.at[tap], w_ref.at[tap], w_sem.at[tap]) for tap in range(KW)]
    for copy in gets + copies:
        copy.start()
    for copy in gets:
        copy.wait()
    gain, shift = gain_ref[...][None], shift_ref[...][None]
    rows = act_ref.shape[0]
    act_ref[...] = gelu(jnp.transpose(x_ref[:, :rows]) * gain + shift)
    edge_ref[0] = act_ref[:EDGE]
    last = jnp.transpose(x_ref[:, length - LANES :])[LANES - EDGE :]
    edge_ref[1] = gelu(last * gain + shift)
    store_taps(hi_ref, lo_ref, act_ref, 2)
    for tap, copy in enumerate(copies):
        copy.wait()
        split_tap(where_ref, tap, w_ref.at[tap], (far_hi, far_lo), True)
        split_tap(where_ref, tap, w_ref.at[tap], (own_hi, own_lo), False)


def opening(where, features, gain, shift, weight, rows):
    channels, length = features.shape
    outs = weight.shape[2]
    depth = KW * channels
    stack, split = bf16(padded(rows), depth), bf16(depth, outs // 2)
    span = -(-(padded(rows) + 6) // LANES) * LANES
    return pl.pallas_call(
        opening_kernel,
        in_specs=[SCALARS] + [IN_HBM] * 4,
        out_specs=[VECTORS] * 7,
        out_shape=[stack, stack, f32(2, EDGE, channels)] + [split] * 4,
        scratch_shapes=[
            pltpu.VMEM((channels, length), jnp.float32),
            pltpu.VMEM((channels,), jnp.float32),
            pltpu.VMEM((channels,), jnp.float32),
            pltpu.VMEM((span, channels), jnp.float32),
            pltpu.VMEM((KW, channels, outs), jnp.float32),
            pltpu.SemaphoreType.DMA((3,)),
            pltpu.SemaphoreType.DMA((KW,)),
        ],
        compiler_params=pltpu.CompilerParams(vmem_limit_bytes=16 * 1024 * 1024),
        cost_estimate=cost(LIGHT),
        name="opening",
    )(where, *map(in_hbm, (gain, shift, features, weight)))


def first_b_kernel(where_ref, x_ref, gain_ref, shift_ref, edge_ref, inner_ref, outer_ref, hi_ref, lo_ref, act_ref, *, chunk):
    gain, shift = gain_ref[...][None], shift_ref[...][None]
    length = x_ref.shape[1]
    base = (chunk + 2) // LANES * LANES
    top = length - base
    act_ref[:top] = gelu(jnp.transpose(x_ref[:, base:]) * gain + shift)
    odd = where_ref[5] > 0
    inner, outer = inner_ref[...], outer_ref[...]
    left = jnp.where(odd, inner, outer)
    right = jnp.where(odd, outer, inner)
    act_ref[top : top + 6] = right[:6]
    act_ref[top + 6 : top + 12] = left[2:]
    act_ref[top + 12 : top + 18] = edge_ref[0, :6]
    act_ref[top + 18 :] = jnp.zeros((act_ref.shape[0] - top - 18, act_ref.shape[1]), jnp.float32)
    store_taps(hi_ref, lo_ref, act_ref, chunk + 2 - base)


def split_kernel(where_ref, w_ref, hi_ref, lo_ref, *, far):
    for tap in range(KW):
        split_tap(where_ref, tap, w_ref.at[tap], (hi_ref, lo_ref), far)


def split_weight(where, weight, far):
    _, channels, outs = weight.shape
    return call(
        functools.partial(split_kernel, far=far), "split_far" if far else "split_own", where, [weight],
        [bf16(KW * channels, outs // 2)] * 2,
    )


def conv_kernel(where_ref, hi_ref, lo_ref, whi_ref, wlo_ref, there_ref, here_ref):
    rows, owned = there_ref.shape
    for start in range(0, 2 * owned, 2 * LANES):
        cols = slice(start, start + 2 * LANES)
        hi, weight_hi = hi_ref[...], whi_ref[:, cols]
        total = jnp.dot(hi, weight_hi, preferred_element_type=jnp.float32)
        total += jnp.dot(lo_ref[...], weight_hi, preferred_element_type=jnp.float32)
        total += jnp.dot(hi, wlo_ref[:, cols], preferred_element_type=jnp.float32)
        for part in range(2):
            at = start + part * LANES
            values = total[:rows, part * LANES : (part + 1) * LANES]
            if at < owned:
                there_ref[:, at : at + LANES] = values
            else:
                here_ref[:, at - owned : at - owned + LANES] = values


def conv(where, stack, weight, rows):
    owned = weight[0].shape[1] // 2
    depth = weight[0].shape[0]
    return call(
        conv_kernel, "conv", where, [*stack, *weight], [f32(rows, owned)] * 2
    )


def put_sum(sum_ref, start, a_ref, b_ref, c_ref):
    for j in range(sum_ref.shape[0]):
        cols = slice(j * LANES, (j + 1) * LANES)
        sum_ref[j, pl.ds(start, a_ref.shape[0])] = a_ref[:, cols] + (b_ref[:, cols] + c_ref[:, cols])


def pool_rows(sum_ref):
    blocks, rows, _ = sum_ref.shape
    return jnp.concatenate(
        [
            jnp.maximum(
                sum_ref[j, pl.ds(0, rows // 2, stride=2)], sum_ref[j, pl.ds(1, rows // 2, stride=2)]
            )
            for j in range(blocks)
        ],
        axis=1,
    )


def second_c_kernel(where_ref, a_ref, b_ref, c_ref, gain_ref, shift_ref, hi_ref, lo_ref, ends_ref, sum_ref, act_ref):
    put_sum(sum_ref, 0, a_ref, b_ref, c_ref)
    rows = a_ref.shape[0] // 2
    act_ref[:rows] = gelu(pool_rows(sum_ref) * gain_ref[...][None] + shift_ref[...][None])
    act_ref[rows:] = jnp.zeros((act_ref.shape[0] - rows, act_ref.shape[1]), jnp.float32)
    ends_ref[:4] = act_ref[:4]
    ends_ref[4:] = act_ref[rows - 4 : rows]
    store_taps(hi_ref, lo_ref, act_ref, 0)


def second_d_kernel(where_ref, a_ref, b_ref, c_ref, gain_ref, shift_ref, ends_ref, hi_ref, lo_ref, sum_ref, act_ref):
    put_sum(sum_ref, 0, a_ref, b_ref, c_ref)
    active = gelu(pool_rows(sum_ref) * gain_ref[...][None] + shift_ref[...][None])
    row = lax.broadcasted_iota(jnp.int32, active.shape, 0)
    main = active.shape[0] - 8
    beyond = (row >= main - 2) & (row < main) & (where_ref[3] == 0)
    before = (row >= main + 2) & (row < main + 4) & (where_ref[2] == 0)
    active = jnp.where(beyond | before, 0.0, active)
    act_ref[:4] = ends_ref[4:]
    act_ref[4 : main + 4] = active[:main]
    act_ref[main + 4 : main + 8] = active[main + 2 : main + 6]
    act_ref[main + 8 : main + 12] = ends_ref[:4]
    act_ref[main + 12 :] = jnp.zeros((act_ref.shape[0] - main - 12, act_ref.shape[1]), jnp.float32)
    store_taps(hi_ref, lo_ref, act_ref, 0)


def pieces_kernel(where_ref, *refs):
    ins, outs, (c_ref, d_ref, all_ref) = refs[:6], refs[6:-3], refs[-3:]
    put_sum(c_ref, 0, *ins[:3])
    put_sum(d_ref, 0, *ins[3:])
    pooled_d = pool_rows(d_ref)
    rows_c = ins[0].shape[0] // 2
    main = all_ref.shape[0] - 2 - rows_c
    all_ref[:2] = pooled_d[main + 2 : main + 4]
    all_ref[2 : 2 + rows_c] = pool_rows(c_ref)
    all_ref[2 + rows_c :] = pooled_d[:main]
    part = all_ref.shape[1] // GROUP
    turned = jnp.transpose(all_ref[...])
    member = where_ref[4]
    for r in range(GROUP):
        for d in range(GROUP):
            @pl.when(member == r ^ d)
            def _():
                outs[d][...] = turned[r * part : (r + 1) * part]


def join_kernel(where_ref, *refs):
    ins, out_ref = refs[:-1], refs[-1]
    width = ins[0].shape[1]
    for d, ref in enumerate(ins):
        out_ref[0, :, pl.ds(pl.multiple_of((where_ref[4] ^ d) * width, LANES), width)] = ref[...]


def after(values, *done):
    return lax.optimization_barrier((values, done))[0]


def body(features, gain_one, shift_one, wide_one, gain_two, shift_two, wide_two):
    seq = lax.axis_index("seq")
    n_seq = lax.axis_size("seq")
    ch = lax.axis_index("ch")
    where = jnp.stack(
        [
            ch // 2, ch % 2, (seq > 0).astype(jnp.int32), (seq < n_seq - 1).astype(jnp.int32),
            seq % GROUP, seq % 2,
        ]
    )
    one = [gain_one, shift_one]
    two = [gain_two, shift_two]
    channels, length = features.shape
    depth = KW * channels
    rows_a, rows_b, rows_c, rows_d = row_plan(length, CHUNK)

    hi_a, lo_a, edge, *split_one = opening(where, features, *one, wide_one, rows_a)
    far_one, own_one = split_one[:2], split_one[2:]
    odd = seq % 2
    to_inner = lax.dynamic_index_in_dim(edge, 1 - odd, 0, keepdims=False)
    to_outer = lax.dynamic_index_in_dim(edge, odd, 0, keepdims=False)
    inner = lax.ppermute(to_inner, "seq", [(i, i ^ 1) for i in range(n_seq)])
    outer = lax.ppermute(
        to_outer, "seq", [p for i in range(1, n_seq - 1, 2) for p in ((i, i + 1), (i + 1, i))]
    )

    there_a, here_a = conv(where, (hi_a, lo_a), far_one, rows_a)
    half_a = here_a + swapped(there_a, "ch", 1)
    sum_a = swapped(half_a, "ch", 2)

    stack_b = call(
        functools.partial(first_b_kernel, chunk=CHUNK), "first_b", where,
        [after(features, half_a), *one, edge, inner, outer],
        [bf16(padded(rows_b), depth)] * 2, [(length - (CHUNK + 2) // LANES * LANES + 48, channels)],
    )
    there_b, here_b = conv(where, stack_b, far_one, rows_b)
    half_b = here_b + swapped(there_b, "ch", 1)
    own_there_a, own_here_a = conv(where, after((hi_a, lo_a), there_b), own_one, rows_a)
    own_a = own_here_a, swapped(own_there_a, "ch", 1)
    half_b = after(half_b, own_here_a)
    sum_b = swapped(half_b, "ch", 2)

    own_there_b, own_here_b = conv(where, after(stack_b, half_b), own_one, rows_b)
    own_b = own_here_b, swapped(own_there_b, "ch", 1)
    far_two = split_weight(where, after(wide_two, own_here_b), True)

    *stack_c, ends = call(
        second_c_kernel, "second_c", where, [after(sum_a, far_two), *own_a, *two],
        [bf16(padded(rows_c), depth)] * 2 + [f32(8, channels)],
        [(channels // LANES, rows_a, LANES), (padded(rows_c) + 8, channels)],
    )
    there_c, here_c = conv(where, stack_c, far_two, rows_c)
    half_c = here_c + swapped(there_c, "ch", 1)
    own_two = split_weight(where, after(wide_two, there_c), False)
    half_c = after(half_c, own_two)
    sum_c = swapped(half_c, "ch", 2)

    stack_d = call(
        second_d_kernel, "second_d", where, [after(sum_b, half_c), *own_b, *two, ends],
        [bf16(padded(rows_d), depth)] * 2,
        [(channels // LANES, rows_b, LANES), (padded(rows_d) + 8, channels)],
    )
    there_d, here_d = conv(where, stack_d, far_two, rows_d)
    half_d = here_d + swapped(there_d, "ch", 1)
    own_there_c, own_here_c = conv(where, after(stack_c, there_d), own_two, rows_c)
    half_d = after(half_d, own_here_c)
    sum_d = swapped(half_d, "ch", 2)
    own_c = own_here_c, swapped(own_there_c, "ch", 1)
    own_there_d, own_here_d = conv(where, after(stack_d, half_d, sum_c), own_two, rows_d)
    own_d = own_here_d, swapped(own_there_d, "ch", 1)

    quarter = length // 4
    pieces = call(
        pieces_kernel, "pieces", where, [sum_c, *own_c, sum_d, *own_d],
        [f32(channels // GROUP, quarter)] * GROUP,
        [(channels // LANES, rows_c, LANES), (channels // LANES, rows_d, LANES), (quarter, channels)],
    )
    blocks = [pieces[0]] + [swapped(pieces[d], "seq", d) for d in range(1, GROUP)]
    shape = jax.ShapeDtypeStruct((1, channels // GROUP, GROUP * quarter), jnp.float32)
    return call(join_kernel, "join", where, blocks, [shape])[0]


def solution(mesh):
    return jax.shard_map(
        body,
        mesh=mesh,
        in_specs=(
            P("ch", "seq"),
            P("ch"),
            P("ch"),
            P(None, "ch", None),
            P("ch"),
            P("ch"),
            P(None, "ch", None),
        ),
        out_specs=P("seq", "ch", None),
        check_vma=False,
    )
```

time: 158 us -> 69.2 us (0.44)
  waiting for transfers between devices: 79.2 us -> 11.8 us
  Pallas kernels: 0 us -> 38 us
  matrix products: 37.6 us -> 0 us
  between operations: 13.7 us -> 0.46 us
  other arithmetic: 7.67 us -> 0.15 us
  local copies, waits for them, and re-layouts: 5.27 us -> 1.39 us
  starting transfers between devices: 14.1 us -> 17.2 us
    reduce_scatter x2 -> x0, waiting for transfers between devices: 67.4 us -> none  [the longest x1 39.1 us: body(): lax.psum_scatter(make_term(tap_stack(extended), wide_one), 'ch', scatter_...]
    pallas_call x0 -> x16, Pallas kernels: none -> 38 us  [the longest x15 30.4 us: call(): pl.pallas_call(kernel, in_specs=[SCALARS] + [VECTORS] * len(args), out_sp...]
    dot_general x2 -> x0, matrix products: 37.6 us -> none  [make_term(): lax.dot_general(weight, stacked, (((0, 1), (0, 1)), ((), ())), precision=...]
    ppermute x6 -> x17, starting transfers between devices: 13.9 us -> 17.2 us  [the longest x15 11.1 us: swapped(): return lax.ppermute(block, axis, [(i, i ^ bit) for i in range(count)])]
    mul x2 -> x0, other arithmetic: 3.26 us -> none  [activate(): jax.nn.gelu(values * gain[:, None] + offset[:, None], approximate=False)]
    unnamed x8 -> x1, other arithmetic: 2.83 us -> 0.01 us
    reshape x2 -> x0, local copies, waits for them, and re-layouts: 2.81 us -> none  [pool_pairs(): values.reshape(values.shape[0], values.shape[1] // 2, 2)]
    ppermute x6 -> x17, waiting for transfers between devices: 11.9 us -> 11.8 us  [the longest x15 11.8 us: swapped(): return lax.ppermute(block, axis, [(i, i ^ bit) for i in range(count)])]
  transfers between devices with their start and end apart: 8 -> 17, of which waited for: 6 -> 6; matrix products, arithmetic and copies ran while one was open for 2% -> 0% of each run, Pallas kernels for 0% -> 33%
where the time goes in v1:
time: 69.2 us; the launch traced here: 69.1 us
  Pallas kernels  38 us (55%)
  starting transfers between devices  17.2 us (25%)
  waiting for transfers between devices  11.8 us (17%)
  local copies, waits for them, and re-layouts  1.39 us (2%)
    pallas_call x15, Pallas kernels, call(): pl.pallas_call(kernel, in_specs=[SCALARS] + [VECTORS] * len(args), out_sp...  30.4 us
    ppermute x15, waiting for transfers between devices, swapped(): return lax.ppermute(block, axis, [(i, i ^ bit) for i in range(count)])  11.8 us
    ppermute x15, starting transfers between devices, swapped(): return lax.ppermute(block, axis, [(i, i ^ bit) for i in range(count)])  11.1 us
    pallas_call x1, Pallas kernels, opening(): pl.pallas_call(opening_kernel, in_specs=[SCALARS] + [IN_HBM] * 4, out_spe...  7.63 us
    ppermute x1, starting transfers between devices, body(): inner = lax.ppermute(to_inner, 'seq', [(i, i ^ 1) for i in range(n_seq)])  5.35 us
  transfers between devices with their start and end apart: 17, of which 6 were waited for; matrix products, arithmetic and copies ran while one was open for 0% of the time, Pallas kernels for 33%

profile of v1, /device:TPU:0, one launch (start us, length us, event | category | flops | bytes accessed | tf_op | source)
XLA Modules:
  0.0 69.1 jit_solution(5793855644407224401)
XLA Ops:
  0.1 7.6 %opening.1 = (bf16[272,1920]{1,0:T(8,128)(2,1)S(1)}, bf16[272,1920]{1,0:T(8,128)(2,1)S(1)}, f32[2,8,384]{2,1,0:T(8,128)S(1)}, bf16[1920,768]{1,0:T(8,128)(2,1)S(...) custom-call(s32[6]{0:T(128)S(1)} %stack.35.where_ref, ...), custom_call_target="tpu_custom_call" | custom-call | flops 10000000000 | tf_op jit(solution)/shard_map/opening/pallas_call | solution.py:122
  7.8 3.3 %conv.8 = (f32[264,384]{1,0:T(8,128)S(1)}, f32[264,384]{1,0:T(8,128)S(1)}) custom-call(s32[6]{0:T(128)S(1)} %stack.35.where_ref, bf16[272,1920]{1,0:T(8,128)(2,1)S(1)} %get-tuple-element.71.hi_ref, bf16[272,1920]{1,0:T(8,128)(2,1)S(1)} %get-tuple-element.72.lo_ref, bf16[1920,768]{1,0:T(8,128)(2,1)S(1)} %get-tuple-element.61.whi_ref, ...), custom_call_target="tpu_custom_call" | custom-call | flops 10000000000 | tf_op jit(solution)/shard_map/conv/pallas_call | solution.py:39
  13.7 5.3 %collective-permute-start.2 = (f32[8,384]{1,0:T(8,128)S(1)}, f32[8,384]{1,0:T(8,128)S(1)}, u32[]{:S(2)}, u32[]{:S(2)}) collective-permute-start(f32[8,384]{1,0:T(8,128)S(1)} %get-tuple-element.114), channel_id=1, source_target_pairs={{0,4},{4,0},{8,12},{12,8},{16,20},{20,16},{24,28},{28,24},{1,5},{5... | collective-permute-start | bytes 36872 | tf_op jit(solution)/shard_map/ppermute | solution.py:294
  19.1 1.6 %collective-permute-start.1 = (f32[264,384]{1,0:T(8,128)S(1)}, f32[264,384]{1,0:T(8,128)S(1)}, u32[]{:S(2)}, u32[]{:S(2)}) collective-permute-start(f32[264,384]{1,0:T(8,128)S(1)} %add.35), channel_id=1, source_target_pairs={{0,2},{1,3},{2,0},{3,1},{4,6},{5,7},{6,4},{7,5},{8,10},{9,11},{10,... | collective-permute-start | bytes 1216520 | tf_op jit(solution)/shard_map/ppermute | solution.py:53
  20.7 1.3 %first_b.1 = (bf16[272,1920]{1,0:T(8,128)(2,1)S(1)}, bf16[272,1920]{1,0:T(8,128)(2,1)S(1)}) custom-call(s32[6]{0:T(128)S(1)} %stack.35.where_ref, f32[384,512]{1,0:T(8,128)S(1)} %copy-done, f32[384]{0:T(512)S(1)} %copy-done.1, f32[384]{0:T(512)S(1)} %copy-done.2, f32[2,8,384]{2,1,0:T(8,128)S(1)} %get-tuple-element.66.edge_ref, ...), custom_call_target="tpu_custom_call" | custom-call | flops 10000000000 | tf_op jit(solution)/shard_map/first_b/pallas_call | solution.py:39
  22.1 3.3 %conv.9 = (f32[264,384]{1,0:T(8,128)S(1)}, f32[264,384]{1,0:T(8,128)S(1)}) custom-call(s32[6]{0:T(128)S(1)} %stack.35.where_ref, bf16[272,1920]{1,0:T(8,128)(2,1)S(1)} %get-tuple-element.77.hi_ref, bf16[272,1920]{1,0:T(8,128)(2,1)S(1)} %get-tuple-element.78.lo_ref, bf16[1920,768]{1,0:T(8,128)(2,1)S(1)} %copy-done.10, bf16[1920,768]{1,0:T(8,128)(2,1)S(1)} %copy-done.12), custom_call_target="tpu_custom_call" | custom-call | flops 10000000000 | tf_op jit(solution)/shard_map/conv/pallas_call | solution.py:39
  25.5 3.3 %conv.10 = (f32[264,384]{1,0:T(8,128)S(1)}, f32[264,384]{1,0:T(8,128)S(1)}) custom-call(s32[6]{0:T(128)S(1)} %stack.35.where_ref, bf16[272,1920]{1,0:T(8,128)(2,1)S(1)} %get-tuple-element.71.hi_ref, bf16[272,1920]{1,0:T(8,128)(2,1)S(1)} %copy-done.14, bf16[1920,768]{1,0:T(8,128)(2,1)S(1)} %copy-done.6, bf16[1920,768]{1,0:T(8,128)(2,1)S(1)} %copy-done.8), custom_call_target="tpu_custom_call" | custom-call | flops 10000000000 | tf_op jit(solution)/shard_map/conv/pallas_call | solution.py:39
  29.5 1.6 %collective-permute-start.8 = (f32[264,384]{1,0:T(8,128)S(1)}, f32[264,384]{1,0:T(8,128)S(1)}, u32[]{:S(2)}, u32[]{:S(2)}) collective-permute-start(f32[264,384]{1,0:T(8,128)S(1)} %add.38), channel_id=1, source_target_pairs={{0,2},{1,3},{2,0},{3,1},{4,6},{5,7},{6,4},{7,5},{8,10},{9,11},{10,... | collective-permute-start | bytes 1216520 | tf_op jit(solution)/shard_map/ppermute | solution.py:53
  31.0 3.3 %conv.11 = (f32[264,384]{1,0:T(8,128)S(1)}, f32[264,384]{1,0:T(8,128)S(1)}) custom-call(s32[6]{0:T(128)S(1)} %stack.35.where_ref, bf16[272,1920]{1,0:T(8,128)(2,1)S(1)} %get-tuple-element.77.hi_ref, bf16[272,1920]{1,0:T(8,128)(2,1)S(1)} %get-tuple-element.78.lo_ref, bf16[1920,768]{1,0:T(8,128)(2,1)S(1)} %copy-done.6, bf16[1920,768]{1,0:T(8,128)(2,1)S(1)} %copy-done.8), custom_call_target="tpu_custom_call" | custom-call | flops 10000000000 | tf_op jit(solution)/shard_map/conv/pallas_call | solution.py:39
  34.4 1.7 %split_far.1 = (bf16[1920,768]{1,0:T(8,128)(2,1)S(1)}, bf16[1920,768]{1,0:T(8,128)(2,1)S(1)}) custom-call(s32[6]{0:T(128)S(1)} %stack.35.where_ref, f32[5,384,1536]{2,1,0:T(8,128)S(1)} %bitcast.11), custom_call_target="tpu_custom_call" | custom-call | flops 10000000000 | tf_op jit(solution)/shard_map/split_far/pallas_call | solution.py:39
  37.2 1.9 %conv.12 = (f32[128,384]{1,0:T(8,128)S(1)}, f32[128,384]{1,0:T(8,128)S(1)}) custom-call(s32[6]{0:T(128)S(1)} %stack.35.where_ref, bf16[128,1920]{1,0:T(8,128)(2,1)S(1)} %get-tuple-element.99.hi_ref, bf16[128,1920]{1,0:T(8,128)(2,1)S(1)} %get-tuple-element.100.lo_ref, bf16[1920,768]{1,0:T(8,128)(2,1)S(1)} %get-tuple-element.81.whi_ref, ...), custom_call_target="tpu_custom_call" | custom-call | flops 10000000000 | tf_op jit(solution)/shard_map/conv/pallas_call | solution.py:39
  39.7 1.7 %split_own.1 = (bf16[1920,768]{1,0:T(8,128)(2,1)S(1)}, bf16[1920,768]{1,0:T(8,128)(2,1)S(1)}) custom-call(s32[6]{0:T(128)S(1)} %stack.35.where_ref, f32[5,384,1536]{2,1,0:T(8,128)S(1)} %bitcast.11), custom_call_target="tpu_custom_call" | custom-call | flops 10000000000 | tf_op jit(solution)/shard_map/split_own/pallas_call | solution.py:39
  41.5 1.3 %collective-permute-start.7 = (f32[128,384]{1,0:T(8,128)S(1)}, f32[128,384]{1,0:T(8,128)S(1)}, u32[]{:S(2)}, u32[]{:S(2)}) collective-permute-start(f32[128,384]{1,0:T(8,128)S(1)} %add.39), channel_id=1, source_target_pairs={{0,2},{1,3},{2,0},{3,1},{4,6},{5,7},{6,4},{7,5},{8,10},{9,11},{10,... | collective-permute-start | bytes 589832 | tf_op jit(solution)/shard_map/ppermute | solution.py:53
  42.7 1.1 %second_d.1 = (bf16[144,1920]{1,0:T(8,128)(2,1)S(1)}, bf16[144,1920]{1,0:T(8,128)(2,1)S(1)}) custom-call(s32[6]{0:T(128)S(1)} %stack.35.where_ref, f32[264,384]{1,0:T(8,128)S(1)} %collective-permute-done.8.a_ref, f32[264,384]{1,0:T(8,128)S(1)} %get-tuple-element.79.b_ref, f32[264,384]{1,0:T(8,128)S(1)} %collective-permute-done.9.c_ref, f32[384]{0:T(512)S(1)} %copy-done.3, ...), custom_call_target="tpu_custom_call" | custom-call | flops 10000000000 | tf_op jit(solution)/shard_map/second_d/pallas_call | solution.py:39
  43.9 2.2 %conv.13 = (f32[136,384]{1,0:T(8,128)S(1)}, f32[136,384]{1,0:T(8,128)S(1)}) custom-call(s32[6]{0:T(128)S(1)} %stack.35.where_ref, bf16[144,1920]{1,0:T(8,128)(2,1)S(1)} %get-tuple-element.105.hi_ref, bf16[144,1920]{1,0:T(8,128)(2,1)S(1)} %get-tuple-element.106.lo_ref, bf16[1920,768]{1,0:T(8,128)(2,1)S(1)} %get-tuple-element.81.whi_ref, ...), custom_call_target="tpu_custom_call" | custom-call | flops 10000000000 | tf_op jit(solution)/shard_map/conv/pallas_call | solution.py:39
  46.1 2.1 %conv.14 = (f32[128,384]{1,0:T(8,128)S(1)}, f32[128,384]{1,0:T(8,128)S(1)}) custom-call(s32[6]{0:T(128)S(1)} %stack.35.where_ref, bf16[128,1920]{1,0:T(8,128)(2,1)S(1)} %get-tuple-element.99.hi_ref, bf16[128,1920]{1,0:T(8,128)(2,1)S(1)} %get-tuple-element.100.lo_ref, bf16[1920,768]{1,0:T(8,128)(2,1)S(1)} %get-tuple-element.90.whi_ref, ...), custom_call_target="tpu_custom_call" | custom-call | flops 10000000000 | tf_op jit(solution)/shard_map/conv/pallas_call | solution.py:39
  48.6 2.1 %conv.15 = (f32[136,384]{1,0:T(8,128)S(1)}, f32[136,384]{1,0:T(8,128)S(1)}) custom-call(s32[6]{0:T(128)S(1)} %stack.35.where_ref, bf16[144,1920]{1,0:T(8,128)(2,1)S(1)} %get-tuple-element.105.hi_ref, bf16[144,1920]{1,0:T(8,128)(2,1)S(1)} %get-tuple-element.106.lo_ref, bf16[1920,768]{1,0:T(8,128)(2,1)S(1)} %get-tuple-element.90.whi_ref, ...), custom_call_target="tpu_custom_call" | custom-call | flops 10000000000 | tf_op jit(solution)/shard_map/conv/pallas_call | solution.py:39
  52.0 1.4 %collective-permute-done.10.refs_2_ = f32[128,384]{1,0:T(8,128)S(1)} collective-permute-done((f32[128,384]{1,0:T(8,128)S(1)}, f32[128,384]{1,0:T(8,128)S(1)}, u32[]{:S(2)}, u32[]{:S(2)}) %collective-permute-start.10) | collective-permute-done | bytes 196640 | tf_op jit(solution)/shard_map/ppermute | solution.py:53
  53.4 5.0 %collective-permute-done.12.refs_3_ = f32[136,384]{1,0:T(8,128)S(1)} collective-permute-done((f32[136,384]{1,0:T(8,128)S(1)}, f32[136,384]{1,0:T(8,128)S(1)}, u32[]{:S(2)}, u32[]{:S(2)}) %collective-permute-start.12) | collective-permute-done | bytes 208928 | tf_op jit(solution)/shard_map/ppermute | solution.py:53
  59.2 2.1 %collective-permute-start.14 = (f32[96,128]{1,0:T(8,128)S(1)}, f32[96,128]{1,0:T(8,128)S(1)}, u32[]{:S(2)}, u32[]{:S(2)}) collective-permute-start(f32[96,128]{1,0:T(8,128)S(1)} %get-tuple-element.110), channel_id=1, source_target_pairs={{0,4},{4,0},{8,12},{12,8},{16,20},{20,16},{24,28},{28,24},{1,5},{5... | collective-permute-start | bytes 147464 | tf_op jit(solution)/shard_map/ppermute | solution.py:53
  61.3 1.6 %collective-permute-start.15 = (f32[96,128]{1,0:T(8,128)S(1)}, f32[96,128]{1,0:T(8,128)S(1)}, u32[]{:S(2)}, u32[]{:S(2)}) collective-permute-start(f32[96,128]{1,0:T(8,128)S(1)} %get-tuple-element.111), channel_id=1, source_target_pairs={{0,8},{4,12},{8,0},{12,4},{16,24},{20,28},{24,16},{28,20},{1,9},{5... | collective-permute-start | bytes 147464 | tf_op jit(solution)/shard_map/ppermute | solution.py:53
  63.3 2.1 %collective-permute-done.15.refs_2_ = f32[96,128]{1,0:T(8,128)S(1)} collective-permute-done((f32[96,128]{1,0:T(8,128)S(1)}, f32[96,128]{1,0:T(8,128)S(1)}, u32[]{:S(2)}, u32[]{:S(2)}) %collective-permute-start.15) | collective-permute-done | bytes 49184 | tf_op jit(solution)/shard_map/ppermute | solution.py:53
  65.4 2.4 %collective-permute-done.16.refs_3_ = f32[96,128]{1,0:T(8,128)S(1)} collective-permute-done((f32[96,128]{1,0:T(8,128)S(1)}, f32[96,128]{1,0:T(8,128)S(1)}, u32[]{:S(2)}, u32[]{:S(2)}) %collective-permute-start.16) | collective-permute-done | bytes 49184 | tf_op jit(solution)/shard_map/ppermute | solution.py:53
  67.8 1.2 %join.1 = f32[1,96,512]{2,1,0:T(8,128)} custom-call(s32[6]{0:T(128)S(1)} %stack.35.where_ref, f32[96,128]{1,0:T(8,128)S(1)} %get-tuple-element.109.refs_0_, f32[96,128]{1,0:T(8,128)S(1)} %collective-permute-done.14.refs_1_, f32[96,128]{1,0:T(8,128)S(1)} %collective-permute-done.15.refs_2_, f32[96,128]{1,0:T(8,128)S(1)} %collective-permute-done.16.refs_3_), custom_call_target="tpu_custom_call" | custom-call | flops 10000000000 | tf_op jit(solution)/shard_map/join/pallas_call | solution.py:39
  (69 shorter events, 8.2 us)
Async XLA Ops:
  7.8 4.6 %copy-start.13 = (bf16[272,1920]{1,0:T(8,128)(2,1)}, bf16[272,1920]{1,0:T(8,128)(2,1)S(1)}, u32[]{:S(2)}) copy-start(bf16[272,1920]{1,0:T(8,128)(2,1)S(1)} %get-tuple-element.72.lo_ref) | copy-start | bytes 3133444
  7.8 12.9 %copy-start = (f32[384,512]{1,0:T(8,128)S(1)}, f32[384,512]{1,0:T(8,128)}, u32[]{:S(2)}) copy-start(f32[384,512]{1,0:T(8,128)} %x_ref) | copy-start | bytes 2359300
  7.8 12.9 %copy-start.1 = (f32[384]{0:T(512)S(1)}, f32[384]{0:T(512)}, u32[]{:S(2)}) copy-start(f32[384]{0:T(512)} %gain_ref.3) | copy-start | bytes 4612
  7.8 12.9 %copy-start.2 = (f32[384]{0:T(512)S(1)}, f32[384]{0:T(512)}, u32[]{:S(2)}) copy-start(f32[384]{0:T(512)} %shift_ref.3) | copy-start | bytes 4612
  12.4 6.6 %collective-permute-start = (f32[264,384]{1,0:T(8,128)S(1)}, f32[264,384]{1,0:T(8,128)S(1)}, u32[]{:S(2)}, u32[]{:S(2)}) collective-permute-start(f32[264,384]{1,0:T(8,128)S(1)} %get-tuple-element.64), channel_id=1, source_target_pairs={{0,1},{1,0},{2,3},{3,2},{4,5},{5,4},{6,7},{7,6},{8,9},{9,8},{10,11... | collective-permute-start | bytes 1216520 | tf_op jit(solution)/shard_map/ppermute | solution.py:53
  12.8 7.9 %collective-permute-start.3 = (f32[8,384]{1,0:T(8,128)S(1)}, f32[8,384]{1,0:T(8,128)S(1)}, u32[]{:S(2)}, u32[]{:S(2)}) collective-permute-start(f32[8,384]{1,0:T(8,128)S(1)} %get-tuple-element.113), channel_id=1, source_target_pairs={{4,8},{8,4},{12,16},{16,12},{20,24},{24,20},{5,9},{9,5},{13,17},{1... | collective-permute-start | bytes 36872 | tf_op jit(solution)/shard_map/ppermute | solution.py:295
  13.7 7.0 %collective-permute-start.2 = (f32[8,384]{1,0:T(8,128)S(1)}, f32[8,384]{1,0:T(8,128)S(1)}, u32[]{:S(2)}, u32[]{:S(2)}) collective-permute-start(f32[8,384]{1,0:T(8,128)S(1)} %get-tuple-element.114), channel_id=1, source_target_pairs={{0,4},{4,0},{8,12},{12,8},{16,20},{20,16},{24,28},{28,24},{1,5},{5... | collective-permute-start | bytes 36872 | tf_op jit(solution)/shard_map/ppermute | solution.py:294
  19.1 17.0 %collective-permute-start.1 = (f32[264,384]{1,0:T(8,128)S(1)}, f32[264,384]{1,0:T(8,128)S(1)}, u32[]{:S(2)}, u32[]{:S(2)}) collective-permute-start(f32[264,384]{1,0:T(8,128)S(1)} %add.35), channel_id=1, source_target_pairs={{0,2},{1,3},{2,0},{3,1},{4,6},{5,7},{6,4},{7,5},{8,10},{9,11},{10,... | collective-permute-start | bytes 1216520 | tf_op jit(solution)/shard_map/ppermute | solution.py:53
  25.4 4.0 %collective-permute-start.4 = (f32[264,384]{1,0:T(8,128)S(1)}, f32[264,384]{1,0:T(8,128)S(1)}, u32[]{:S(2)}, u32[]{:S(2)}) collective-permute-start(f32[264,384]{1,0:T(8,128)S(1)} %get-tuple-element.70), channel_id=1, source_target_pairs={{0,1},{1,0},{2,3},{3,2},{4,5},{5,4},{6,7},{7,6},{8,9},{9,8},{10,11... | collective-permute-start | bytes 1216520 | tf_op jit(solution)/shard_map/ppermute | solution.py:53
  28.8 7.3 %collective-permute-start.5 = (f32[264,384]{1,0:T(8,128)S(1)}, f32[264,384]{1,0:T(8,128)S(1)}, u32[]{:S(2)}, u32[]{:S(2)}) collective-permute-start(f32[264,384]{1,0:T(8,128)S(1)} %get-tuple-element.84), channel_id=1, source_target_pairs={{0,1},{1,0},{2,3},{3,2},{4,5},{5,4},{6,7},{7,6},{8,9},{9,8},{10,11... | collective-permute-start | bytes 1216520 | tf_op jit(solution)/shard_map/ppermute | solution.py:53
  29.4 4.9 %slice-start = ((s8[11796480]{0:T(1024)(128)(4,1)}), s8[4194304]{0:T(1024)(128)(4,1)S(1)}, s32[]{:S(2)}) async-start(s8[11796480]{0:T(1024)(128)(4,1)} %bitcast.10), calls=%async_computation | async-start | bytes 8388608
  29.4 4.9 %slice-start.1 = ((s8[11796480]{0:T(1024)(128)(4,1)}), s8[4194304]{0:T(1024)(128)(4,1)S(1)}, s32[]{:S(2)}) async-start(s8[11796480]{0:T(1024)(128)(4,1)} %bitcast.10), calls=%async_computation.1 | async-start | bytes 8388608
  29.4 4.9 %slice-start.2 = ((s8[11796480]{0:T(1024)(128)(4,1)}), s8[3407872]{0:T(1024)(128)(4,1)S(1)}, s32[]{:S(2)}) async-start(s8[11796480]{0:T(1024)(128)(4,1)} %bitcast.10), calls=%async_computation.2 | async-start | bytes 6815744
  29.5 13.3 %collective-permute-start.8 = (f32[264,384]{1,0:T(8,128)S(1)}, f32[264,384]{1,0:T(8,128)S(1)}, u32[]{:S(2)}, u32[]{:S(2)}) collective-permute-start(f32[264,384]{1,0:T(8,128)S(1)} %add.38), channel_id=1, source_target_pairs={{0,2},{1,3},{2,0},{3,1},{4,6},{5,7},{6,4},{7,5},{8,10},{9,11},{10,... | collective-permute-start | bytes 1216520 | tf_op jit(solution)/shard_map/ppermute | solution.py:53
  39.1 2.3 %collective-permute-start.6 = (f32[128,384]{1,0:T(8,128)S(1)}, f32[128,384]{1,0:T(8,128)S(1)}, u32[]{:S(2)}, u32[]{:S(2)}) collective-permute-start(f32[128,384]{1,0:T(8,128)S(1)} %get-tuple-element.88), channel_id=1, source_target_pairs={{0,1},{1,0},{2,3},{3,2},{4,5},{5,4},{6,7},{7,6},{8,9},{9,8},{10,11... | collective-permute-start | bytes 589832 | tf_op jit(solution)/shard_map/ppermute | solution.py:53
  39.2 3.5 %collective-permute-start.9 = (f32[264,384]{1,0:T(8,128)S(1)}, f32[264,384]{1,0:T(8,128)S(1)}, u32[]{:S(2)}, u32[]{:S(2)}) collective-permute-start(f32[264,384]{1,0:T(8,128)S(1)} %get-tuple-element.94), channel_id=1, source_target_pairs={{0,1},{1,0},{2,3},{3,2},{4,5},{5,4},{6,7},{7,6},{8,9},{9,8},{10,11... | collective-permute-start | bytes 1216520 | tf_op jit(solution)/shard_map/ppermute | solution.py:53
  41.5 7.2 %collective-permute-start.7 = (f32[128,384]{1,0:T(8,128)S(1)}, f32[128,384]{1,0:T(8,128)S(1)}, u32[]{:S(2)}, u32[]{:S(2)}) collective-permute-start(f32[128,384]{1,0:T(8,128)S(1)} %add.39), channel_id=1, source_target_pairs={{0,2},{1,3},{2,0},{3,1},{4,6},{5,7},{6,4},{7,5},{8,10},{9,11},{10,... | collective-permute-start | bytes 589832 | tf_op jit(solution)/shard_map/ppermute | solution.py:53
  46.0 2.1 %collective-permute-start.11 = (f32[136,384]{1,0:T(8,128)S(1)}, f32[136,384]{1,0:T(8,128)S(1)}, u32[]{:S(2)}, u32[]{:S(2)}) collective-permute-start(f32[136,384]{1,0:T(8,128)S(1)} %get-tuple-element.98), channel_id=1, source_target_pairs={{0,1},{1,0},{2,3},{3,2},{4,5},{5,4},{6,7},{7,6},{8,9},{9,8},{10,11... | collective-permute-start | bytes 626696 | tf_op jit(solution)/shard_map/ppermute | solution.py:53
  50.7 2.7 %collective-permute-start.13 = (f32[136,384]{1,0:T(8,128)S(1)}, f32[136,384]{1,0:T(8,128)S(1)}, u32[]{:S(2)}, u32[]{:S(2)}) collective-permute-start(f32[136,384]{1,0:T(8,128)S(1)} %get-tuple-element.108), channel_id=1, source_target_pairs={{0,1},{1,0},{2,3},{3,2},{4,5},{5,4},{6,7},{7,6},{8,9},{9,8},{10,11... | collective-permute-start | bytes 626696 | tf_op jit(solution)/shard_map/ppermute | solution.py:53
  50.9 7.5 %collective-permute-start.12 = (f32[136,384]{1,0:T(8,128)S(1)}, f32[136,384]{1,0:T(8,128)S(1)}, u32[]{:S(2)}, u32[]{:S(2)}) collective-permute-start(f32[136,384]{1,0:T(8,128)S(1)} %add.40), channel_id=1, source_target_pairs={{0,2},{1,3},{2,0},{3,1},{4,6},{5,7},{6,4},{7,5},{8,10},{9,11},{10,... | collective-permute-start | bytes 626696 | tf_op jit(solution)/shard_map/ppermute | solution.py:53
  51.9 1.4 %collective-permute-start.10 = (f32[128,384]{1,0:T(8,128)S(1)}, f32[128,384]{1,0:T(8,128)S(1)}, u32[]{:S(2)}, u32[]{:S(2)}) collective-permute-start(f32[128,384]{1,0:T(8,128)S(1)} %get-tuple-element.102), channel_id=1, source_target_pairs={{0,1},{1,0},{2,3},{3,2},{4,5},{5,4},{6,7},{7,6},{8,9},{9,8},{10,11... | collective-permute-start | bytes 589832 | tf_op jit(solution)/shard_map/ppermute | solution.py:53
  59.2 4.2 %collective-permute-start.14 = (f32[96,128]{1,0:T(8,128)S(1)}, f32[96,128]{1,0:T(8,128)S(1)}, u32[]{:S(2)}, u32[]{:S(2)}) collective-permute-start(f32[96,128]{1,0:T(8,128)S(1)} %get-tuple-element.110), channel_id=1, source_target_pairs={{0,4},{4,0},{8,12},{12,8},{16,20},{20,16},{24,28},{28,24},{1,5},{5... | collective-permute-start | bytes 147464 | tf_op jit(solution)/shard_map/ppermute | solution.py:53
  61.3 4.1 %collective-permute-start.15 = (f32[96,128]{1,0:T(8,128)S(1)}, f32[96,128]{1,0:T(8,128)S(1)}, u32[]{:S(2)}, u32[]{:S(2)}) collective-permute-start(f32[96,128]{1,0:T(8,128)S(1)} %get-tuple-element.111), channel_id=1, source_target_pairs={{0,8},{4,12},{8,0},{12,4},{16,24},{20,28},{24,16},{28,20},{1,9},{5... | collective-permute-start | bytes 147464 | tf_op jit(solution)/shard_map/ppermute | solution.py:53
  62.9 5.0 %collective-permute-start.16 = (f32[96,128]{1,0:T(8,128)S(1)}, f32[96,128]{1,0:T(8,128)S(1)}, u32[]{:S(2)}, u32[]{:S(2)}) collective-permute-start(f32[96,128]{1,0:T(8,128)S(1)} %get-tuple-element.112), channel_id=1, source_target_pairs={{0,12},{4,8},{8,4},{12,0},{16,28},{20,24},{24,20},{28,16},{1,13},{... | collective-permute-start | bytes 147464 | tf_op jit(solution)/shard_map/ppermute | solution.py:53
  (11 other events, 34.3 us)

commit v2 on v1

v2 whole, which is shorter than its diff:
```python
import functools

import jax
import jax.numpy as jnp
from jax import lax
from jax.experimental import pallas as pl
from jax.experimental.pallas import tpu as pltpu
from jax.sharding import PartitionSpec as P

KW = 5
GROUP = 4
EDGE = 8
CHUNK = 264
LANES = 128
VMEM_LIMIT = 2 * 1024 * 1024
VECTORS = pl.BlockSpec(memory_space=pltpu.VMEM)
IN_HBM = pl.BlockSpec(memory_space=pltpu.HBM)
LIGHT = 1_000_000_000
MIDDLE = 10 * LIGHT
EARLY = 30 * LIGHT
HEAVY = 300 * LIGHT


def f32(*shape):
    return jax.ShapeDtypeStruct(shape, jnp.float32)


def bf16(*shape):
    return jax.ShapeDtypeStruct(shape, jnp.bfloat16)


def in_hbm(array):
    return pltpu.with_memory_space_constraint(array, pltpu.HBM)


def cost(flops):
    return pl.CostEstimate(flops=flops, transcendentals=0, bytes_accessed=0)


def call(kernel, name, args, outs, scratch=(), flops=LIGHT):
    return pl.pallas_call(
        kernel,
        in_specs=[VECTORS] * len(args),
        out_specs=[VECTORS] * len(outs),
        out_shape=list(outs),
        scratch_shapes=[pltpu.VMEM(shape, jnp.float32) for shape in scratch],
        compiler_params=pltpu.CompilerParams(vmem_limit_bytes=VMEM_LIMIT),
        cost_estimate=cost(flops),
        name=name,
    )(*args)


def swapped(block, axis, bit):
    count = lax.axis_size(axis)
    return lax.ppermute(block, axis, [(i, i ^ bit) for i in range(count)])


def gelu(values):
    return 0.5 * values * (1.0 + lax.erf(values * (0.5**0.5)))


def store_taps(hi_ref, lo_ref, act_ref, start):
    rows, channels = hi_ref.shape[0], act_ref.shape[1]
    for tap in range(KW):
        values = act_ref[pl.ds(start + tap, rows)]
        hi = values.astype(jnp.bfloat16)
        cols = slice(tap * channels, (tap + 1) * channels)
        hi_ref[:, cols] = hi
        lo_ref[:, cols] = (values - hi.astype(jnp.float32)).astype(jnp.bfloat16)


def row_plan(length, chunk):
    return chunk, length - chunk + 16, chunk // 2 - 4, (length - chunk) // 2 + 12


def padded(rows):
    return -(-rows // 16) * 16


def split_tap(tap, w_ref, outs, far):
    channels, owned = w_ref.shape[0], w_ref.shape[1] // 4
    hi_ref, lo_ref = outs
    ch = lax.axis_index("ch")
    high, core = (1 - ch // 2 if far else ch // 2), ch % 2
    for half, owner in enumerate((2 * high + 1 - core, 2 * high + core)):
        weight = w_ref[:, pl.ds(pl.multiple_of(owner * owned, LANES), owned)]
        hi = weight.astype(jnp.bfloat16)
        place = (slice(tap * channels, (tap + 1) * channels), slice(half * owned, (half + 1) * owned))
        hi_ref[place] = hi
        lo_ref[place] = (weight - hi.astype(jnp.float32)).astype(jnp.bfloat16)


def opening_kernel(gain_hbm, shift_hbm, x_hbm, w_hbm, hi_ref, lo_ref, head_ref, inner_ref, outer_ref,
                   far_hi, far_lo, own_hi, own_lo,
                   x_ref, gain_ref, shift_ref, act_ref, w_ref, x_sem, w_sem):
    length = x_ref.shape[1]
    gets = [
        pltpu.make_async_copy(src, dst, x_sem.at[i])
        for i, (src, dst) in enumerate(((gain_hbm, gain_ref), (shift_hbm, shift_ref), (x_hbm, x_ref)))
    ]
    copies = [pltpu.make_async_copy(w_hbm.at[tap], w_ref.at[tap], w_sem.at[tap]) for tap in range(KW)]
    ahead = 2
    for copy in gets + copies[:ahead]:
        copy.start()
    for copy in gets:
        copy.wait()
    gain, shift = gain_ref[...][None], shift_ref[...][None]
    rows = act_ref.shape[0]
    act_ref[...] = gelu(jnp.transpose(x_ref[:, :rows]) * gain + shift)
    head = act_ref[:EDGE]
    tail = gelu(jnp.transpose(x_ref[:, length - LANES :])[LANES - EDGE :] * gain + shift)
    odd = lax.axis_index("seq") % 2 == 1
    head_ref[...] = head
    inner_ref[...] = jnp.where(odd, head, tail)
    outer_ref[...] = jnp.where(odd, tail, head)
    store_taps(hi_ref, lo_ref, act_ref, 2)
    for tap, copy in enumerate(copies):
        copy.wait()
        if tap + ahead < KW:
            copies[tap + ahead].start()
        split_tap(tap, w_ref.at[tap], (far_hi, far_lo), True)
        split_tap(tap, w_ref.at[tap], (own_hi, own_lo), False)


def opening(features, gain, shift, weight, rows):
    channels, length = features.shape
    outs = weight.shape[2]
    depth = KW * channels
    stack, split = bf16(padded(rows), depth), bf16(depth, outs // 2)
    span = -(-(padded(rows) + 6) // LANES) * LANES
    return pl.pallas_call(
        opening_kernel,
        in_specs=[IN_HBM] * 4,
        out_specs=[VECTORS] * 9,
        out_shape=[stack] * 2 + [f32(EDGE, channels)] * 3 + [split] * 4,
        scratch_shapes=[
            pltpu.VMEM((channels, length), jnp.float32),
            pltpu.VMEM((channels,), jnp.float32),
            pltpu.VMEM((channels,), jnp.float32),
            pltpu.VMEM((span, channels), jnp.float32),
            pltpu.VMEM((KW, channels, outs), jnp.float32),
            pltpu.SemaphoreType.DMA((3,)),
            pltpu.SemaphoreType.DMA((KW,)),
        ],
        compiler_params=pltpu.CompilerParams(vmem_limit_bytes=16 * 1024 * 1024),
        cost_estimate=cost(LIGHT),
        name="opening",
    )(*map(in_hbm, (gain, shift, features, weight)))


def first_b_kernel(x_ref, gain_ref, shift_ref, head_ref, inner_ref, outer_ref, hi_ref, lo_ref, act_ref, *, chunk):
    gain, shift = gain_ref[...][None], shift_ref[...][None]
    length = x_ref.shape[1]
    base = (chunk + 2) // LANES * LANES
    top = length - base
    act_ref[:top] = gelu(jnp.transpose(x_ref[:, base:]) * gain + shift)
    odd = lax.axis_index("seq") % 2 == 1
    inner, outer = inner_ref[...], outer_ref[...]
    left = jnp.where(odd, inner, outer)
    right = jnp.where(odd, outer, inner)
    act_ref[top : top + 6] = right[:6]
    act_ref[top + 6 : top + 12] = left[2:]
    act_ref[top + 12 : top + 18] = head_ref[:6]
    act_ref[top + 18 :] = jnp.zeros((act_ref.shape[0] - top - 18, act_ref.shape[1]), jnp.float32)
    store_taps(hi_ref, lo_ref, act_ref, chunk + 2 - base)


def split_kernel(w_ref, hi_ref, lo_ref, *, far):
    for tap in range(KW):
        split_tap(tap, w_ref.at[tap], (hi_ref, lo_ref), far)


def split_weight(weight, far, flops=LIGHT):
    _, channels, outs = weight.shape
    return call(
        functools.partial(split_kernel, far=far), "split_far" if far else "split_own", [weight],
        [bf16(KW * channels, outs // 2)] * 2, flops=flops,
    )


def conv_kernel(hi_ref, lo_ref, whi_ref, wlo_ref, there_ref, here_ref):
    rows, owned = there_ref.shape
    for start in range(0, 2 * owned, 2 * LANES):
        cols = slice(start, start + 2 * LANES)
        hi, weight_hi = hi_ref[...], whi_ref[:, cols]
        total = jnp.dot(hi, weight_hi, preferred_element_type=jnp.float32)
        total += jnp.dot(lo_ref[...], weight_hi, preferred_element_type=jnp.float32)
        total += jnp.dot(hi, wlo_ref[:, cols], preferred_element_type=jnp.float32)
        for part in range(2):
            at = start + part * LANES
            values = total[:rows, part * LANES : (part + 1) * LANES]
            if at < owned:
                there_ref[:, at : at + LANES] = values
            else:
                here_ref[:, at - owned : at - owned + LANES] = values


def conv(stack, weight, rows, flops=LIGHT):
    owned = weight[0].shape[1] // 2
    depth = weight[0].shape[0]
    return call(
        conv_kernel, "conv", [*stack, *weight], [f32(rows, owned)] * 2, flops=flops
    )


def add_kernel(a_ref, b_ref, out_ref):
    out_ref[...] = a_ref[...] + b_ref[...]


def added(a, b):
    return call(add_kernel, "added", [a, b], [f32(*a.shape)])[0]


def put_sum(sum_ref, *refs):
    for j in range(sum_ref.shape[0]):
        cols = slice(j * LANES, (j + 1) * LANES)
        sum_ref[j] = sum(ref[:, cols] for ref in refs)


def pool_rows(sum_ref):
    blocks, rows, _ = sum_ref.shape
    return jnp.concatenate(
        [
            jnp.maximum(
                sum_ref[j, pl.ds(0, rows // 2, stride=2)], sum_ref[j, pl.ds(1, rows // 2, stride=2)]
            )
            for j in range(blocks)
        ],
        axis=1,
    )


def second_c_kernel(a_ref, b_ref, c_ref, gain_ref, shift_ref, hi_ref, lo_ref, ends_ref, sum_ref, act_ref):
    put_sum(sum_ref, a_ref, b_ref, c_ref)
    rows = a_ref.shape[0] // 2
    act_ref[:rows] = gelu(pool_rows(sum_ref) * gain_ref[...][None] + shift_ref[...][None])
    act_ref[rows:] = jnp.zeros((act_ref.shape[0] - rows, act_ref.shape[1]), jnp.float32)
    ends_ref[:4] = act_ref[:4]
    ends_ref[4:] = act_ref[rows - 4 : rows]
    store_taps(hi_ref, lo_ref, act_ref, 0)


def second_d_kernel(a_ref, b_ref, c_ref, gain_ref, shift_ref, ends_ref, hi_ref, lo_ref, sum_ref, act_ref):
    put_sum(sum_ref, a_ref, b_ref, c_ref)
    active = gelu(pool_rows(sum_ref) * gain_ref[...][None] + shift_ref[...][None])
    row = lax.broadcasted_iota(jnp.int32, active.shape, 0)
    main = active.shape[0] - 8
    seq = lax.axis_index("seq")
    ends = lax.axis_size("seq") - 1
    beyond = (row >= main - 2) & (row < main) & (seq == ends)
    before = (row >= main + 2) & (row < main + 4) & (seq == 0)
    active = jnp.where(beyond | before, 0.0, active)
    act_ref[:4] = ends_ref[4:]
    act_ref[4 : main + 4] = active[:main]
    act_ref[main + 4 : main + 8] = active[main + 2 : main + 6]
    act_ref[main + 8 : main + 12] = ends_ref[:4]
    act_ref[main + 12 :] = jnp.zeros((act_ref.shape[0] - main - 12, act_ref.shape[1]), jnp.float32)
    store_taps(hi_ref, lo_ref, act_ref, 0)


def pieces_kernel(*refs):
    ins, outs, (c_ref, d_ref, all_ref) = refs[:5], refs[5:-3], refs[-3:]
    put_sum(c_ref, *ins[:3])
    put_sum(d_ref, *ins[3:])
    pooled_d = pool_rows(d_ref)
    rows_c = ins[0].shape[0] // 2
    main = all_ref.shape[0] - 2 - rows_c
    all_ref[:2] = pooled_d[main + 2 : main + 4]
    all_ref[2 : 2 + rows_c] = pool_rows(c_ref)
    all_ref[2 + rows_c :] = pooled_d[:main]
    part = all_ref.shape[1] // GROUP
    turned = jnp.transpose(all_ref[...])
    member = lax.axis_index("seq") % GROUP
    for r in range(GROUP):
        for d in range(GROUP):
            @pl.when(member == r ^ d)
            def _():
                outs[d][...] = turned[r * part : (r + 1) * part]


def join_kernel(*refs):
    ins, out_ref = refs[:-1], refs[-1]
    width = ins[0].shape[1]
    member = lax.axis_index("seq") % GROUP
    for d, ref in enumerate(ins):
        out_ref[0, :, pl.ds(pl.multiple_of((member ^ d) * width, LANES), width)] = ref[...]


def after(values, *done):
    return lax.optimization_barrier((values, done))[0]


def body(features, gain_one, shift_one, wide_one, gain_two, shift_two, wide_two):
    n_seq = lax.axis_size("seq")
    one = [gain_one, shift_one]
    two = [gain_two, shift_two]
    channels, length = features.shape
    depth = KW * channels
    rows_a, rows_b, rows_c, rows_d = row_plan(length, CHUNK)

    hi_a, lo_a, head, to_inner, to_outer, *split_one = opening(features, *one, wide_one, rows_a)
    far_one, own_one = split_one[:2], split_one[2:]
    there_a, here_a = conv((hi_a, lo_a), far_one, rows_a)
    half_a = added(here_a, swapped(there_a, "ch", 1))
    sum_a = swapped(half_a, "ch", 2)

    to_inner, to_outer = after((to_inner, to_outer), half_a)
    inner = lax.ppermute(to_inner, "seq", [(i, i ^ 1) for i in range(n_seq)])
    outer = lax.ppermute(
        to_outer, "seq", [p for i in range(1, n_seq - 1, 2) for p in ((i, i + 1), (i + 1, i))]
    )
    own_there_a, own_here_a = conv(after((hi_a, lo_a), half_a), own_one, rows_a, EARLY)
    own_a = own_here_a, swapped(own_there_a, "ch", 1)
    stack_b = call(
        functools.partial(first_b_kernel, chunk=CHUNK), "first_b",
        [after(features, own_here_a), *one, head, inner, outer],
        [bf16(padded(rows_b), depth)] * 2, [(length - (CHUNK + 2) // LANES * LANES + 48, channels)], EARLY,
    )
    there_b, here_b = conv(stack_b, far_one, rows_b, EARLY)
    half_b = added(here_b, swapped(there_b, "ch", 1))
    far_two = split_weight(after(wide_two, there_b), True, EARLY)
    half_b = after(half_b, far_two)
    sum_b = swapped(half_b, "ch", 2)

    own_there_b, own_here_b = conv(after(stack_b, half_b), own_one, rows_b)
    own_b = own_here_b, swapped(own_there_b, "ch", 1)

    *stack_c, ends = call(
        second_c_kernel, "second_c", [after(sum_a, own_here_b), *own_a, *two],
        [bf16(padded(rows_c), depth)] * 2 + [f32(8, channels)],
        [(channels // LANES, rows_a, LANES), (padded(rows_c) + 8, channels)],
    )
    there_c, here_c = conv(stack_c, far_two, rows_c)
    own_two = split_weight(after(wide_two, there_c), False)
    half_c = added(here_c, swapped(there_c, "ch", 1))
    half_c = after(half_c, own_two)
    sum_c = swapped(half_c, "ch", 2)

    stack_d = call(
        second_d_kernel, "second_d", [after(sum_b, half_c), *own_b, *two, ends],
        [bf16(padded(rows_d), depth)] * 2,
        [(channels // LANES, rows_b, LANES), (padded(rows_d) + 8, channels)], MIDDLE,
    )
    there_d, here_d = conv(stack_d, far_two, rows_d, MIDDLE)
    half_d = added(here_d, swapped(there_d, "ch", 1))
    own_there_c, own_here_c = conv(after(stack_c, there_d), own_two, rows_c, MIDDLE)
    half_d = after(half_d, own_here_c)
    sum_d = swapped(half_d, "ch", 2)
    own_there_d, own_here_d = conv(after(stack_d, half_d, sum_c), own_two, rows_d)
    here_d = call(add_kernel, "added", [sum_d, own_here_d], [f32(*sum_d.shape)], flops=HEAVY)[0]
    last_c, last_d = after((swapped(own_there_c, "ch", 1), swapped(own_there_d, "ch", 1)), here_d)

    quarter = length // 4
    pieces = call(
        pieces_kernel, "pieces", [sum_c, own_here_c, last_c, here_d, last_d],
        [f32(channels // GROUP, quarter)] * GROUP,
        [(channels // LANES, rows_c, LANES), (channels // LANES, rows_d, LANES), (quarter, channels)],
    )
    blocks = [pieces[0]] + [swapped(pieces[d], "seq", d) for d in range(1, GROUP)]
    shape = jax.ShapeDtypeStruct((1, channels // GROUP, GROUP * quarter), jnp.float32)
    return call(join_kernel, "join", blocks, [shape])[0]


def solution(mesh):
    return jax.shard_map(
        body,
        mesh=mesh,
        in_specs=(
            P("ch", "seq"),
            P("ch"),
            P("ch"),
            P(None, "ch", None),
            P("ch"),
            P("ch"),
            P(None, "ch", None),
        ),
        out_specs=P("seq", "ch", None),
        check_vma=False,
    )
```

time: 69.2 us -> 64 us (0.925)
  Pallas kernels: 38 us -> 31.7 us
  waiting for transfers between devices: 11.8 us -> 14.1 us
  starting transfers between devices: 17.2 us -> 16.3 us
    pallas_call x16 -> x21, Pallas kernels: 38 us -> 31.7 us  [the longest x20 25 us: call(): pl.pallas_call(kernel, in_specs=[VECTORS] * len(args), out_specs=[VECTORS...]
    ppermute x1, starting transfers between devices: 5.35 us -> 1.49 us  [body(): inner = lax.ppermute(to_inner, 'seq', [(i, i ^ 1) for i in range(n_seq)])]
    ppermute x15, starting transfers between devices: 11.1 us -> 14 us  [swapped(): return lax.ppermute(block, axis, [(i, i ^ bit) for i in range(count)])]
    ppermute x15, waiting for transfers between devices: 11.8 us -> 14.1 us  [swapped(): return lax.ppermute(block, axis, [(i, i ^ bit) for i in range(count)])]
    unnamed x36 -> x20, local copies, waits for them, and re-layouts: 1.31 us -> 1.44 us
  transfers between devices with their start and end apart: 17 -> 17, of which waited for: 6 -> 6; matrix products, arithmetic and copies ran while one was open for 0% -> 0% of each run, Pallas kernels for 33% -> 32%
where the time goes in v2:
time: 64 us; the launch traced here: 63.8 us
  Pallas kernels  31.7 us (50%)
  starting transfers between devices  16.3 us (25%)
  waiting for transfers between devices  14.1 us (22%)
  local copies, waits for them, and re-layouts  1.44 us (2%)
    pallas_call x20, Pallas kernels, call(): pl.pallas_call(kernel, in_specs=[VECTORS] * len(args), out_specs=[VECTORS...  25 us
    ppermute x15, waiting for transfers between devices, swapped(): return lax.ppermute(block, axis, [(i, i ^ bit) for i in range(count)])  14.1 us
    ppermute x15, starting transfers between devices, swapped(): return lax.ppermute(block, axis, [(i, i ^ bit) for i in range(count)])  14 us
    pallas_call x1, Pallas kernels, opening(): pl.pallas_call(opening_kernel, in_specs=[IN_HBM] * 4, out_specs=[VECTORS]...  6.7 us
    ppermute x1, starting transfers between devices, body(): inner = lax.ppermute(to_inner, 'seq', [(i, i ^ 1) for i in range(n_seq)])  1.49 us
    unnamed x20, local copies, waits for them, and re-layouts  1.44 us
  transfers between devices with their start and end apart: 17, of which 6 were waited for; matrix products, arithmetic and copies ran while one was open for 0% of the time, Pallas kernels for 32%

profile of v2, /device:TPU:0, one launch (start us, length us, event | category | flops | bytes accessed | tf_op | source)
XLA Modules:
  0.0 63.8 jit_solution(8178080800891971066)
XLA Ops:
  0.0 6.7 %opening.1 = (bf16[272,1920]{1,0:T(8,128)(2,1)S(1)}, bf16[272,1920]{1,0:T(8,128)(2,1)S(1)}, f32[8,384]{1,0:T(8,128)S(1)}, f32[8,384]{1,0:T(8,128)S(1)}, f32[8,38...) custom-call(f32[384]{0:T(512)} %gain_ref.3, ...), custom_call_target="tpu_custom_call" | custom-call | flops 1000000000 | tf_op jit(solution)/shard_map/opening/pallas_call | solution.py:131
  6.7 2.8 %conv.8 = (f32[264,384]{1,0:T(8,128)S(1)}, f32[264,384]{1,0:T(8,128)S(1)}) custom-call(bf16[272,1920]{1,0:T(8,128)(2,1)S(1)} %get-tuple-element.71.hi_ref, bf16[272,1920]{1,0:T(8,128)(2,1)S(1)} %get-tuple-element.72.lo_ref, bf16[1920,768]{1,0:T(8,128)(2,1)S(1)} %get-tuple-element.67.whi_ref, bf16[1920,768]{1,0:T(8,128)(2,1)S(1)} %get-tuple-element.68.wlo_ref), custom_call_target="tpu_custom_call" | custom-call | flops 1000000000 | tf_op jit(solution)/shard_map/conv/pallas_call | solution.py:41
  10.0 1.4 %collective-permute-done.b_ref = f32[264,384]{1,0:T(8,128)S(1)} collective-permute-done((f32[264,384]{1,0:T(8,128)S(1)}, f32[264,384]{1,0:T(8,128)S(1)}, u32[]{:S(2)}, u32[]{:S(2)}) %collective-permute-start) | collective-permute-done | bytes 405536 | tf_op jit(solution)/shard_map/ppermute | solution.py:55
  11.4 3.0 %collective-permute-start.1 = (f32[264,384]{1,0:T(8,128)S(1)}, f32[264,384]{1,0:T(8,128)S(1)}, u32[]{:S(2)}, u32[]{:S(2)}) collective-permute-start(f32[264,384]{1,0:T(8,128)S(1)} %added.5), channel_id=1, source_target_pairs={{0,2},{1,3},{2,0},{3,1},{4,6},{5,7},{6,4},{7,5},{8,10},{9,11},{10,... | collective-permute-start | bytes 1216520 | tf_op jit(solution)/shard_map/ppermute | solution.py:55
  14.4 1.5 %collective-permute-start.2 = (f32[8,384]{1,0:T(8,128)S(1)}, f32[8,384]{1,0:T(8,128)S(1)}, u32[]{:S(2)}, u32[]{:S(2)}) collective-permute-start(f32[8,384]{1,0:T(8,128)S(1)} %get-tuple-element.80), channel_id=1, source_target_pairs={{0,4},{4,0},{8,12},{12,8},{16,20},{20,16},{24,28},{28,24},{1,5},{5... | collective-permute-start | bytes 36872 | tf_op jit(solution)/shard_map/ppermute | solution.py:308
  15.9 0.8 %collective-permute-start.3 = (f32[8,384]{1,0:T(8,128)S(1)}, f32[8,384]{1,0:T(8,128)S(1)}, u32[]{:S(2)}, u32[]{:S(2)}) collective-permute-start(f32[8,384]{1,0:T(8,128)S(1)} %get-tuple-element.81), channel_id=1, source_target_pairs={{4,8},{8,4},{12,16},{16,12},{20,24},{24,20},{5,9},{9,5},{13,17},{1... | collective-permute-start | bytes 36872 | tf_op jit(solution)/shard_map/ppermute | solution.py:309
  16.7 2.8 %conv.9 = (f32[264,384]{1,0:T(8,128)S(1)}, f32[264,384]{1,0:T(8,128)S(1)}) custom-call(bf16[272,1920]{1,0:T(8,128)(2,1)S(1)} %get-tuple-element.71.hi_ref, bf16[272,1920]{1,0:T(8,128)(2,1)S(1)} %get-tuple-element.72.lo_ref, bf16[1920,768]{1,0:T(8,128)(2,1)S(1)} %get-tuple-element.73.whi_ref, bf16[1920,768]{1,0:T(8,128)(2,1)S(1)} %get-tuple-element.74.wlo_ref), custom_call_target="tpu_custom_call" | custom-call | flops 30000001024 | tf_op jit(solution)/shard_map/conv/pallas_call | solution.py:41
  20.4 2.8 %conv.10 = (f32[264,384]{1,0:T(8,128)S(1)}, f32[264,384]{1,0:T(8,128)S(1)}) custom-call(bf16[272,1920]{1,0:T(8,128)(2,1)S(1)} %get-tuple-element.90.hi_ref, bf16[272,1920]{1,0:T(8,128)(2,1)S(1)} %get-tuple-element.91.lo_ref, bf16[1920,768]{1,0:T(8,128)(2,1)S(1)} %get-tuple-element.67.whi_ref, bf16[1920,768]{1,0:T(8,128)(2,1)S(1)} %get-tuple-element.68.wlo_ref), custom_call_target="tpu_custom_call" | custom-call | flops 30000001024 | tf_op jit(solution)/shard_map/conv/pallas_call | solution.py:41
  24.3 1.1 %split_far.1 = (bf16[1920,768]{1,0:T(8,128)(2,1)S(1)}, bf16[1920,768]{1,0:T(8,128)(2,1)S(1)}) custom-call(f32[5,384,1536]{2,1,0:T(8,128)S(1)} %bitcast.1), custom_call_target="tpu_custom_call" | custom-call | flops 30000001024 | tf_op jit(solution)/shard_map/split_far/pallas_call | solution.py:41
  26.1 2.8 %conv.11 = (f32[264,384]{1,0:T(8,128)S(1)}, f32[264,384]{1,0:T(8,128)S(1)}) custom-call(bf16[272,1920]{1,0:T(8,128)(2,1)S(1)} %get-tuple-element.90.hi_ref, bf16[272,1920]{1,0:T(8,128)(2,1)S(1)} %get-tuple-element.91.lo_ref, bf16[1920,768]{1,0:T(8,128)(2,1)S(1)} %get-tuple-element.73.whi_ref, bf16[1920,768]{1,0:T(8,128)(2,1)S(1)} %get-tuple-element.74.wlo_ref), custom_call_target="tpu_custom_call" | custom-call | flops 1000000000 | tf_op jit(solution)/shard_map/conv/pallas_call | solution.py:41
  29.7 1.5 %conv.12 = (f32[128,384]{1,0:T(8,128)S(1)}, f32[128,384]{1,0:T(8,128)S(1)}) custom-call(bf16[128,1920]{1,0:T(8,128)(2,1)S(1)} %get-tuple-element.109.hi_ref, bf16[128,1920]{1,0:T(8,128)(2,1)S(1)} %get-tuple-element.110.lo_ref, bf16[1920,768]{1,0:T(8,128)(2,1)S(1)} %get-tuple-element.87.whi_ref, bf16[1920,768]{1,0:T(8,128)(2,1)S(1)} %get-tuple-element.88.wlo_ref), custom_call_target="tpu_custom_call" | custom-call | flops 1000000000 | tf_op jit(solution)/shard_map/conv/pallas_call | solution.py:41
  31.5 1.1 %split_own.1 = (bf16[1920,768]{1,0:T(8,128)(2,1)S(1)}, bf16[1920,768]{1,0:T(8,128)(2,1)S(1)}) custom-call(f32[5,384,1536]{2,1,0:T(8,128)S(1)} %bitcast.1), custom_call_target="tpu_custom_call" | custom-call | flops 1000000000 | tf_op jit(solution)/shard_map/split_own/pallas_call | solution.py:41
  32.7 1.6 %collective-permute-start.7 = (f32[128,384]{1,0:T(8,128)S(1)}, f32[128,384]{1,0:T(8,128)S(1)}, u32[]{:S(2)}, u32[]{:S(2)}) collective-permute-start(f32[128,384]{1,0:T(8,128)S(1)} %added.7), channel_id=1, source_target_pairs={{0,2},{1,3},{2,0},{3,1},{4,6},{5,7},{6,4},{7,5},{8,10},{9,11},{10,... | collective-permute-start | bytes 589832 | tf_op jit(solution)/shard_map/ppermute | solution.py:55
  34.3 3.4 %collective-permute-done.8.a_ref = f32[264,384]{1,0:T(8,128)S(1)} collective-permute-done((f32[264,384]{1,0:T(8,128)S(1)}, f32[264,384]{1,0:T(8,128)S(1)}, u32[]{:S(2)}, u32[]{:S(2)}) %collective-permute-start.8) | collective-permute-done | bytes 405536 | tf_op jit(solution)/shard_map/ppermute | solution.py:55
  38.6 1.6 %conv.13 = (f32[136,384]{1,0:T(8,128)S(1)}, f32[136,384]{1,0:T(8,128)S(1)}) custom-call(bf16[144,1920]{1,0:T(8,128)(2,1)S(1)} %get-tuple-element.115.hi_ref, bf16[144,1920]{1,0:T(8,128)(2,1)S(1)} %get-tuple-element.116.lo_ref, bf16[1920,768]{1,0:T(8,128)(2,1)S(1)} %get-tuple-element.87.whi_ref, bf16[1920,768]{1,0:T(8,128)(2,1)S(1)} %get-tuple-element.88.wlo_ref), custom_call_target="tpu_custom_call" | custom-call | flops 10000000000 | tf_op jit(solution)/shard_map/conv/pallas_call | solution.py:41
  40.3 2.1 %conv.14 = (f32[128,384]{1,0:T(8,128)}, f32[128,384]{1,0:T(8,128)S(1)}) custom-call(bf16[128,1920]{1,0:T(8,128)(2,1)S(1)} %get-tuple-element.109.hi_ref, bf16[128,1920]{1,0:T(8,128)(2,1)S(1)} %get-tuple-element.110.lo_ref, bf16[1920,768]{1,0:T(8,128)(2,1)S(1)} %get-tuple-element.100.whi_ref, bf16[1920,768]{1,0:T(8,128)(2,1)S(1)} %get-tuple-element.101.wlo_ref), custom_call_target="tpu_custom_call" | custom-call | flops 10000000000 | tf_op jit(solution)/shard_map/conv/pallas_call | solution.py:41
  43.2 2.3 %conv.15 = (f32[136,384]{1,0:T(8,128)}, f32[136,384]{1,0:T(8,128)S(1)}) custom-call(bf16[144,1920]{1,0:T(8,128)(2,1)S(1)} %get-tuple-element.115.hi_ref, bf16[144,1920]{1,0:T(8,128)(2,1)S(1)} %get-tuple-element.116.lo_ref, bf16[1920,768]{1,0:T(8,128)(2,1)S(1)} %get-tuple-element.100.whi_ref, bf16[1920,768]{1,0:T(8,128)(2,1)S(1)} %get-tuple-element.101.wlo_ref), custom_call_target="tpu_custom_call" | custom-call | flops 1000000000 | tf_op jit(solution)/shard_map/conv/pallas_call | solution.py:41
  45.8 4.3 %collective-permute-done.13.a_ref = f32[136,384]{1,0:T(8,128)S(1)} collective-permute-done((f32[136,384]{1,0:T(8,128)S(1)}, f32[136,384]{1,0:T(8,128)S(1)}, u32[]{:S(2)}, u32[]{:S(2)}) %collective-permute-start.13) | collective-permute-done | bytes 208928 | tf_op jit(solution)/shard_map/ppermute | solution.py:55
  50.1 0.9 %copy-done.4 = f32[128,384]{1,0:T(8,128)S(1)} copy-done((f32[128,384]{1,0:T(8,128)S(1)}, f32[128,384]{1,0:T(8,128)}, u32[]{:S(2)}) %copy-start.4) | copy-done | bytes 196632
  51.0 1.2 %pieces.1 = (f32[96,128]{1,0:T(8,128)S(1)}, f32[96,128]{1,0:T(8,128)S(1)}, f32[96,128]{1,0:T(8,128)S(1)}, f32[96,128]{1,0:T(8,128)S(1)}) custom-call(f32[128,384]{1,0:T(8,128)S(1)} %copy-done.4, f32[128,384]{1,0:T(8,128)S(1)} %get-tuple-element.111.refs_1_, f32[128,384]{1,0:T(8,128)} %collective-permute-done.10.refs_2_, f32[136,384]{1,0:T(8,128)S(1)} %added.9.refs_3_, ...), custom_call_target="tpu_custom_call" | custom-call | flops 1000000000 | tf_op jit(solution)/shard_map/pieces/pallas_call | solution.py:41
  52.2 4.4 %collective-permute-start.14 = (f32[96,128]{1,0:T(8,128)S(1)}, f32[96,128]{1,0:T(8,128)S(1)}, u32[]{:S(2)}, u32[]{:S(2)}) collective-permute-start(f32[96,128]{1,0:T(8,128)S(1)} %get-tuple-element.122), channel_id=1, source_target_pairs={{0,4},{4,0},{8,12},{12,8},{16,20},{20,16},{24,28},{28,24},{1,5},{5... | collective-permute-start | bytes 147464 | tf_op jit(solution)/shard_map/ppermute | solution.py:55
  56.6 1.6 %collective-permute-start.15 = (f32[96,128]{1,0:T(8,128)S(1)}, f32[96,128]{1,0:T(8,128)S(1)}, u32[]{:S(2)}, u32[]{:S(2)}) collective-permute-start(f32[96,128]{1,0:T(8,128)S(1)} %get-tuple-element.123), channel_id=1, source_target_pairs={{0,8},{4,12},{8,0},{12,4},{16,24},{20,28},{24,16},{28,20},{1,9},{5... | collective-permute-start | bytes 147464 | tf_op jit(solution)/shard_map/ppermute | solution.py:55
  58.6 2.1 %collective-permute-done.15.refs_2_ = f32[96,128]{1,0:T(8,128)S(1)} collective-permute-done((f32[96,128]{1,0:T(8,128)S(1)}, f32[96,128]{1,0:T(8,128)S(1)}, u32[]{:S(2)}, u32[]{:S(2)}) %collective-permute-start.15) | collective-permute-done | bytes 49184 | tf_op jit(solution)/shard_map/ppermute | solution.py:55
  60.7 2.4 %collective-permute-done.16.refs_3_ = f32[96,128]{1,0:T(8,128)S(1)} collective-permute-done((f32[96,128]{1,0:T(8,128)S(1)}, f32[96,128]{1,0:T(8,128)S(1)}, u32[]{:S(2)}, u32[]{:S(2)}) %collective-permute-start.16) | collective-permute-done | bytes 49184 | tf_op jit(solution)/shard_map/ppermute | solution.py:55
  (52 shorter events, 7.5 us)
Async XLA Ops:
  9.5 1.9 %collective-permute-start = (f32[264,384]{1,0:T(8,128)S(1)}, f32[264,384]{1,0:T(8,128)S(1)}, u32[]{:S(2)}, u32[]{:S(2)}) collective-permute-start(f32[264,384]{1,0:T(8,128)S(1)} %get-tuple-element.70), channel_id=1, source_target_pairs={{0,1},{1,0},{2,3},{3,2},{4,5},{5,4},{6,7},{7,6},{8,9},{9,8},{10,11... | collective-permute-start | bytes 1216520 | tf_op jit(solution)/shard_map/ppermute | solution.py:55
  11.4 17.4 %collective-permute-start.1 = (f32[264,384]{1,0:T(8,128)S(1)}, f32[264,384]{1,0:T(8,128)S(1)}, u32[]{:S(2)}, u32[]{:S(2)}) collective-permute-start(f32[264,384]{1,0:T(8,128)S(1)} %added.5), channel_id=1, source_target_pairs={{0,2},{1,3},{2,0},{3,1},{4,6},{5,7},{6,4},{7,5},{8,10},{9,11},{10,... | collective-permute-start | bytes 1216520 | tf_op jit(solution)/shard_map/ppermute | solution.py:55
  14.4 5.2 %collective-permute-start.2 = (f32[8,384]{1,0:T(8,128)S(1)}, f32[8,384]{1,0:T(8,128)S(1)}, u32[]{:S(2)}, u32[]{:S(2)}) collective-permute-start(f32[8,384]{1,0:T(8,128)S(1)} %get-tuple-element.80), channel_id=1, source_target_pairs={{0,4},{4,0},{8,12},{12,8},{16,20},{20,16},{24,28},{28,24},{1,5},{5... | collective-permute-start | bytes 36872 | tf_op jit(solution)/shard_map/ppermute | solution.py:308
  15.9 3.7 %collective-permute-start.3 = (f32[8,384]{1,0:T(8,128)S(1)}, f32[8,384]{1,0:T(8,128)S(1)}, u32[]{:S(2)}, u32[]{:S(2)}) collective-permute-start(f32[8,384]{1,0:T(8,128)S(1)} %get-tuple-element.81), channel_id=1, source_target_pairs={{4,8},{8,4},{12,16},{16,12},{20,24},{24,20},{5,9},{9,5},{13,17},{1... | collective-permute-start | bytes 36872 | tf_op jit(solution)/shard_map/ppermute | solution.py:309
  16.7 2.9 %copy-start = (f32[384,512]{1,0:T(8,128)S(1)}, f32[384,512]{1,0:T(8,128)}, u32[]{:S(2)}) copy-start(f32[384,512]{1,0:T(8,128)} %x_ref) | copy-start | bytes 2359300
  16.7 2.9 %copy-start.1 = (f32[384]{0:T(512)S(1)}, f32[384]{0:T(512)}, u32[]{:S(2)}) copy-start(f32[384]{0:T(512)} %gain_ref.3) | copy-start | bytes 4612
  19.5 9.6 %collective-permute-start.5 = (f32[264,384]{1,0:T(8,128)S(1)}, f32[264,384]{1,0:T(8,128)S(1)}, u32[]{:S(2)}, u32[]{:S(2)}) collective-permute-start(f32[264,384]{1,0:T(8,128)S(1)} %get-tuple-element.94), channel_id=1, source_target_pairs={{0,1},{1,0},{2,3},{3,2},{4,5},{5,4},{6,7},{7,6},{8,9},{9,8},{10,11... | collective-permute-start | bytes 1216520 | tf_op jit(solution)/shard_map/ppermute | solution.py:55
  19.6 4.1 %slice-start = ((s8[11796480]{0:T(1024)(128)(4,1)}), s8[4194304]{0:T(1024)(128)(4,1)S(1)}, s32[]{:S(2)}) async-start(s8[11796480]{0:T(1024)(128)(4,1)} %bitcast), calls=%async_computation | async-start | bytes 8388608
  19.6 4.1 %slice-start.1 = ((s8[11796480]{0:T(1024)(128)(4,1)}), s8[4194304]{0:T(1024)(128)(4,1)S(1)}, s32[]{:S(2)}) async-start(s8[11796480]{0:T(1024)(128)(4,1)} %bitcast), calls=%async_computation.1 | async-start | bytes 8388608
  20.4 3.8 %slice-start.2 = ((s8[11796480]{0:T(1024)(128)(4,1)}), s8[3407872]{0:T(1024)(128)(4,1)S(1)}, s32[]{:S(2)}) async-start(s8[11796480]{0:T(1024)(128)(4,1)} %bitcast), calls=%async_computation.2 | async-start | bytes 6815744
  23.2 2.2 %collective-permute-start.4 = (f32[264,384]{1,0:T(8,128)S(1)}, f32[264,384]{1,0:T(8,128)S(1)}, u32[]{:S(2)}, u32[]{:S(2)}) collective-permute-start(f32[264,384]{1,0:T(8,128)S(1)} %get-tuple-element.85), channel_id=1, source_target_pairs={{0,1},{1,0},{2,3},{3,2},{4,5},{5,4},{6,7},{7,6},{8,9},{9,8},{10,11... | collective-permute-start | bytes 1216520 | tf_op jit(solution)/shard_map/ppermute | solution.py:55
  25.5 3.7 %copy-start.5 = (f32[384]{0:T(512)S(1)}, f32[384]{0:T(512)}, u32[]{:S(2)}) copy-start(f32[384]{0:T(512)} %gain_ref.5) | copy-start | bytes 4612
  25.5 3.6 %copy-start.6 = (f32[384]{0:T(512)S(1)}, f32[384]{0:T(512)}, u32[]{:S(2)}) copy-start(f32[384]{0:T(512)} %shift_ref.5) | copy-start | bytes 4612
  25.5 12.2 %collective-permute-start.8 = (f32[264,384]{1,0:T(8,128)S(1)}, f32[264,384]{1,0:T(8,128)S(1)}, u32[]{:S(2)}, u32[]{:S(2)}) collective-permute-start(f32[264,384]{1,0:T(8,128)S(1)} %added.6), channel_id=1, source_target_pairs={{0,2},{1,3},{2,0},{3,1},{4,6},{5,7},{6,4},{7,5},{8,10},{9,11},{10,... | collective-permute-start | bytes 1216520 | tf_op jit(solution)/shard_map/ppermute | solution.py:55
  28.9 8.9 %collective-permute-start.9 = (f32[264,384]{1,0:T(8,128)S(1)}, f32[264,384]{1,0:T(8,128)S(1)}, u32[]{:S(2)}, u32[]{:S(2)}) collective-permute-start(f32[264,384]{1,0:T(8,128)S(1)} %get-tuple-element.104), channel_id=1, source_target_pairs={{0,1},{1,0},{2,3},{3,2},{4,5},{5,4},{6,7},{7,6},{8,9},{9,8},{10,11... | collective-permute-start | bytes 1216520 | tf_op jit(solution)/shard_map/ppermute | solution.py:55
  31.2 1.5 %collective-permute-start.6 = (f32[128,384]{1,0:T(8,128)S(1)}, f32[128,384]{1,0:T(8,128)S(1)}, u32[]{:S(2)}, u32[]{:S(2)}) collective-permute-start(f32[128,384]{1,0:T(8,128)S(1)} %get-tuple-element.98), channel_id=1, source_target_pairs={{0,1},{1,0},{2,3},{3,2},{4,5},{5,4},{6,7},{7,6},{8,9},{9,8},{10,11... | collective-permute-start | bytes 589832 | tf_op jit(solution)/shard_map/ppermute | solution.py:55
  32.7 10.5 %collective-permute-start.7 = (f32[128,384]{1,0:T(8,128)S(1)}, f32[128,384]{1,0:T(8,128)S(1)}, u32[]{:S(2)}, u32[]{:S(2)}) collective-permute-start(f32[128,384]{1,0:T(8,128)S(1)} %added.7), channel_id=1, source_target_pairs={{0,2},{1,3},{2,0},{3,1},{4,6},{5,7},{6,4},{7,5},{8,10},{9,11},{10,... | collective-permute-start | bytes 589832 | tf_op jit(solution)/shard_map/ppermute | solution.py:55
  40.2 2.2 %collective-permute-start.11 = (f32[136,384]{1,0:T(8,128)S(1)}, f32[136,384]{1,0:T(8,128)S(1)}, u32[]{:S(2)}, u32[]{:S(2)}) collective-permute-start(f32[136,384]{1,0:T(8,128)S(1)} %get-tuple-element.108), channel_id=1, source_target_pairs={{0,1},{1,0},{2,3},{3,2},{4,5},{5,4},{6,7},{7,6},{8,9},{9,8},{10,11... | collective-permute-start | bytes 626696 | tf_op jit(solution)/shard_map/ppermute | solution.py:55
  42.4 7.6 %collective-permute-start.13 = (f32[136,384]{1,0:T(8,128)S(1)}, f32[136,384]{1,0:T(8,128)S(1)}, u32[]{:S(2)}, u32[]{:S(2)}) collective-permute-start(f32[136,384]{1,0:T(8,128)S(1)} %added.8), channel_id=1, source_target_pairs={{0,2},{1,3},{2,0},{3,1},{4,6},{5,7},{6,4},{7,5},{8,10},{9,11},{10,... | collective-permute-start | bytes 626696 | tf_op jit(solution)/shard_map/ppermute | solution.py:55
  43.0 7.1 %collective-permute-start.10 = (f32[128,384]{1,0:T(8,128)}, f32[128,384]{1,0:T(8,128)}, u32[]{:S(2)}, u32[]{:S(2)}) collective-permute-start(f32[128,384]{1,0:T(8,128)} %get-tuple-element.112), channel_id=1, source_target_pairs={{0,1},{1,0},{2,3},{3,2},{4,5},{5,4},{6,7},{7,6},{8,9},{9,8},{10,11... | collective-permute-start | bytes 589832 | tf_op jit(solution)/shard_map/ppermute | solution.py:55
  45.5 4.6 %collective-permute-start.12 = (f32[136,384]{1,0:T(8,128)}, f32[136,384]{1,0:T(8,128)}, u32[]{:S(2)}, u32[]{:S(2)}) collective-permute-start(f32[136,384]{1,0:T(8,128)} %get-tuple-element.117), channel_id=1, source_target_pairs={{0,1},{1,0},{2,3},{3,2},{4,5},{5,4},{6,7},{7,6},{8,9},{9,8},{10,11... | collective-permute-start | bytes 626696 | tf_op jit(solution)/shard_map/ppermute | solution.py:55
  52.2 6.4 %collective-permute-start.14 = (f32[96,128]{1,0:T(8,128)S(1)}, f32[96,128]{1,0:T(8,128)S(1)}, u32[]{:S(2)}, u32[]{:S(2)}) collective-permute-start(f32[96,128]{1,0:T(8,128)S(1)} %get-tuple-element.122), channel_id=1, source_target_pairs={{0,4},{4,0},{8,12},{12,8},{16,20},{20,16},{24,28},{28,24},{1,5},{5... | collective-permute-start | bytes 147464 | tf_op jit(solution)/shard_map/ppermute | solution.py:55
  56.6 4.2 %collective-permute-start.15 = (f32[96,128]{1,0:T(8,128)S(1)}, f32[96,128]{1,0:T(8,128)S(1)}, u32[]{:S(2)}, u32[]{:S(2)}) collective-permute-start(f32[96,128]{1,0:T(8,128)S(1)} %get-tuple-element.123), channel_id=1, source_target_pairs={{0,8},{4,12},{8,0},{12,4},{16,24},{20,28},{24,16},{28,20},{1,9},{5... | collective-permute-start | bytes 147464 | tf_op jit(solution)/shard_map/ppermute | solution.py:55
  58.2 5.0 %collective-permute-start.16 = (f32[96,128]{1,0:T(8,128)S(1)}, f32[96,128]{1,0:T(8,128)S(1)}, u32[]{:S(2)}, u32[]{:S(2)}) collective-permute-start(f32[96,128]{1,0:T(8,128)S(1)} %get-tuple-element.124), channel_id=1, source_target_pairs={{0,12},{4,8},{8,4},{12,0},{16,28},{20,24},{24,20},{28,16},{1,13},{... | collective-permute-start | bytes 147464 | tf_op jit(solution)/shard_map/ppermute | solution.py:55
  (3 other events, 6.1 us)

commit v3 on v2

--- a/solution.py
+++ b/solution.py
@@ -10,7 +10,7 @@
 KW = 5
 GROUP = 4
 EDGE = 8
-CHUNK = 264
+CHUNK = 296
 LANES = 128
 VMEM_LIMIT = 2 * 1024 * 1024
 VECTORS = pl.BlockSpec(memory_space=pltpu.VMEM)
@@ -77,12 +77,15 @@
     return -(-rows // 16) * 16
 
 
-def split_tap(tap, w_ref, outs, far):
-    channels, owned = w_ref.shape[0], w_ref.shape[1] // 4
-    hi_ref, lo_ref = outs
-    ch = lax.axis_index("ch")
-    high, core = (1 - ch // 2 if far else ch // 2), ch % 2
-    for half, owner in enumerate((2 * high + 1 - core, 2 * high + core)):
+def half_columns(outs, far):
+    high = lax.axis_index("ch") // 2
+    return pl.ds(pl.multiple_of((1 - high if far else high) * (outs // 2), LANES), outs // 2)
+
+
+def split_tap(tap, w_ref, hi_ref, lo_ref):
+    channels, owned = w_ref.shape[0], w_ref.shape[1] // 2
+    core = lax.axis_index("ch") % 2
+    for half, owner in enumerate((1 - core, core)):
         weight = w_ref[:, pl.ds(pl.multiple_of(owner * owned, LANES), owned)]
         hi = weight.astype(jnp.bfloat16)
         place = (slice(tap * channels, (tap + 1) * channels), slice(half * owned, (half + 1) * owned))
@@ -90,16 +93,18 @@
         lo_ref[place] = (weight - hi.astype(jnp.float32)).astype(jnp.bfloat16)
 
 
-def opening_kernel(gain_hbm, shift_hbm, x_hbm, w_hbm, hi_ref, lo_ref, head_ref, inner_ref, outer_ref,
-                   far_hi, far_lo, own_hi, own_lo,
-                   x_ref, gain_ref, shift_ref, act_ref, w_ref, x_sem, w_sem):
+def opening_kernel(gain_hbm, shift_hbm, x_hbm, w_hbm, hi_ref, lo_ref, head_ref, inner_ref, outer_ref, far_hi, far_lo,
+                                      x_ref, gain_ref, shift_ref, act_ref, w_ref, x_sem, w_sem):
     length = x_ref.shape[1]
     gets = [
         pltpu.make_async_copy(src, dst, x_sem.at[i])
         for i, (src, dst) in enumerate(((gain_hbm, gain_ref), (shift_hbm, shift_ref), (x_hbm, x_ref)))
     ]
-    copies = [pltpu.make_async_copy(w_hbm.at[tap], w_ref.at[tap], w_sem.at[tap]) for tap in range(KW)]
-    ahead = 2
+    cols = half_columns(w_hbm.shape[2], True)
+    copies = [
+        pltpu.make_async_copy(w_hbm.at[tap, :, cols], w_ref.at[tap], w_sem.at[tap]) for tap in range(KW)
+    ]
+    ahead = KW
     for copy in gets + copies[:ahead]:
         copy.start()
     for copy in gets:
@@ -118,8 +123,7 @@
         copy.wait()
         if tap + ahead < KW:
             copies[tap + ahead].start()
-        split_tap(tap, w_ref.at[tap], (far_hi, far_lo), True)
-        split_tap(tap, w_ref.at[tap], (own_hi, own_lo), False)
+        split_tap(tap, w_ref.at[tap], far_hi, far_lo)
 
 
 def opening(features, gain, shift, weight, rows):
@@ -131,18 +135,18 @@
     return pl.pallas_call(
         opening_kernel,
         in_specs=[IN_HBM] * 4,
-        out_specs=[VECTORS] * 9,
-        out_shape=[stack] * 2 + [f32(EDGE, channels)] * 3 + [split] * 4,
+        out_specs=[VECTORS] * 7,
+        out_shape=[stack] * 2 + [f32(EDGE, channels)] * 3 + [split] * 2,
         scratch_shapes=[
             pltpu.VMEM((channels, length), jnp.float32),
             pltpu.VMEM((channels,), jnp.float32),
             pltpu.VMEM((channels,), jnp.float32),
             pltpu.VMEM((span, channels), jnp.float32),
-            pltpu.VMEM((KW, channels, outs), jnp.float32),
+            pltpu.VMEM((KW, channels, outs // 2), jnp.float32),
             pltpu.SemaphoreType.DMA((3,)),
             pltpu.SemaphoreType.DMA((KW,)),
         ],
-        compiler_params=pltpu.CompilerParams(vmem_limit_bytes=16 * 1024 * 1024),
+        compiler_params=pltpu.CompilerParams(vmem_limit_bytes=10 * 1024 * 1024),
         cost_estimate=cost(LIGHT),
         name="opening",
     )(*map(in_hbm, (gain, shift, features, weight)))
@@ -166,12 +170,16 @@
 
 
 def split_kernel(w_ref, hi_ref, lo_ref, *, far):
+    outs = 2 * hi_ref.shape[1]
     for tap in range(KW):
-        split_tap(tap, w_ref.at[tap], (hi_ref, lo_ref), far)
-
-
-def split_weight(weight, far, flops=LIGHT):
-    _, channels, outs = weight.shape
+        block = w_ref.at[tap]
+        if w_ref.shape[2] == outs:
+            block = block.at[:, half_columns(outs, far)]
+        split_tap(tap, block, hi_ref, lo_ref)
+
+
+def split_weight(weight, outs, far, flops=LIGHT):
+    _, channels, _ = weight.shape
     return call(
         functools.partial(split_kernel, far=far), "split_far" if far else "split_own", [weight],
         [bf16(KW * channels, outs // 2)] * 2, flops=flops,
@@ -298,10 +306,12 @@
     depth = KW * channels
     rows_a, rows_b, rows_c, rows_d = row_plan(length, CHUNK)
 
-    hi_a, lo_a, head, to_inner, to_outer, *split_one = opening(features, *one, wide_one, rows_a)
-    far_one, own_one = split_one[:2], split_one[2:]
+    outs = wide_one.shape[2]
+
+    hi_a, lo_a, head, to_inner, to_outer, *far_one = opening(features, *one, wide_one, rows_a)
     there_a, here_a = conv((hi_a, lo_a), far_one, rows_a)
-    half_a = added(here_a, swapped(there_a, "ch", 1))
+    own_one = split_weight(after(wide_one, there_a), outs, False)
+    half_a = after(added(here_a, swapped(there_a, "ch", 1)), own_one)
     sum_a = swapped(half_a, "ch", 2)
 
     to_inner, to_outer = after((to_inner, to_outer), half_a)
@@ -318,7 +328,7 @@
     )
     there_b, here_b = conv(stack_b, far_one, rows_b, EARLY)
     half_b = added(here_b, swapped(there_b, "ch", 1))
-    far_two = split_weight(after(wide_two, there_b), True, EARLY)
+    far_two = split_weight(after(wide_two, there_b), outs, True, EARLY)
     half_b = after(half_b, far_two)
     sum_b = swapped(half_b, "ch", 2)
 
@@ -331,7 +341,7 @@
         [(channels // LANES, rows_a, LANES), (padded(rows_c) + 8, channels)],
     )
     there_c, here_c = conv(stack_c, far_two, rows_c)
-    own_two = split_weight(after(wide_two, there_c), False)
+    own_two = split_weight(after(wide_two, there_c), outs, False)
     half_c = added(here_c, swapped(there_c, "ch", 1))
     half_c = after(half_c, own_two)
     sum_c = swapped(half_c, "ch", 2)

time: 64 us -> 58.8 us (0.919)
  Pallas kernels: 31.7 us -> 29.5 us
  waiting for transfers between devices: 14.1 us -> 12.1 us
    pallas_call x1, Pallas kernels: 6.7 us -> 3.39 us  [opening(): pl.pallas_call(opening_kernel, in_specs=[IN_HBM] * 4, out_specs=[VECTORS]...]
    ppermute x15, waiting for transfers between devices: 14.1 us -> 12.1 us  [swapped(): return lax.ppermute(block, axis, [(i, i ^ bit) for i in range(count)])]
    pallas_call x20 -> x21, Pallas kernels: 25 us -> 26.1 us  [call(): pl.pallas_call(kernel, in_specs=[VECTORS] * len(args), out_specs=[VECTORS...]
    unnamed x20 -> x18, local copies, waits for them, and re-layouts: 1.44 us -> 0.92 us
  transfers between devices with their start and end apart: 17 -> 17, of which waited for: 6 -> 6; matrix products, arithmetic and copies ran while one was open for 0% -> 0% of each run, Pallas kernels for 32% -> 36%
where the time goes in v3:
time: 58.8 us; the launch traced here: 58.7 us
  Pallas kernels  29.5 us (50%)
  starting transfers between devices  15.9 us (27%)
  waiting for transfers between devices  12.1 us (21%)
  local copies, waits for them, and re-layouts  0.92 us (2%)
    pallas_call x21, Pallas kernels, call(): pl.pallas_call(kernel, in_specs=[VECTORS] * len(args), out_specs=[VECTORS...  26.1 us
    ppermute x15, starting transfers between devices, swapped(): return lax.ppermute(block, axis, [(i, i ^ bit) for i in range(count)])  13.5 us
    ppermute x15, waiting for transfers between devices, swapped(): return lax.ppermute(block, axis, [(i, i ^ bit) for i in range(count)])  12.1 us
    pallas_call x1, Pallas kernels, opening(): pl.pallas_call(opening_kernel, in_specs=[IN_HBM] * 4, out_specs=[VECTORS]...  3.39 us
    ppermute x1, starting transfers between devices, body(): inner = lax.ppermute(to_inner, 'seq', [(i, i ^ 1) for i in range(n_seq)])  1.49 us
  transfers between devices with their start and end apart: 17, of which 6 were waited for; matrix products, arithmetic and copies ran while one was open for 0% of the time, Pallas kernels for 36%

profile of v3, /device:TPU:0, one launch (start us, length us, event | category | flops | bytes accessed | tf_op | source)
XLA Modules:
  0.0 58.7 jit_solution(8707875189452757115)
XLA Ops:
  0.0 3.4 %opening.1 = (bf16[304,1920]{1,0:T(8,128)(2,1)S(1)}, bf16[304,1920]{1,0:T(8,128)(2,1)S(1)}, f32[8,384]{1,0:T(8,128)S(1)}, f32[8,384]{1,0:T(8,128)S(1)}, f32[8,38...) custom-call(f32[384]{0:T(512)} %gain_ref.3, f32[384]{0:T(512)} %shift_ref.3, ...), custom_call_target="tpu_custom_call" | custom-call | flops 1000000000 | tf_op jit(solution)/shard_map/opening/pallas_call | solution.py:135
  3.4 3.0 %conv.8 = (f32[296,384]{1,0:T(8,128)S(1)}, f32[296,384]{1,0:T(8,128)S(1)}) custom-call(bf16[304,1920]{1,0:T(8,128)(2,1)S(1)} %get-tuple-element.77.hi_ref, bf16[304,1920]{1,0:T(8,128)(2,1)S(1)} %get-tuple-element.78.lo_ref, bf16[1920,768]{1,0:T(8,128)(2,1)S(1)} %get-tuple-element.69.whi_ref, bf16[1920,768]{1,0:T(8,128)(2,1)S(1)} %get-tuple-element.70.wlo_ref), custom_call_target="tpu_custom_call" | custom-call | flops 1000000000 | tf_op jit(solution)/shard_map/conv/pallas_call | solution.py:41
  7.0 1.1 %split_own.2 = (bf16[1920,768]{1,0:T(8,128)(2,1)S(1)}, bf16[1920,768]{1,0:T(8,128)(2,1)S(1)}) custom-call(f32[5,384,1536]{2,1,0:T(8,128)S(1)} %copy-done), custom_call_target="tpu_custom_call" | custom-call | flops 1000000000 | tf_op jit(solution)/shard_map/split_own/pallas_call | solution.py:41
  8.5 3.0 %collective-permute-start.1 = (f32[296,384]{1,0:T(8,128)S(1)}, f32[296,384]{1,0:T(8,128)S(1)}, u32[]{:S(2)}, u32[]{:S(2)}) collective-permute-start(f32[296,384]{1,0:T(8,128)S(1)} %added.5), channel_id=1, source_target_pairs={{0,2},{1,3},{2,0},{3,1},{4,6},{5,7},{6,4},{7,5},{8,10},{9,11},{10,... | collective-permute-start | bytes 1363976 | tf_op jit(solution)/shard_map/ppermute | solution.py:55
  11.4 1.5 %collective-permute-start.2 = (f32[8,384]{1,0:T(8,128)S(1)}, f32[8,384]{1,0:T(8,128)S(1)}, u32[]{:S(2)}, u32[]{:S(2)}) collective-permute-start(f32[8,384]{1,0:T(8,128)S(1)} %get-tuple-element.84), channel_id=1, source_target_pairs={{0,4},{4,0},{8,12},{12,8},{16,20},{20,16},{24,28},{28,24},{1,5},{5... | collective-permute-start | bytes 36872 | tf_op jit(solution)/shard_map/ppermute | solution.py:318
  12.9 0.8 %collective-permute-start.3 = (f32[8,384]{1,0:T(8,128)S(1)}, f32[8,384]{1,0:T(8,128)S(1)}, u32[]{:S(2)}, u32[]{:S(2)}) collective-permute-start(f32[8,384]{1,0:T(8,128)S(1)} %get-tuple-element.85), channel_id=1, source_target_pairs={{4,8},{8,4},{12,16},{16,12},{20,24},{24,20},{5,9},{9,5},{13,17},{1... | collective-permute-start | bytes 36872 | tf_op jit(solution)/shard_map/ppermute | solution.py:319
  13.8 3.0 %conv.9 = (f32[296,384]{1,0:T(8,128)S(1)}, f32[296,384]{1,0:T(8,128)S(1)}) custom-call(bf16[304,1920]{1,0:T(8,128)(2,1)S(1)} %get-tuple-element.77.hi_ref, bf16[304,1920]{1,0:T(8,128)(2,1)S(1)} %get-tuple-element.78.lo_ref, bf16[1920,768]{1,0:T(8,128)(2,1)S(1)} %get-tuple-element.74.whi_ref, bf16[1920,768]{1,0:T(8,128)(2,1)S(1)} %get-tuple-element.75.wlo_ref), custom_call_target="tpu_custom_call" | custom-call | flops 30000001024 | tf_op jit(solution)/shard_map/conv/pallas_call | solution.py:41
  17.7 2.5 %conv.10 = (f32[232,384]{1,0:T(8,128)S(1)}, f32[232,384]{1,0:T(8,128)S(1)}) custom-call(bf16[240,1920]{1,0:T(8,128)(2,1)S(1)} %get-tuple-element.94.hi_ref, bf16[240,1920]{1,0:T(8,128)(2,1)S(1)} %get-tuple-element.95.lo_ref, bf16[1920,768]{1,0:T(8,128)(2,1)S(1)} %get-tuple-element.69.whi_ref, bf16[1920,768]{1,0:T(8,128)(2,1)S(1)} %get-tuple-element.70.wlo_ref), custom_call_target="tpu_custom_call" | custom-call | flops 30000001024 | tf_op jit(solution)/shard_map/conv/pallas_call | solution.py:41
  20.7 0.9 %slice-done.2 = s8[3407872]{0:T(1024)(128)(4,1)S(1)} async-done(((s8[11796480]{0:T(1024)(128)(4,1)}), s8[3407872]{0:T(1024)(128)(4,1)S(1)}, s32[]{:S(2)}) %slice-start.2) | async-done | bytes 3407896
  21.6 1.1 %split_far.1 = (bf16[1920,768]{1,0:T(8,128)(2,1)S(1)}, bf16[1920,768]{1,0:T(8,128)(2,1)S(1)}) custom-call(f32[5,384,1536]{2,1,0:T(8,128)S(1)} %bitcast.1), custom_call_target="tpu_custom_call" | custom-call | flops 30000001024 | tf_op jit(solution)/shard_map/split_far/pallas_call | solution.py:41
  23.4 2.5 %conv.11 = (f32[232,384]{1,0:T(8,128)S(1)}, f32[232,384]{1,0:T(8,128)S(1)}) custom-call(bf16[240,1920]{1,0:T(8,128)(2,1)S(1)} %get-tuple-element.94.hi_ref, bf16[240,1920]{1,0:T(8,128)(2,1)S(1)} %get-tuple-element.95.lo_ref, bf16[1920,768]{1,0:T(8,128)(2,1)S(1)} %get-tuple-element.74.whi_ref, bf16[1920,768]{1,0:T(8,128)(2,1)S(1)} %get-tuple-element.75.wlo_ref), custom_call_target="tpu_custom_call" | custom-call | flops 1000000000 | tf_op jit(solution)/shard_map/conv/pallas_call | solution.py:41
  26.7 1.6 %conv.12 = (f32[144,384]{1,0:T(8,128)S(1)}, f32[144,384]{1,0:T(8,128)S(1)}) custom-call(bf16[144,1920]{1,0:T(8,128)(2,1)S(1)} %get-tuple-element.113.hi_ref, bf16[144,1920]{1,0:T(8,128)(2,1)S(1)} %get-tuple-element.114.lo_ref, bf16[1920,768]{1,0:T(8,128)(2,1)S(1)} %get-tuple-element.91.whi_ref, bf16[1920,768]{1,0:T(8,128)(2,1)S(1)} %get-tuple-element.92.wlo_ref), custom_call_target="tpu_custom_call" | custom-call | flops 1000000000 | tf_op jit(solution)/shard_map/conv/pallas_call | solution.py:41
  28.7 1.1 %split_own.3 = (bf16[1920,768]{1,0:T(8,128)(2,1)S(1)}, bf16[1920,768]{1,0:T(8,128)(2,1)S(1)}) custom-call(f32[5,384,1536]{2,1,0:T(8,128)S(1)} %bitcast.1), custom_call_target="tpu_custom_call" | custom-call | flops 1000000000 | tf_op jit(solution)/shard_map/split_own/pallas_call | solution.py:41
  29.9 1.6 %collective-permute-start.7 = (f32[144,384]{1,0:T(8,128)S(1)}, f32[144,384]{1,0:T(8,128)S(1)}, u32[]{:S(2)}, u32[]{:S(2)}) collective-permute-start(f32[144,384]{1,0:T(8,128)S(1)} %added.7), channel_id=1, source_target_pairs={{0,2},{1,3},{2,0},{3,1},{4,6},{5,7},{6,4},{7,5},{8,10},{9,11},{10,... | collective-permute-start | bytes 663560 | tf_op jit(solution)/shard_map/ppermute | solution.py:55
  31.5 2.5 %collective-permute-done.8.a_ref = f32[232,384]{1,0:T(8,128)S(1)} collective-permute-done((f32[232,384]{1,0:T(8,128)S(1)}, f32[232,384]{1,0:T(8,128)S(1)}, u32[]{:S(2)}, u32[]{:S(2)}) %collective-permute-start.8) | collective-permute-done | bytes 356384 | tf_op jit(solution)/shard_map/ppermute | solution.py:55
  34.7 1.5 %conv.13 = (f32[120,384]{1,0:T(8,128)S(1)}, f32[120,384]{1,0:T(8,128)S(1)}) custom-call(bf16[128,1920]{1,0:T(8,128)(2,1)S(1)} %get-tuple-element.119.hi_ref, bf16[128,1920]{1,0:T(8,128)(2,1)S(1)} %get-tuple-element.120.lo_ref, bf16[1920,768]{1,0:T(8,128)(2,1)S(1)} %get-tuple-element.91.whi_ref, bf16[1920,768]{1,0:T(8,128)(2,1)S(1)} %get-tuple-element.92.wlo_ref), custom_call_target="tpu_custom_call" | custom-call | flops 10000000000 | tf_op jit(solution)/shard_map/conv/pallas_call | solution.py:41
  36.3 2.3 %conv.14 = (f32[144,384]{1,0:T(8,128)}, f32[144,384]{1,0:T(8,128)S(1)}) custom-call(bf16[144,1920]{1,0:T(8,128)(2,1)S(1)} %get-tuple-element.113.hi_ref, bf16[144,1920]{1,0:T(8,128)(2,1)S(1)} %get-tuple-element.114.lo_ref, bf16[1920,768]{1,0:T(8,128)(2,1)S(1)} %get-tuple-element.104.whi_ref, bf16[1920,768]{1,0:T(8,128)(2,1)S(1)} %get-tuple-element.105.wlo_ref), custom_call_target="tpu_custom_call" | custom-call | flops 10000000000 | tf_op jit(solution)/shard_map/conv/pallas_call | solution.py:41
  39.3 2.2 %conv.15 = (f32[120,384]{1,0:T(8,128)}, f32[120,384]{1,0:T(8,128)S(1)}) custom-call(bf16[128,1920]{1,0:T(8,128)(2,1)S(1)} %get-tuple-element.119.hi_ref, bf16[128,1920]{1,0:T(8,128)(2,1)S(1)} %get-tuple-element.120.lo_ref, bf16[1920,768]{1,0:T(8,128)(2,1)S(1)} %get-tuple-element.104.whi_ref, bf16[1920,768]{1,0:T(8,128)(2,1)S(1)} %get-tuple-element.105.wlo_ref), custom_call_target="tpu_custom_call" | custom-call | flops 1000000000 | tf_op jit(solution)/shard_map/conv/pallas_call | solution.py:41
  41.5 4.2 %collective-permute-done.13.a_ref = f32[120,384]{1,0:T(8,128)S(1)} collective-permute-done((f32[120,384]{1,0:T(8,128)S(1)}, f32[120,384]{1,0:T(8,128)S(1)}, u32[]{:S(2)}, u32[]{:S(2)}) %collective-permute-start.13) | collective-permute-done | bytes 184352 | tf_op jit(solution)/shard_map/ppermute | solution.py:55
  45.8 1.2 %pieces.1 = (f32[96,128]{1,0:T(8,128)S(1)}, f32[96,128]{1,0:T(8,128)S(1)}, f32[96,128]{1,0:T(8,128)S(1)}, f32[96,128]{1,0:T(8,128)S(1)}) custom-call(f32[144,384]{1,0:T(8,128)S(1)} %collective-permute-done.7.refs_0_, f32[144,384]{1,0:T(8,128)S(1)} %get-tuple-element.115.refs_1_, f32[144,384]{1,0:T(8,128)} %collective-permute-done.10.refs_2_, ...), custom_call_target="tpu_custom_call" | custom-call | flops 1000000000 | tf_op jit(solution)/shard_map/pieces/pallas_call | solution.py:41
  47.0 4.4 %collective-permute-start.14 = (f32[96,128]{1,0:T(8,128)S(1)}, f32[96,128]{1,0:T(8,128)S(1)}, u32[]{:S(2)}, u32[]{:S(2)}) collective-permute-start(f32[96,128]{1,0:T(8,128)S(1)} %get-tuple-element.126), channel_id=1, source_target_pairs={{0,4},{4,0},{8,12},{12,8},{16,20},{20,16},{24,28},{28,24},{1,5},{5... | collective-permute-start | bytes 147464 | tf_op jit(solution)/shard_map/ppermute | solution.py:55
  51.4 1.6 %collective-permute-start.15 = (f32[96,128]{1,0:T(8,128)S(1)}, f32[96,128]{1,0:T(8,128)S(1)}, u32[]{:S(2)}, u32[]{:S(2)}) collective-permute-start(f32[96,128]{1,0:T(8,128)S(1)} %get-tuple-element.127), channel_id=1, source_target_pairs={{0,8},{4,12},{8,0},{12,4},{16,24},{20,28},{24,16},{28,20},{1,9},{5... | collective-permute-start | bytes 147464 | tf_op jit(solution)/shard_map/ppermute | solution.py:55
  53.5 2.1 %collective-permute-done.15.refs_2_ = f32[96,128]{1,0:T(8,128)S(1)} collective-permute-done((f32[96,128]{1,0:T(8,128)S(1)}, f32[96,128]{1,0:T(8,128)S(1)}, u32[]{:S(2)}, u32[]{:S(2)}) %collective-permute-start.15) | collective-permute-done | bytes 49184 | tf_op jit(solution)/shard_map/ppermute | solution.py:55
  55.6 2.4 %collective-permute-done.16.refs_3_ = f32[96,128]{1,0:T(8,128)S(1)} collective-permute-done((f32[96,128]{1,0:T(8,128)S(1)}, f32[96,128]{1,0:T(8,128)S(1)}, u32[]{:S(2)}, u32[]{:S(2)}) %collective-permute-start.16) | collective-permute-done | bytes 49184 | tf_op jit(solution)/shard_map/ppermute | solution.py:55
  (51 shorter events, 6.9 us)
Async XLA Ops:
  0.0 7.0 %copy-start = (f32[5,384,1536]{2,1,0:T(8,128)S(1)}, f32[5,384,1536]{2,1,0:T(8,128)}, u32[]{:S(2)}) copy-start(f32[5,384,1536]{2,1,0:T(8,128)} %w_ref) | copy-start | bytes 35389444
  6.5 2.0 %collective-permute-start = (f32[296,384]{1,0:T(8,128)S(1)}, f32[296,384]{1,0:T(8,128)S(1)}, u32[]{:S(2)}, u32[]{:S(2)}) collective-permute-start(f32[296,384]{1,0:T(8,128)S(1)} %get-tuple-element.72), channel_id=1, source_target_pairs={{0,1},{1,0},{2,3},{3,2},{4,5},{5,4},{6,7},{7,6},{8,9},{9,8},{10,11... | collective-permute-start | bytes 1363976 | tf_op jit(solution)/shard_map/ppermute | solution.py:55
  8.5 17.6 %collective-permute-start.1 = (f32[296,384]{1,0:T(8,128)S(1)}, f32[296,384]{1,0:T(8,128)S(1)}, u32[]{:S(2)}, u32[]{:S(2)}) collective-permute-start(f32[296,384]{1,0:T(8,128)S(1)} %added.5), channel_id=1, source_target_pairs={{0,2},{1,3},{2,0},{3,1},{4,6},{5,7},{6,4},{7,5},{8,10},{9,11},{10,... | collective-permute-start | bytes 1363976 | tf_op jit(solution)/shard_map/ppermute | solution.py:55
  11.4 5.5 %copy-start.1 = (f32[384,512]{1,0:T(8,128)S(1)}, f32[384,512]{1,0:T(8,128)}, u32[]{:S(2)}) copy-start(f32[384,512]{1,0:T(8,128)} %x_ref) | copy-start | bytes 2359300
  11.4 5.5 %copy-start.2 = (f32[384]{0:T(512)S(1)}, f32[384]{0:T(512)}, u32[]{:S(2)}) copy-start(f32[384]{0:T(512)} %gain_ref.3) | copy-start | bytes 4612
  11.4 5.5 %copy-start.3 = (f32[384]{0:T(512)S(1)}, f32[384]{0:T(512)}, u32[]{:S(2)}) copy-start(f32[384]{0:T(512)} %shift_ref.3) | copy-start | bytes 4612
  11.4 5.5 %collective-permute-start.2 = (f32[8,384]{1,0:T(8,128)S(1)}, f32[8,384]{1,0:T(8,128)S(1)}, u32[]{:S(2)}, u32[]{:S(2)}) collective-permute-start(f32[8,384]{1,0:T(8,128)S(1)} %get-tuple-element.84), channel_id=1, source_target_pairs={{0,4},{4,0},{8,12},{12,8},{16,20},{20,16},{24,28},{28,24},{1,5},{5... | collective-permute-start | bytes 36872 | tf_op jit(solution)/shard_map/ppermute | solution.py:318
  12.9 4.0 %collective-permute-start.3 = (f32[8,384]{1,0:T(8,128)S(1)}, f32[8,384]{1,0:T(8,128)S(1)}, u32[]{:S(2)}, u32[]{:S(2)}) collective-permute-start(f32[8,384]{1,0:T(8,128)S(1)} %get-tuple-element.85), channel_id=1, source_target_pairs={{4,8},{8,4},{12,16},{16,12},{20,24},{24,20},{5,9},{9,5},{13,17},{1... | collective-permute-start | bytes 36872 | tf_op jit(solution)/shard_map/ppermute | solution.py:319
  16.8 9.3 %collective-permute-start.5 = (f32[296,384]{1,0:T(8,128)S(1)}, f32[296,384]{1,0:T(8,128)S(1)}, u32[]{:S(2)}, u32[]{:S(2)}) collective-permute-start(f32[296,384]{1,0:T(8,128)S(1)} %get-tuple-element.98), channel_id=1, source_target_pairs={{0,1},{1,0},{2,3},{3,2},{4,5},{5,4},{6,7},{7,6},{8,9},{9,8},{10,11... | collective-permute-start | bytes 1363976 | tf_op jit(solution)/shard_map/ppermute | solution.py:55
  16.9 3.7 %slice-start = ((s8[11796480]{0:T(1024)(128)(4,1)}), s8[4194304]{0:T(1024)(128)(4,1)S(1)}, s32[]{:S(2)}) async-start(s8[11796480]{0:T(1024)(128)(4,1)} %bitcast), calls=%async_computation | async-start | bytes 8388608
  17.0 3.7 %slice-start.1 = ((s8[11796480]{0:T(1024)(128)(4,1)}), s8[4194304]{0:T(1024)(128)(4,1)S(1)}, s32[]{:S(2)}) async-start(s8[11796480]{0:T(1024)(128)(4,1)} %bitcast), calls=%async_computation.1 | async-start | bytes 8388608
  17.7 3.9 %slice-start.2 = ((s8[11796480]{0:T(1024)(128)(4,1)}), s8[3407872]{0:T(1024)(128)(4,1)S(1)}, s32[]{:S(2)}) async-start(s8[11796480]{0:T(1024)(128)(4,1)} %bitcast), calls=%async_computation.2 | async-start | bytes 6815744
  20.1 2.6 %collective-permute-start.4 = (f32[232,384]{1,0:T(8,128)S(1)}, f32[232,384]{1,0:T(8,128)S(1)}, u32[]{:S(2)}, u32[]{:S(2)}) collective-permute-start(f32[232,384]{1,0:T(8,128)S(1)} %get-tuple-element.89), channel_id=1, source_target_pairs={{0,1},{1,0},{2,3},{3,2},{4,5},{5,4},{6,7},{7,6},{8,9},{9,8},{10,11... | collective-permute-start | bytes 1069064 | tf_op jit(solution)/shard_map/ppermute | solution.py:55
  22.8 11.2 %collective-permute-start.8 = (f32[232,384]{1,0:T(8,128)S(1)}, f32[232,384]{1,0:T(8,128)S(1)}, u32[]{:S(2)}, u32[]{:S(2)}) collective-permute-start(f32[232,384]{1,0:T(8,128)S(1)} %added.6), channel_id=1, source_target_pairs={{0,2},{1,3},{2,0},{3,1},{4,6},{5,7},{6,4},{7,5},{8,10},{9,11},{10,... | collective-permute-start | bytes 1069064 | tf_op jit(solution)/shard_map/ppermute | solution.py:55
  25.8 8.2 %collective-permute-start.9 = (f32[232,384]{1,0:T(8,128)S(1)}, f32[232,384]{1,0:T(8,128)S(1)}, u32[]{:S(2)}, u32[]{:S(2)}) collective-permute-start(f32[232,384]{1,0:T(8,128)S(1)} %get-tuple-element.108), channel_id=1, source_target_pairs={{0,1},{1,0},{2,3},{3,2},{4,5},{5,4},{6,7},{7,6},{8,9},{9,8},{10,11... | collective-permute-start | bytes 1069064 | tf_op jit(solution)/shard_map/ppermute | solution.py:55
  28.3 1.5 %collective-permute-start.6 = (f32[144,384]{1,0:T(8,128)S(1)}, f32[144,384]{1,0:T(8,128)S(1)}, u32[]{:S(2)}, u32[]{:S(2)}) collective-permute-start(f32[144,384]{1,0:T(8,128)S(1)} %get-tuple-element.102), channel_id=1, source_target_pairs={{0,1},{1,0},{2,3},{3,2},{4,5},{5,4},{6,7},{7,6},{8,9},{9,8},{10,11... | collective-permute-start | bytes 663560 | tf_op jit(solution)/shard_map/ppermute | solution.py:55
  29.9 9.4 %collective-permute-start.7 = (f32[144,384]{1,0:T(8,128)S(1)}, f32[144,384]{1,0:T(8,128)S(1)}, u32[]{:S(2)}, u32[]{:S(2)}) collective-permute-start(f32[144,384]{1,0:T(8,128)S(1)} %added.7), channel_id=1, source_target_pairs={{0,2},{1,3},{2,0},{3,1},{4,6},{5,7},{6,4},{7,5},{8,10},{9,11},{10,... | collective-permute-start | bytes 663560 | tf_op jit(solution)/shard_map/ppermute | solution.py:55
  36.3 2.3 %collective-permute-start.11 = (f32[120,384]{1,0:T(8,128)S(1)}, f32[120,384]{1,0:T(8,128)S(1)}, u32[]{:S(2)}, u32[]{:S(2)}) collective-permute-start(f32[120,384]{1,0:T(8,128)S(1)} %get-tuple-element.112), channel_id=1, source_target_pairs={{0,1},{1,0},{2,3},{3,2},{4,5},{5,4},{6,7},{7,6},{8,9},{9,8},{10,11... | collective-permute-start | bytes 552968 | tf_op jit(solution)/shard_map/ppermute | solution.py:55
  38.6 7.1 %collective-permute-start.13 = (f32[120,384]{1,0:T(8,128)S(1)}, f32[120,384]{1,0:T(8,128)S(1)}, u32[]{:S(2)}, u32[]{:S(2)}) collective-permute-start(f32[120,384]{1,0:T(8,128)S(1)} %added.8), channel_id=1, source_target_pairs={{0,2},{1,3},{2,0},{3,1},{4,6},{5,7},{6,4},{7,5},{8,10},{9,11},{10,... | collective-permute-start | bytes 552968 | tf_op jit(solution)/shard_map/ppermute | solution.py:55
  38.8 7.0 %collective-permute-start.10 = (f32[144,384]{1,0:T(8,128)}, f32[144,384]{1,0:T(8,128)}, u32[]{:S(2)}, u32[]{:S(2)}) collective-permute-start(f32[144,384]{1,0:T(8,128)} %get-tuple-element.116), channel_id=1, source_target_pairs={{0,1},{1,0},{2,3},{3,2},{4,5},{5,4},{6,7},{7,6},{8,9},{9,8},{10,11... | collective-permute-start | bytes 663560 | tf_op jit(solution)/shard_map/ppermute | solution.py:55
  41.5 4.3 %collective-permute-start.12 = (f32[120,384]{1,0:T(8,128)}, f32[120,384]{1,0:T(8,128)}, u32[]{:S(2)}, u32[]{:S(2)}) collective-permute-start(f32[120,384]{1,0:T(8,128)} %get-tuple-element.121), channel_id=1, source_target_pairs={{0,1},{1,0},{2,3},{3,2},{4,5},{5,4},{6,7},{7,6},{8,9},{9,8},{10,11... | collective-permute-start | bytes 552968 | tf_op jit(solution)/shard_map/ppermute | solution.py:55
  47.0 6.4 %collective-permute-start.14 = (f32[96,128]{1,0:T(8,128)S(1)}, f32[96,128]{1,0:T(8,128)S(1)}, u32[]{:S(2)}, u32[]{:S(2)}) collective-permute-start(f32[96,128]{1,0:T(8,128)S(1)} %get-tuple-element.126), channel_id=1, source_target_pairs={{0,4},{4,0},{8,12},{12,8},{16,20},{20,16},{24,28},{28,24},{1,5},{5... | collective-permute-start | bytes 147464 | tf_op jit(solution)/shard_map/ppermute | solution.py:55
  51.4 4.2 %collective-permute-start.15 = (f32[96,128]{1,0:T(8,128)S(1)}, f32[96,128]{1,0:T(8,128)S(1)}, u32[]{:S(2)}, u32[]{:S(2)}) collective-permute-start(f32[96,128]{1,0:T(8,128)S(1)} %get-tuple-element.127), channel_id=1, source_target_pairs={{0,8},{4,12},{8,0},{12,4},{16,24},{20,28},{24,16},{28,20},{1,9},{5... | collective-permute-start | bytes 147464 | tf_op jit(solution)/shard_map/ppermute | solution.py:55
  53.0 5.0 %collective-permute-start.16 = (f32[96,128]{1,0:T(8,128)S(1)}, f32[96,128]{1,0:T(8,128)S(1)}, u32[]{:S(2)}, u32[]{:S(2)}) collective-permute-start(f32[96,128]{1,0:T(8,128)S(1)} %get-tuple-element.128), channel_id=1, source_target_pairs={{0,12},{4,8},{8,4},{12,0},{16,28},{20,24},{24,20},{28,16},{1,13},{... | collective-permute-start | bytes 147464 | tf_op jit(solution)/shard_map/ppermute | solution.py:55
  (2 other events, 6.7 us)

commit v4 on v3

--- a/solution.py
+++ b/solution.py
@@ -18,7 +18,7 @@
 LIGHT = 1_000_000_000
 MIDDLE = 10 * LIGHT
 EARLY = 30 * LIGHT
-HEAVY = 300 * LIGHT
+HEAVY = 30 * LIGHT
 
 
 def f32(*shape):
@@ -267,9 +267,9 @@
 
 
 def pieces_kernel(*refs):
-    ins, outs, (c_ref, d_ref, all_ref) = refs[:5], refs[5:-3], refs[-3:]
-    put_sum(c_ref, *ins[:3])
-    put_sum(d_ref, *ins[3:])
+    ins, outs, (c_ref, d_ref, all_ref) = refs[:4], refs[4:-3], refs[-3:]
+    put_sum(c_ref, *ins[:2])
+    put_sum(d_ref, *ins[2:])
     pooled_d = pool_rows(d_ref)
     rows_c = ins[0].shape[0] // 2
     main = all_ref.shape[0] - 2 - rows_c
@@ -358,11 +358,12 @@
     sum_d = swapped(half_d, "ch", 2)
     own_there_d, own_here_d = conv(after(stack_d, half_d, sum_c), own_two, rows_d)
     here_d = call(add_kernel, "added", [sum_d, own_here_d], [f32(*sum_d.shape)], flops=HEAVY)[0]
-    last_c, last_d = after((swapped(own_there_c, "ch", 1), swapped(own_there_d, "ch", 1)), here_d)
+    own_c = added(own_here_c, swapped(own_there_c, "ch", 1))
+    last_d = after(swapped(own_there_d, "ch", 1), here_d)
 
     quarter = length // 4
     pieces = call(
-        pieces_kernel, "pieces", [sum_c, own_here_c, last_c, here_d, last_d],
+        pieces_kernel, "pieces", [sum_c, own_c, here_d, last_d],
         [f32(channels // GROUP, quarter)] * GROUP,
         [(channels // LANES, rows_c, LANES), (channels // LANES, rows_d, LANES), (quarter, channels)],
     )

time: 58.8 us -> 57.2 us (0.973)
  Pallas kernels: 29.5 us -> 27.2 us
    pallas_call x21 -> x22, Pallas kernels: 26.1 us -> 23.9 us  [call(): pl.pallas_call(kernel, in_specs=[VECTORS] * len(args), out_specs=[VECTORS...]
  transfers between devices with their start and end apart: 17 -> 17, of which waited for: 6 -> 6; matrix products, arithmetic and copies ran while one was open for 0% -> 0% of each run, Pallas kernels for 36% -> 35%
where the time goes in v4:
time: 57.2 us; the launch traced here: 57.1 us
  Pallas kernels  27.2 us (48%)
  starting transfers between devices  16 us (28%)
  waiting for transfers between devices  12.6 us (22%)
  local copies, waits for them, and re-layouts  0.92 us (2%)
    pallas_call x22, Pallas kernels, call(): pl.pallas_call(kernel, in_specs=[VECTORS] * len(args), out_specs=[VECTORS...  23.9 us
    ppermute x15, starting transfers between devices, swapped(): return lax.ppermute(block, axis, [(i, i ^ bit) for i in range(count)])  13.7 us
    ppermute x15, waiting for transfers between devices, swapped(): return lax.ppermute(block, axis, [(i, i ^ bit) for i in range(count)])  12.6 us
    pallas_call x1, Pallas kernels, opening(): pl.pallas_call(opening_kernel, in_specs=[IN_HBM] * 4, out_specs=[VECTORS]...  3.39 us
    ppermute x1, starting transfers between devices, body(): inner = lax.ppermute(to_inner, 'seq', [(i, i ^ 1) for i in range(n_seq)])  1.49 us
  transfers between devices with their start and end apart: 17, of which 6 were waited for; matrix products, arithmetic and copies ran while one was open for 0% of the time, Pallas kernels for 35%

profile of v4, /device:TPU:0, one launch (start us, length us, event | category | flops | bytes accessed | tf_op | source)
XLA Modules:
  0.0 57.1 jit_solution(7815399821058200372)
XLA Ops:
  0.0 3.4 %opening.1 = (bf16[304,1920]{1,0:T(8,128)(2,1)S(1)}, bf16[304,1920]{1,0:T(8,128)(2,1)S(1)}, f32[8,384]{1,0:T(8,128)S(1)}, f32[8,384]{1,0:T(8,128)S(1)}, f32[8,38...) custom-call(f32[384]{0:T(512)} %gain_ref.3, f32[384]{0:T(512)} %shift_ref.3, ...), custom_call_target="tpu_custom_call" | custom-call | flops 1000000000 | tf_op jit(solution)/shard_map/opening/pallas_call | solution.py:135
  3.4 3.0 %conv.8 = (f32[296,384]{1,0:T(8,128)S(1)}, f32[296,384]{1,0:T(8,128)S(1)}) custom-call(bf16[304,1920]{1,0:T(8,128)(2,1)S(1)} %get-tuple-element.76.hi_ref, bf16[304,1920]{1,0:T(8,128)(2,1)S(1)} %get-tuple-element.77.lo_ref, bf16[1920,768]{1,0:T(8,128)(2,1)S(1)} %get-tuple-element.68.whi_ref, bf16[1920,768]{1,0:T(8,128)(2,1)S(1)} %get-tuple-element.69.wlo_ref), custom_call_target="tpu_custom_call" | custom-call | flops 1000000000 | tf_op jit(solution)/shard_map/conv/pallas_call | solution.py:41
  7.0 1.1 %split_own.2 = (bf16[1920,768]{1,0:T(8,128)(2,1)S(1)}, bf16[1920,768]{1,0:T(8,128)(2,1)S(1)}) custom-call(f32[5,384,1536]{2,1,0:T(8,128)S(1)} %copy-done), custom_call_target="tpu_custom_call" | custom-call | flops 1000000000 | tf_op jit(solution)/shard_map/split_own/pallas_call | solution.py:41
  8.5 3.0 %collective-permute-start.1 = (f32[296,384]{1,0:T(8,128)S(1)}, f32[296,384]{1,0:T(8,128)S(1)}, u32[]{:S(2)}, u32[]{:S(2)}) collective-permute-start(f32[296,384]{1,0:T(8,128)S(1)} %added.6), channel_id=1, source_target_pairs={{0,2},{1,3},{2,0},{3,1},{4,6},{5,7},{6,4},{7,5},{8,10},{9,11},{10,... | collective-permute-start | bytes 1363976 | tf_op jit(solution)/shard_map/ppermute | solution.py:55
  11.4 1.5 %collective-permute-start.2 = (f32[8,384]{1,0:T(8,128)S(1)}, f32[8,384]{1,0:T(8,128)S(1)}, u32[]{:S(2)}, u32[]{:S(2)}) collective-permute-start(f32[8,384]{1,0:T(8,128)S(1)} %get-tuple-element.83), channel_id=1, source_target_pairs={{0,4},{4,0},{8,12},{12,8},{16,20},{20,16},{24,28},{28,24},{1,5},{5... | collective-permute-start | bytes 36872 | tf_op jit(solution)/shard_map/ppermute | solution.py:318
  12.9 0.8 %collective-permute-start.3 = (f32[8,384]{1,0:T(8,128)S(1)}, f32[8,384]{1,0:T(8,128)S(1)}, u32[]{:S(2)}, u32[]{:S(2)}) collective-permute-start(f32[8,384]{1,0:T(8,128)S(1)} %get-tuple-element.84), channel_id=1, source_target_pairs={{4,8},{8,4},{12,16},{16,12},{20,24},{24,20},{5,9},{9,5},{13,17},{1... | collective-permute-start | bytes 36872 | tf_op jit(solution)/shard_map/ppermute | solution.py:319
  13.8 3.0 %conv.9 = (f32[296,384]{1,0:T(8,128)S(1)}, f32[296,384]{1,0:T(8,128)S(1)}) custom-call(bf16[304,1920]{1,0:T(8,128)(2,1)S(1)} %get-tuple-element.76.hi_ref, bf16[304,1920]{1,0:T(8,128)(2,1)S(1)} %get-tuple-element.77.lo_ref, bf16[1920,768]{1,0:T(8,128)(2,1)S(1)} %get-tuple-element.73.whi_ref, bf16[1920,768]{1,0:T(8,128)(2,1)S(1)} %get-tuple-element.74.wlo_ref), custom_call_target="tpu_custom_call" | custom-call | flops 30000001024 | tf_op jit(solution)/shard_map/conv/pallas_call | solution.py:41
  17.7 2.5 %conv.10 = (f32[232,384]{1,0:T(8,128)S(1)}, f32[232,384]{1,0:T(8,128)S(1)}) custom-call(bf16[240,1920]{1,0:T(8,128)(2,1)S(1)} %get-tuple-element.93.hi_ref, bf16[240,1920]{1,0:T(8,128)(2,1)S(1)} %get-tuple-element.94.lo_ref, bf16[1920,768]{1,0:T(8,128)(2,1)S(1)} %get-tuple-element.68.whi_ref, bf16[1920,768]{1,0:T(8,128)(2,1)S(1)} %get-tuple-element.69.wlo_ref), custom_call_target="tpu_custom_call" | custom-call | flops 30000001024 | tf_op jit(solution)/shard_map/conv/pallas_call | solution.py:41
  20.7 0.9 %slice-done.2 = s8[3407872]{0:T(1024)(128)(4,1)S(1)} async-done(((s8[11796480]{0:T(1024)(128)(4,1)}), s8[3407872]{0:T(1024)(128)(4,1)S(1)}, s32[]{:S(2)}) %slice-start.2) | async-done | bytes 3407896
  21.6 1.1 %split_far.1 = (bf16[1920,768]{1,0:T(8,128)(2,1)S(1)}, bf16[1920,768]{1,0:T(8,128)(2,1)S(1)}) custom-call(f32[5,384,1536]{2,1,0:T(8,128)S(1)} %bitcast.1), custom_call_target="tpu_custom_call" | custom-call | flops 30000001024 | tf_op jit(solution)/shard_map/split_far/pallas_call | solution.py:41
  23.4 2.5 %conv.11 = (f32[232,384]{1,0:T(8,128)S(1)}, f32[232,384]{1,0:T(8,128)S(1)}) custom-call(bf16[240,1920]{1,0:T(8,128)(2,1)S(1)} %get-tuple-element.93.hi_ref, bf16[240,1920]{1,0:T(8,128)(2,1)S(1)} %get-tuple-element.94.lo_ref, bf16[1920,768]{1,0:T(8,128)(2,1)S(1)} %get-tuple-element.73.whi_ref, bf16[1920,768]{1,0:T(8,128)(2,1)S(1)} %get-tuple-element.74.wlo_ref), custom_call_target="tpu_custom_call" | custom-call | flops 1000000000 | tf_op jit(solution)/shard_map/conv/pallas_call | solution.py:41
  26.7 1.6 %conv.12 = (f32[144,384]{1,0:T(8,128)S(1)}, f32[144,384]{1,0:T(8,128)S(1)}) custom-call(bf16[144,1920]{1,0:T(8,128)(2,1)S(1)} %get-tuple-element.112.hi_ref, bf16[144,1920]{1,0:T(8,128)(2,1)S(1)} %get-tuple-element.113.lo_ref, bf16[1920,768]{1,0:T(8,128)(2,1)S(1)} %get-tuple-element.90.whi_ref, bf16[1920,768]{1,0:T(8,128)(2,1)S(1)} %get-tuple-element.91.wlo_ref), custom_call_target="tpu_custom_call" | custom-call | flops 1000000000 | tf_op jit(solution)/shard_map/conv/pallas_call | solution.py:41
  28.7 1.1 %split_own.3 = (bf16[1920,768]{1,0:T(8,128)(2,1)S(1)}, bf16[1920,768]{1,0:T(8,128)(2,1)S(1)}) custom-call(f32[5,384,1536]{2,1,0:T(8,128)S(1)} %bitcast.1), custom_call_target="tpu_custom_call" | custom-call | flops 1000000000 | tf_op jit(solution)/shard_map/split_own/pallas_call | solution.py:41
  29.9 1.6 %collective-permute-start.7 = (f32[144,384]{1,0:T(8,128)S(1)}, f32[144,384]{1,0:T(8,128)S(1)}, u32[]{:S(2)}, u32[]{:S(2)}) collective-permute-start(f32[144,384]{1,0:T(8,128)S(1)} %added.8), channel_id=1, source_target_pairs={{0,2},{1,3},{2,0},{3,1},{4,6},{5,7},{6,4},{7,5},{8,10},{9,11},{10,... | collective-permute-start | bytes 663560 | tf_op jit(solution)/shard_map/ppermute | solution.py:55
  31.5 2.5 %collective-permute-done.8.a_ref = f32[232,384]{1,0:T(8,128)S(1)} collective-permute-done((f32[232,384]{1,0:T(8,128)S(1)}, f32[232,384]{1,0:T(8,128)S(1)}, u32[]{:S(2)}, u32[]{:S(2)}) %collective-permute-start.8) | collective-permute-done | bytes 356384 | tf_op jit(solution)/shard_map/ppermute | solution.py:55
  34.0 0.7 %second_d.1 = (bf16[128,1920]{1,0:T(8,128)(2,1)S(1)}, bf16[128,1920]{1,0:T(8,128)(2,1)S(1)}) custom-call(f32[232,384]{1,0:T(8,128)S(1)} %collective-permute-done.8.a_ref, f32[232,384]{1,0:T(8,128)S(1)} %get-tuple-element.95.b_ref, f32[232,384]{1,0:T(8,128)S(1)} %collective-permute-done.9.c_ref, f32[384]{0:T(512)S(1)} %copy-done.4, f32[384]{0:T(512)S(1)} %copy-done.5, ...), custom_call_target="tpu_custom_call" | custom-call | flops 10000000000 | tf_op jit(solution)/shard_map/second_d/pallas_call | solution.py:41
  34.7 1.5 %conv.13 = (f32[120,384]{1,0:T(8,128)S(1)}, f32[120,384]{1,0:T(8,128)S(1)}) custom-call(bf16[128,1920]{1,0:T(8,128)(2,1)S(1)} %get-tuple-element.118.hi_ref, bf16[128,1920]{1,0:T(8,128)(2,1)S(1)} %get-tuple-element.119.lo_ref, bf16[1920,768]{1,0:T(8,128)(2,1)S(1)} %get-tuple-element.90.whi_ref, bf16[1920,768]{1,0:T(8,128)(2,1)S(1)} %get-tuple-element.91.wlo_ref), custom_call_target="tpu_custom_call" | custom-call | flops 10000000000 | tf_op jit(solution)/shard_map/conv/pallas_call | solution.py:41
  36.3 1.6 %conv.14 = (f32[144,384]{1,0:T(8,128)S(1)}, f32[144,384]{1,0:T(8,128)S(1)}) custom-call(bf16[144,1920]{1,0:T(8,128)(2,1)S(1)} %get-tuple-element.112.hi_ref, bf16[144,1920]{1,0:T(8,128)(2,1)S(1)} %get-tuple-element.113.lo_ref, bf16[1920,768]{1,0:T(8,128)(2,1)S(1)} %get-tuple-element.103.whi_ref, bf16[1920,768]{1,0:T(8,128)(2,1)S(1)} %get-tuple-element.104.wlo_ref), custom_call_target="tpu_custom_call" | custom-call | flops 10000000000 | tf_op jit(solution)/shard_map/conv/pallas_call | solution.py:41
  38.7 1.5 %conv.15 = (f32[120,384]{1,0:T(8,128)S(1)}, f32[120,384]{1,0:T(8,128)S(1)}) custom-call(bf16[128,1920]{1,0:T(8,128)(2,1)S(1)} %get-tuple-element.118.hi_ref, bf16[128,1920]{1,0:T(8,128)(2,1)S(1)} %get-tuple-element.119.lo_ref, bf16[1920,768]{1,0:T(8,128)(2,1)S(1)} %get-tuple-element.103.whi_ref, bf16[1920,768]{1,0:T(8,128)(2,1)S(1)} %get-tuple-element.104.wlo_ref), custom_call_target="tpu_custom_call" | custom-call | flops 1000000000 | tf_op jit(solution)/shard_map/conv/pallas_call | solution.py:41
  40.4 4.8 %collective-permute-done.12.a_ref = f32[120,384]{1,0:T(8,128)S(1)} collective-permute-done((f32[120,384]{1,0:T(8,128)S(1)}, f32[120,384]{1,0:T(8,128)S(1)}, u32[]{:S(2)}, u32[]{:S(2)}) %collective-permute-start.12) | collective-permute-done | bytes 184352 | tf_op jit(solution)/shard_map/ppermute | solution.py:55
  45.5 4.4 %collective-permute-start.14 = (f32[96,128]{1,0:T(8,128)S(1)}, f32[96,128]{1,0:T(8,128)S(1)}, u32[]{:S(2)}, u32[]{:S(2)}) collective-permute-start(f32[96,128]{1,0:T(8,128)S(1)} %get-tuple-element.124), channel_id=1, source_target_pairs={{0,4},{4,0},{8,12},{12,8},{16,20},{20,16},{24,28},{28,24},{1,5},{5... | collective-permute-start | bytes 147464 | tf_op jit(solution)/shard_map/ppermute | solution.py:55
  49.8 1.6 %collective-permute-start.15 = (f32[96,128]{1,0:T(8,128)S(1)}, f32[96,128]{1,0:T(8,128)S(1)}, u32[]{:S(2)}, u32[]{:S(2)}) collective-permute-start(f32[96,128]{1,0:T(8,128)S(1)} %get-tuple-element.125), channel_id=1, source_target_pairs={{0,8},{4,12},{8,0},{12,4},{16,24},{20,28},{24,16},{28,20},{1,9},{5... | collective-permute-start | bytes 147464 | tf_op jit(solution)/shard_map/ppermute | solution.py:55
  51.9 2.0 %collective-permute-done.15.refs_2_ = f32[96,128]{1,0:T(8,128)S(1)} collective-permute-done((f32[96,128]{1,0:T(8,128)S(1)}, f32[96,128]{1,0:T(8,128)S(1)}, u32[]{:S(2)}, u32[]{:S(2)}) %collective-permute-start.15) | collective-permute-done | bytes 49184 | tf_op jit(solution)/shard_map/ppermute | solution.py:55
  53.9 2.5 %collective-permute-done.16.refs_3_ = f32[96,128]{1,0:T(8,128)S(1)} collective-permute-done((f32[96,128]{1,0:T(8,128)S(1)}, f32[96,128]{1,0:T(8,128)S(1)}, u32[]{:S(2)}, u32[]{:S(2)}) %collective-permute-start.16) | collective-permute-done | bytes 49184 | tf_op jit(solution)/shard_map/ppermute | solution.py:55
  (52 shorter events, 6.5 us)
Async XLA Ops:
  0.0 7.0 %copy-start = (f32[5,384,1536]{2,1,0:T(8,128)S(1)}, f32[5,384,1536]{2,1,0:T(8,128)}, u32[]{:S(2)}) copy-start(f32[5,384,1536]{2,1,0:T(8,128)} %w_ref) | copy-start | bytes 35389444
  6.5 2.0 %collective-permute-start = (f32[296,384]{1,0:T(8,128)S(1)}, f32[296,384]{1,0:T(8,128)S(1)}, u32[]{:S(2)}, u32[]{:S(2)}) collective-permute-start(f32[296,384]{1,0:T(8,128)S(1)} %get-tuple-element.71), channel_id=1, source_target_pairs={{0,1},{1,0},{2,3},{3,2},{4,5},{5,4},{6,7},{7,6},{8,9},{9,8},{10,11... | collective-permute-start | bytes 1363976 | tf_op jit(solution)/shard_map/ppermute | solution.py:55
  8.5 17.6 %collective-permute-start.1 = (f32[296,384]{1,0:T(8,128)S(1)}, f32[296,384]{1,0:T(8,128)S(1)}, u32[]{:S(2)}, u32[]{:S(2)}) collective-permute-start(f32[296,384]{1,0:T(8,128)S(1)} %added.6), channel_id=1, source_target_pairs={{0,2},{1,3},{2,0},{3,1},{4,6},{5,7},{6,4},{7,5},{8,10},{9,11},{10,... | collective-permute-start | bytes 1363976 | tf_op jit(solution)/shard_map/ppermute | solution.py:55
  11.4 5.5 %copy-start.1 = (f32[384,512]{1,0:T(8,128)S(1)}, f32[384,512]{1,0:T(8,128)}, u32[]{:S(2)}) copy-start(f32[384,512]{1,0:T(8,128)} %x_ref) | copy-start | bytes 2359300
  11.4 5.5 %copy-start.2 = (f32[384]{0:T(512)S(1)}, f32[384]{0:T(512)}, u32[]{:S(2)}) copy-start(f32[384]{0:T(512)} %gain_ref.3) | copy-start | bytes 4612
  11.4 5.5 %copy-start.3 = (f32[384]{0:T(512)S(1)}, f32[384]{0:T(512)}, u32[]{:S(2)}) copy-start(f32[384]{0:T(512)} %shift_ref.3) | copy-start | bytes 4612
  11.4 5.5 %collective-permute-start.2 = (f32[8,384]{1,0:T(8,128)S(1)}, f32[8,384]{1,0:T(8,128)S(1)}, u32[]{:S(2)}, u32[]{:S(2)}) collective-permute-start(f32[8,384]{1,0:T(8,128)S(1)} %get-tuple-element.83), channel_id=1, source_target_pairs={{0,4},{4,0},{8,12},{12,8},{16,20},{20,16},{24,28},{28,24},{1,5},{5... | collective-permute-start | bytes 36872 | tf_op jit(solution)/shard_map/ppermute | solution.py:318
  12.9 4.0 %collective-permute-start.3 = (f32[8,384]{1,0:T(8,128)S(1)}, f32[8,384]{1,0:T(8,128)S(1)}, u32[]{:S(2)}, u32[]{:S(2)}) collective-permute-start(f32[8,384]{1,0:T(8,128)S(1)} %get-tuple-element.84), channel_id=1, source_target_pairs={{4,8},{8,4},{12,16},{16,12},{20,24},{24,20},{5,9},{9,5},{13,17},{1... | collective-permute-start | bytes 36872 | tf_op jit(solution)/shard_map/ppermute | solution.py:319
  16.8 9.3 %collective-permute-start.5 = (f32[296,384]{1,0:T(8,128)S(1)}, f32[296,384]{1,0:T(8,128)S(1)}, u32[]{:S(2)}, u32[]{:S(2)}) collective-permute-start(f32[296,384]{1,0:T(8,128)S(1)} %get-tuple-element.97), channel_id=1, source_target_pairs={{0,1},{1,0},{2,3},{3,2},{4,5},{5,4},{6,7},{7,6},{8,9},{9,8},{10,11... | collective-permute-start | bytes 1363976 | tf_op jit(solution)/shard_map/ppermute | solution.py:55
  16.9 3.7 %slice-start = ((s8[11796480]{0:T(1024)(128)(4,1)}), s8[4194304]{0:T(1024)(128)(4,1)S(1)}, s32[]{:S(2)}) async-start(s8[11796480]{0:T(1024)(128)(4,1)} %bitcast), calls=%async_computation | async-start | bytes 8388608
  17.0 3.7 %slice-start.1 = ((s8[11796480]{0:T(1024)(128)(4,1)}), s8[4194304]{0:T(1024)(128)(4,1)S(1)}, s32[]{:S(2)}) async-start(s8[11796480]{0:T(1024)(128)(4,1)} %bitcast), calls=%async_computation.1 | async-start | bytes 8388608
  17.7 3.9 %slice-start.2 = ((s8[11796480]{0:T(1024)(128)(4,1)}), s8[3407872]{0:T(1024)(128)(4,1)S(1)}, s32[]{:S(2)}) async-start(s8[11796480]{0:T(1024)(128)(4,1)} %bitcast), calls=%async_computation.2 | async-start | bytes 6815744
  20.1 2.6 %collective-permute-start.4 = (f32[232,384]{1,0:T(8,128)S(1)}, f32[232,384]{1,0:T(8,128)S(1)}, u32[]{:S(2)}, u32[]{:S(2)}) collective-permute-start(f32[232,384]{1,0:T(8,128)S(1)} %get-tuple-element.88), channel_id=1, source_target_pairs={{0,1},{1,0},{2,3},{3,2},{4,5},{5,4},{6,7},{7,6},{8,9},{9,8},{10,11... | collective-permute-start | bytes 1069064 | tf_op jit(solution)/shard_map/ppermute | solution.py:55
  22.8 11.2 %collective-permute-start.8 = (f32[232,384]{1,0:T(8,128)S(1)}, f32[232,384]{1,0:T(8,128)S(1)}, u32[]{:S(2)}, u32[]{:S(2)}) collective-permute-start(f32[232,384]{1,0:T(8,128)S(1)} %added.7), channel_id=1, source_target_pairs={{0,2},{1,3},{2,0},{3,1},{4,6},{5,7},{6,4},{7,5},{8,10},{9,11},{10,... | collective-permute-start | bytes 1069064 | tf_op jit(solution)/shard_map/ppermute | solution.py:55
  25.8 8.2 %collective-permute-start.9 = (f32[232,384]{1,0:T(8,128)S(1)}, f32[232,384]{1,0:T(8,128)S(1)}, u32[]{:S(2)}, u32[]{:S(2)}) collective-permute-start(f32[232,384]{1,0:T(8,128)S(1)} %get-tuple-element.107), channel_id=1, source_target_pairs={{0,1},{1,0},{2,3},{3,2},{4,5},{5,4},{6,7},{7,6},{8,9},{9,8},{10,11... | collective-permute-start | bytes 1069064 | tf_op jit(solution)/shard_map/ppermute | solution.py:55
  28.3 1.5 %collective-permute-start.6 = (f32[144,384]{1,0:T(8,128)S(1)}, f32[144,384]{1,0:T(8,128)S(1)}, u32[]{:S(2)}, u32[]{:S(2)}) collective-permute-start(f32[144,384]{1,0:T(8,128)S(1)} %get-tuple-element.101), channel_id=1, source_target_pairs={{0,1},{1,0},{2,3},{3,2},{4,5},{5,4},{6,7},{7,6},{8,9},{9,8},{10,11... | collective-permute-start | bytes 663560 | tf_op jit(solution)/shard_map/ppermute | solution.py:55
  29.9 8.8 %collective-permute-start.7 = (f32[144,384]{1,0:T(8,128)S(1)}, f32[144,384]{1,0:T(8,128)S(1)}, u32[]{:S(2)}, u32[]{:S(2)}) collective-permute-start(f32[144,384]{1,0:T(8,128)S(1)} %added.8), channel_id=1, source_target_pairs={{0,2},{1,3},{2,0},{3,1},{4,6},{5,7},{6,4},{7,5},{8,10},{9,11},{10,... | collective-permute-start | bytes 663560 | tf_op jit(solution)/shard_map/ppermute | solution.py:55
  36.3 2.3 %collective-permute-start.11 = (f32[120,384]{1,0:T(8,128)S(1)}, f32[120,384]{1,0:T(8,128)S(1)}, u32[]{:S(2)}, u32[]{:S(2)}) collective-permute-start(f32[120,384]{1,0:T(8,128)S(1)} %get-tuple-element.111), channel_id=1, source_target_pairs={{0,1},{1,0},{2,3},{3,2},{4,5},{5,4},{6,7},{7,6},{8,9},{9,8},{10,11... | collective-permute-start | bytes 552968 | tf_op jit(solution)/shard_map/ppermute | solution.py:55
  38.0 2.4 %collective-permute-start.10 = (f32[144,384]{1,0:T(8,128)S(1)}, f32[144,384]{1,0:T(8,128)S(1)}, u32[]{:S(2)}, u32[]{:S(2)}) collective-permute-start(f32[144,384]{1,0:T(8,128)S(1)} %get-tuple-element.115), channel_id=1, source_target_pairs={{0,1},{1,0},{2,3},{3,2},{4,5},{5,4},{6,7},{7,6},{8,9},{9,8},{10,11... | collective-permute-start | bytes 663560 | tf_op jit(solution)/shard_map/ppermute | solution.py:55
  38.6 6.6 %collective-permute-start.12 = (f32[120,384]{1,0:T(8,128)S(1)}, f32[120,384]{1,0:T(8,128)S(1)}, u32[]{:S(2)}, u32[]{:S(2)}) collective-permute-start(f32[120,384]{1,0:T(8,128)S(1)} %added.10), channel_id=1, source_target_pairs={{0,2},{1,3},{2,0},{3,1},{4,6},{5,7},{6,4},{7,5},{8,10},{9,11},{10,... | collective-permute-start | bytes 552968 | tf_op jit(solution)/shard_map/ppermute | solution.py:55
  40.3 5.0 %collective-permute-start.13 = (f32[120,384]{1,0:T(8,128)S(1)}, f32[120,384]{1,0:T(8,128)S(1)}, u32[]{:S(2)}, u32[]{:S(2)}) collective-permute-start(f32[120,384]{1,0:T(8,128)S(1)} %get-tuple-element.121), channel_id=1, source_target_pairs={{0,1},{1,0},{2,3},{3,2},{4,5},{5,4},{6,7},{7,6},{8,9},{9,8},{10,11... | collective-permute-start | bytes 552968 | tf_op jit(solution)/shard_map/ppermute | solution.py:55
  45.5 6.4 %collective-permute-start.14 = (f32[96,128]{1,0:T(8,128)S(1)}, f32[96,128]{1,0:T(8,128)S(1)}, u32[]{:S(2)}, u32[]{:S(2)}) collective-permute-start(f32[96,128]{1,0:T(8,128)S(1)} %get-tuple-element.124), channel_id=1, source_target_pairs={{0,4},{4,0},{8,12},{12,8},{16,20},{20,16},{24,28},{28,24},{1,5},{5... | collective-permute-start | bytes 147464 | tf_op jit(solution)/shard_map/ppermute | solution.py:55
  49.8 4.1 %collective-permute-start.15 = (f32[96,128]{1,0:T(8,128)S(1)}, f32[96,128]{1,0:T(8,128)S(1)}, u32[]{:S(2)}, u32[]{:S(2)}) collective-permute-start(f32[96,128]{1,0:T(8,128)S(1)} %get-tuple-element.125), channel_id=1, source_target_pairs={{0,8},{4,12},{8,0},{12,4},{16,24},{20,28},{24,16},{28,20},{1,9},{5... | collective-permute-start | bytes 147464 | tf_op jit(solution)/shard_map/ppermute | solution.py:55
  51.4 5.0 %collective-permute-start.16 = (f32[96,128]{1,0:T(8,128)S(1)}, f32[96,128]{1,0:T(8,128)S(1)}, u32[]{:S(2)}, u32[]{:S(2)}) collective-permute-start(f32[96,128]{1,0:T(8,128)S(1)} %get-tuple-element.126), channel_id=1, source_target_pairs={{0,12},{4,8},{8,4},{12,0},{16,28},{20,24},{24,20},{28,16},{1,13},{... | collective-permute-start | bytes 147464 | tf_op jit(solution)/shard_map/ppermute | solution.py:55
  (2 other events, 6.7 us)

commit v5 on v4

--- a/solution.py
+++ b/solution.py
@@ -319,24 +319,23 @@
     outer = lax.ppermute(
         to_outer, "seq", [p for i in range(1, n_seq - 1, 2) for p in ((i, i + 1), (i + 1, i))]
     )
-    own_there_a, own_here_a = conv(after((hi_a, lo_a), half_a), own_one, rows_a, EARLY)
-    own_a = own_here_a, swapped(own_there_a, "ch", 1)
     stack_b = call(
         functools.partial(first_b_kernel, chunk=CHUNK), "first_b",
-        [after(features, own_here_a), *one, head, inner, outer],
+        [after(features, half_a), *one, head, inner, outer],
         [bf16(padded(rows_b), depth)] * 2, [(length - (CHUNK + 2) // LANES * LANES + 48, channels)], EARLY,
     )
     there_b, here_b = conv(stack_b, far_one, rows_b, EARLY)
-    half_b = added(here_b, swapped(there_b, "ch", 1))
-    far_two = split_weight(after(wide_two, there_b), outs, True, EARLY)
-    half_b = after(half_b, far_two)
+    own_there_a, own_here_a = conv(after((hi_a, lo_a), there_b), own_one, rows_a, EARLY)
+    own_a = own_here_a, swapped(own_there_a, "ch", 1)
+    half_b = after(added(here_b, swapped(there_b, "ch", 1)), own_here_a)
     sum_b = swapped(half_b, "ch", 2)
 
     own_there_b, own_here_b = conv(after(stack_b, half_b), own_one, rows_b)
     own_b = own_here_b, swapped(own_there_b, "ch", 1)
+    far_two = split_weight(after(wide_two, own_here_b), outs, True)
 
     *stack_c, ends = call(
-        second_c_kernel, "second_c", [after(sum_a, own_here_b), *own_a, *two],
+        second_c_kernel, "second_c", [after(sum_a, far_two), *own_a, *two],
         [bf16(padded(rows_c), depth)] * 2 + [f32(8, channels)],
         [(channels // LANES, rows_a, LANES), (padded(rows_c) + 8, channels)],
     )

time: 57.2 us -> 55 us (0.962)
  waiting for transfers between devices: 12.6 us -> 9.44 us
  starting transfers between devices: 16 us -> 18 us
  local copies, waits for them, and re-layouts: 0.92 us -> 0.06 us
    ppermute x15, waiting for transfers between devices: 12.6 us -> 9.44 us  [swapped(): return lax.ppermute(block, axis, [(i, i ^ bit) for i in range(count)])]
    ppermute x1, starting transfers between devices: 1.49 us -> 2.92 us  [body(): inner = lax.ppermute(to_inner, 'seq', [(i, i ^ 1) for i in range(n_seq)])]
    unnamed x18, local copies, waits for them, and re-layouts: 0.92 us -> 0.06 us
  transfers between devices with their start and end apart: 17 -> 17, of which waited for: 6 -> 5; matrix products, arithmetic and copies ran while one was open for 0% -> 0% of each run, Pallas kernels for 35% -> 36%
where the time goes in v5:
time: 55 us; the launch traced here: 54.9 us
  Pallas kernels  27.1 us (49%)
  starting transfers between devices  18 us (33%)
  waiting for transfers between devices  9.44 us (17%)
    pallas_call x22, Pallas kernels, call(): pl.pallas_call(kernel, in_specs=[VECTORS] * len(args), out_specs=[VECTORS...  23.7 us
    ppermute x15, starting transfers between devices, swapped(): return lax.ppermute(block, axis, [(i, i ^ bit) for i in range(count)])  14.2 us
    ppermute x15, waiting for transfers between devices, swapped(): return lax.ppermute(block, axis, [(i, i ^ bit) for i in range(count)])  9.44 us
    pallas_call x1, Pallas kernels, opening(): pl.pallas_call(opening_kernel, in_specs=[IN_HBM] * 4, out_specs=[VECTORS]...  3.39 us
    ppermute x1, starting transfers between devices, body(): inner = lax.ppermute(to_inner, 'seq', [(i, i ^ 1) for i in range(n_seq)])  2.92 us
  transfers between devices with their start and end apart: 17, of which 5 were waited for; matrix products, arithmetic and copies ran while one was open for 0% of the time, Pallas kernels for 36%

profile of v5, /device:TPU:0, one launch (start us, length us, event | category | flops | bytes accessed | tf_op | source)
XLA Modules:
  0.0 54.9 jit_solution(2167116118699393494)
XLA Ops:
  0.0 3.4 %opening.1 = (bf16[304,1920]{1,0:T(8,128)(2,1)S(1)}, bf16[304,1920]{1,0:T(8,128)(2,1)S(1)}, f32[8,384]{1,0:T(8,128)S(1)}, f32[8,384]{1,0:T(8,128)S(1)}, f32[8,38...) custom-call(f32[384]{0:T(512)} %gain_ref.3, f32[384]{0:T(512)} %shift_ref.3, ...), custom_call_target="tpu_custom_call" | custom-call | flops 1000000000 | tf_op jit(solution)/shard_map/opening/pallas_call | solution.py:135
  3.4 3.1 %conv.8 = (f32[296,384]{1,0:T(8,128)S(1)}, f32[296,384]{1,0:T(8,128)S(1)}) custom-call(bf16[304,1920]{1,0:T(8,128)(2,1)S(1)} %get-tuple-element.86.hi_ref, bf16[304,1920]{1,0:T(8,128)(2,1)S(1)} %get-tuple-element.87.lo_ref, bf16[1920,768]{1,0:T(8,128)(2,1)S(1)} %get-tuple-element.68.whi_ref, bf16[1920,768]{1,0:T(8,128)(2,1)S(1)} %get-tuple-element.69.wlo_ref), custom_call_target="tpu_custom_call" | custom-call | flops 1000000000 | tf_op jit(solution)/shard_map/conv/pallas_call | solution.py:41
  7.0 1.1 %split_own.2 = (bf16[1920,768]{1,0:T(8,128)(2,1)S(1)}, bf16[1920,768]{1,0:T(8,128)(2,1)S(1)}) custom-call(f32[5,384,1536]{2,1,0:T(8,128)S(1)} %copy-done), custom_call_target="tpu_custom_call" | custom-call | flops 1000000000 | tf_op jit(solution)/shard_map/split_own/pallas_call | solution.py:41
  8.5 2.9 %collective-permute-start.2 = (f32[8,384]{1,0:T(8,128)S(1)}, f32[8,384]{1,0:T(8,128)S(1)}, u32[]{:S(2)}, u32[]{:S(2)}) collective-permute-start(f32[8,384]{1,0:T(8,128)S(1)} %get-tuple-element.80), channel_id=1, source_target_pairs={{0,4},{4,0},{8,12},{12,8},{16,20},{20,16},{24,28},{28,24},{1,5},{5... | collective-permute-start | bytes 36872 | tf_op jit(solution)/shard_map/ppermute | solution.py:318
  11.4 0.8 %collective-permute-start.3 = (f32[8,384]{1,0:T(8,128)S(1)}, f32[8,384]{1,0:T(8,128)S(1)}, u32[]{:S(2)}, u32[]{:S(2)}) collective-permute-start(f32[8,384]{1,0:T(8,128)S(1)} %get-tuple-element.81), channel_id=1, source_target_pairs={{4,8},{8,4},{12,16},{16,12},{20,24},{24,20},{5,9},{9,5},{13,17},{1... | collective-permute-start | bytes 36872 | tf_op jit(solution)/shard_map/ppermute | solution.py:319
  12.2 1.6 %collective-permute-start.1 = (f32[296,384]{1,0:T(8,128)S(1)}, f32[296,384]{1,0:T(8,128)S(1)}, u32[]{:S(2)}, u32[]{:S(2)}) collective-permute-start(f32[296,384]{1,0:T(8,128)S(1)} %added.6), channel_id=1, source_target_pairs={{0,2},{1,3},{2,0},{3,1},{4,6},{5,7},{6,4},{7,5},{8,10},{9,11},{10,... | collective-permute-start | bytes 1363976 | tf_op jit(solution)/shard_map/ppermute | solution.py:55
  14.6 2.5 %conv.9 = (f32[232,384]{1,0:T(8,128)S(1)}, f32[232,384]{1,0:T(8,128)S(1)}) custom-call(bf16[240,1920]{1,0:T(8,128)(2,1)S(1)} %get-tuple-element.90.hi_ref, bf16[240,1920]{1,0:T(8,128)(2,1)S(1)} %get-tuple-element.91.lo_ref, bf16[1920,768]{1,0:T(8,128)(2,1)S(1)} %get-tuple-element.68.whi_ref, bf16[1920,768]{1,0:T(8,128)(2,1)S(1)} %get-tuple-element.69.wlo_ref), custom_call_target="tpu_custom_call" | custom-call | flops 30000001024 | tf_op jit(solution)/shard_map/conv/pallas_call | solution.py:41
  17.1 3.1 %conv.10 = (f32[296,384]{1,0:T(8,128)S(1)}, f32[296,384]{1,0:T(8,128)S(1)}) custom-call(bf16[304,1920]{1,0:T(8,128)(2,1)S(1)} %get-tuple-element.86.hi_ref, bf16[304,1920]{1,0:T(8,128)(2,1)S(1)} %get-tuple-element.87.lo_ref, bf16[1920,768]{1,0:T(8,128)(2,1)S(1)} %get-tuple-element.73.whi_ref, bf16[1920,768]{1,0:T(8,128)(2,1)S(1)} %get-tuple-element.74.wlo_ref), custom_call_target="tpu_custom_call" | custom-call | flops 30000001024 | tf_op jit(solution)/shard_map/conv/pallas_call | solution.py:41
  20.8 1.4 %collective-permute-start.8 = (f32[232,384]{1,0:T(8,128)S(1)}, f32[232,384]{1,0:T(8,128)S(1)}, u32[]{:S(2)}, u32[]{:S(2)}) collective-permute-start(f32[232,384]{1,0:T(8,128)S(1)} %added.7), channel_id=1, source_target_pairs={{0,2},{1,3},{2,0},{3,1},{4,6},{5,7},{6,4},{7,5},{8,10},{9,11},{10,... | collective-permute-start | bytes 1069064 | tf_op jit(solution)/shard_map/ppermute | solution.py:55
  22.2 2.5 %conv.11 = (f32[232,384]{1,0:T(8,128)S(1)}, f32[232,384]{1,0:T(8,128)S(1)}) custom-call(bf16[240,1920]{1,0:T(8,128)(2,1)S(1)} %get-tuple-element.90.hi_ref, bf16[240,1920]{1,0:T(8,128)(2,1)S(1)} %get-tuple-element.91.lo_ref, bf16[1920,768]{1,0:T(8,128)(2,1)S(1)} %get-tuple-element.73.whi_ref, bf16[1920,768]{1,0:T(8,128)(2,1)S(1)} %get-tuple-element.74.wlo_ref), custom_call_target="tpu_custom_call" | custom-call | flops 1000000000 | tf_op jit(solution)/shard_map/conv/pallas_call | solution.py:41
  24.8 1.2 %split_far.1 = (bf16[1920,768]{1,0:T(8,128)(2,1)S(1)}, bf16[1920,768]{1,0:T(8,128)(2,1)S(1)}) custom-call(f32[5,384,1536]{2,1,0:T(8,128)S(1)} %bitcast.1), custom_call_target="tpu_custom_call" | custom-call | flops 1000000000 | tf_op jit(solution)/shard_map/split_far/pallas_call | solution.py:41
  26.6 1.6 %conv.12 = (f32[144,384]{1,0:T(8,128)S(1)}, f32[144,384]{1,0:T(8,128)S(1)}) custom-call(bf16[144,1920]{1,0:T(8,128)(2,1)S(1)} %get-tuple-element.112.hi_ref, bf16[144,1920]{1,0:T(8,128)(2,1)S(1)} %get-tuple-element.113.lo_ref, bf16[1920,768]{1,0:T(8,128)(2,1)S(1)} %get-tuple-element.94.whi_ref, bf16[1920,768]{1,0:T(8,128)(2,1)S(1)} %get-tuple-element.95.wlo_ref), custom_call_target="tpu_custom_call" | custom-call | flops 1000000000 | tf_op jit(solution)/shard_map/conv/pallas_call | solution.py:41
  28.7 1.1 %split_own.3 = (bf16[1920,768]{1,0:T(8,128)(2,1)S(1)}, bf16[1920,768]{1,0:T(8,128)(2,1)S(1)}) custom-call(f32[5,384,1536]{2,1,0:T(8,128)S(1)} %bitcast.1), custom_call_target="tpu_custom_call" | custom-call | flops 1000000000 | tf_op jit(solution)/shard_map/split_own/pallas_call | solution.py:41
  29.9 1.1 %collective-permute-start.7 = (f32[144,384]{1,0:T(8,128)S(1)}, f32[144,384]{1,0:T(8,128)S(1)}, u32[]{:S(2)}, u32[]{:S(2)}) collective-permute-start(f32[144,384]{1,0:T(8,128)S(1)} %added.8), channel_id=1, source_target_pairs={{0,2},{1,3},{2,0},{3,1},{4,6},{5,7},{6,4},{7,5},{8,10},{9,11},{10,... | collective-permute-start | bytes 663560 | tf_op jit(solution)/shard_map/ppermute | solution.py:55
  31.0 1.1 %collective-permute-done.8.a_ref = f32[232,384]{1,0:T(8,128)S(1)} collective-permute-done((f32[232,384]{1,0:T(8,128)S(1)}, f32[232,384]{1,0:T(8,128)S(1)}, u32[]{:S(2)}, u32[]{:S(2)}) %collective-permute-start.8) | collective-permute-done | bytes 356384 | tf_op jit(solution)/shard_map/ppermute | solution.py:55
  32.9 1.5 %conv.13 = (f32[120,384]{1,0:T(8,128)S(1)}, f32[120,384]{1,0:T(8,128)S(1)}) custom-call(bf16[128,1920]{1,0:T(8,128)(2,1)S(1)} %get-tuple-element.118.hi_ref, bf16[128,1920]{1,0:T(8,128)(2,1)S(1)} %get-tuple-element.119.lo_ref, bf16[1920,768]{1,0:T(8,128)(2,1)S(1)} %get-tuple-element.94.whi_ref, bf16[1920,768]{1,0:T(8,128)(2,1)S(1)} %get-tuple-element.95.wlo_ref), custom_call_target="tpu_custom_call" | custom-call | flops 10000000000 | tf_op jit(solution)/shard_map/conv/pallas_call | solution.py:41
  34.5 1.6 %conv.14 = (f32[144,384]{1,0:T(8,128)S(1)}, f32[144,384]{1,0:T(8,128)S(1)}) custom-call(bf16[144,1920]{1,0:T(8,128)(2,1)S(1)} %get-tuple-element.112.hi_ref, bf16[144,1920]{1,0:T(8,128)(2,1)S(1)} %get-tuple-element.113.lo_ref, bf16[1920,768]{1,0:T(8,128)(2,1)S(1)} %get-tuple-element.103.whi_ref, bf16[1920,768]{1,0:T(8,128)(2,1)S(1)} %get-tuple-element.104.wlo_ref), custom_call_target="tpu_custom_call" | custom-call | flops 10000000000 | tf_op jit(solution)/shard_map/conv/pallas_call | solution.py:41
  36.6 1.6 %collective-permute-start.12 = (f32[120,384]{1,0:T(8,128)S(1)}, f32[120,384]{1,0:T(8,128)S(1)}, u32[]{:S(2)}, u32[]{:S(2)}) collective-permute-start(f32[120,384]{1,0:T(8,128)S(1)} %added.10), channel_id=1, source_target_pairs={{0,2},{1,3},{2,0},{3,1},{4,6},{5,7},{6,4},{7,5},{8,10},{9,11},{10,... | collective-permute-start | bytes 552968 | tf_op jit(solution)/shard_map/ppermute | solution.py:55
  38.2 1.4 %conv.15 = (f32[120,384]{1,0:T(8,128)S(1)}, f32[120,384]{1,0:T(8,128)S(1)}) custom-call(bf16[128,1920]{1,0:T(8,128)(2,1)S(1)} %get-tuple-element.118.hi_ref, bf16[128,1920]{1,0:T(8,128)(2,1)S(1)} %get-tuple-element.119.lo_ref, bf16[1920,768]{1,0:T(8,128)(2,1)S(1)} %get-tuple-element.103.whi_ref, bf16[1920,768]{1,0:T(8,128)(2,1)S(1)} %get-tuple-element.104.wlo_ref), custom_call_target="tpu_custom_call" | custom-call | flops 1000000000 | tf_op jit(solution)/shard_map/conv/pallas_call | solution.py:41
  39.7 3.5 %collective-permute-done.12.a_ref = f32[120,384]{1,0:T(8,128)S(1)} collective-permute-done((f32[120,384]{1,0:T(8,128)S(1)}, f32[120,384]{1,0:T(8,128)S(1)}, u32[]{:S(2)}, u32[]{:S(2)}) %collective-permute-start.12) | collective-permute-done | bytes 184352 | tf_op jit(solution)/shard_map/ppermute | solution.py:55
  43.5 4.1 %collective-permute-start.14 = (f32[96,128]{1,0:T(8,128)S(1)}, f32[96,128]{1,0:T(8,128)S(1)}, u32[]{:S(2)}, u32[]{:S(2)}) collective-permute-start(f32[96,128]{1,0:T(8,128)S(1)} %get-tuple-element.124), channel_id=1, source_target_pairs={{0,4},{4,0},{8,12},{12,8},{16,20},{20,16},{24,28},{28,24},{1,5},{5... | collective-permute-start | bytes 147464 | tf_op jit(solution)/shard_map/ppermute | solution.py:55
  47.6 1.6 %collective-permute-start.15 = (f32[96,128]{1,0:T(8,128)S(1)}, f32[96,128]{1,0:T(8,128)S(1)}, u32[]{:S(2)}, u32[]{:S(2)}) collective-permute-start(f32[96,128]{1,0:T(8,128)S(1)} %get-tuple-element.125), channel_id=1, source_target_pairs={{0,8},{4,12},{8,0},{12,4},{16,24},{20,28},{24,16},{28,20},{1,9},{5... | collective-permute-start | bytes 147464 | tf_op jit(solution)/shard_map/ppermute | solution.py:55
  49.7 2.2 %collective-permute-done.15.refs_2_ = f32[96,128]{1,0:T(8,128)S(1)} collective-permute-done((f32[96,128]{1,0:T(8,128)S(1)}, f32[96,128]{1,0:T(8,128)S(1)}, u32[]{:S(2)}, u32[]{:S(2)}) %collective-permute-start.15) | collective-permute-done | bytes 49184 | tf_op jit(solution)/shard_map/ppermute | solution.py:55
  51.9 2.3 %collective-permute-done.16.refs_3_ = f32[96,128]{1,0:T(8,128)S(1)} collective-permute-done((f32[96,128]{1,0:T(8,128)S(1)}, f32[96,128]{1,0:T(8,128)S(1)}, u32[]{:S(2)}, u32[]{:S(2)}) %collective-permute-start.16) | collective-permute-done | bytes 49184 | tf_op jit(solution)/shard_map/ppermute | solution.py:55
  (52 shorter events, 6.4 us)
Async XLA Ops:
  0.0 7.0 %copy-start = (f32[5,384,1536]{2,1,0:T(8,128)S(1)}, f32[5,384,1536]{2,1,0:T(8,128)}, u32[]{:S(2)}) copy-start(f32[5,384,1536]{2,1,0:T(8,128)} %w_ref) | copy-start | bytes 35389444
  6.5 2.0 %collective-permute-start = (f32[296,384]{1,0:T(8,128)S(1)}, f32[296,384]{1,0:T(8,128)S(1)}, u32[]{:S(2)}, u32[]{:S(2)}) collective-permute-start(f32[296,384]{1,0:T(8,128)S(1)} %get-tuple-element.71), channel_id=1, source_target_pairs={{0,1},{1,0},{2,3},{3,2},{4,5},{5,4},{6,7},{7,6},{8,9},{9,8},{10,11... | collective-permute-start | bytes 1363976 | tf_op jit(solution)/shard_map/ppermute | solution.py:55
  8.1 5.7 %copy-start.1 = (f32[384,512]{1,0:T(8,128)S(1)}, f32[384,512]{1,0:T(8,128)}, u32[]{:S(2)}) copy-start(f32[384,512]{1,0:T(8,128)} %x_ref) | copy-start | bytes 2359300
  8.1 5.7 %copy-start.2 = (f32[384]{0:T(512)S(1)}, f32[384]{0:T(512)}, u32[]{:S(2)}) copy-start(f32[384]{0:T(512)} %gain_ref.3) | copy-start | bytes 4612
  8.2 5.7 %copy-start.3 = (f32[384]{0:T(512)S(1)}, f32[384]{0:T(512)}, u32[]{:S(2)}) copy-start(f32[384]{0:T(512)} %shift_ref.3) | copy-start | bytes 4612
  8.5 5.4 %collective-permute-start.2 = (f32[8,384]{1,0:T(8,128)S(1)}, f32[8,384]{1,0:T(8,128)S(1)}, u32[]{:S(2)}, u32[]{:S(2)}) collective-permute-start(f32[8,384]{1,0:T(8,128)S(1)} %get-tuple-element.80), channel_id=1, source_target_pairs={{0,4},{4,0},{8,12},{12,8},{16,20},{20,16},{24,28},{28,24},{1,5},{5... | collective-permute-start | bytes 36872 | tf_op jit(solution)/shard_map/ppermute | solution.py:318
  11.4 2.4 %collective-permute-start.3 = (f32[8,384]{1,0:T(8,128)S(1)}, f32[8,384]{1,0:T(8,128)S(1)}, u32[]{:S(2)}, u32[]{:S(2)}) collective-permute-start(f32[8,384]{1,0:T(8,128)S(1)} %get-tuple-element.81), channel_id=1, source_target_pairs={{4,8},{8,4},{12,16},{16,12},{20,24},{24,20},{5,9},{9,5},{13,17},{1... | collective-permute-start | bytes 36872 | tf_op jit(solution)/shard_map/ppermute | solution.py:319
  12.2 13.7 %collective-permute-start.1 = (f32[296,384]{1,0:T(8,128)S(1)}, f32[296,384]{1,0:T(8,128)S(1)}, u32[]{:S(2)}, u32[]{:S(2)}) collective-permute-start(f32[296,384]{1,0:T(8,128)S(1)} %added.6), channel_id=1, source_target_pairs={{0,2},{1,3},{2,0},{3,1},{4,6},{5,7},{6,4},{7,5},{8,10},{9,11},{10,... | collective-permute-start | bytes 1363976 | tf_op jit(solution)/shard_map/ppermute | solution.py:55
  14.6 10.2 %slice-start = ((s8[11796480]{0:T(1024)(128)(4,1)}), s8[4194304]{0:T(1024)(128)(4,1)S(1)}, s32[]{:S(2)}) async-start(s8[11796480]{0:T(1024)(128)(4,1)} %bitcast), calls=%async_computation | async-start | bytes 8388608
  14.6 10.2 %slice-start.1 = ((s8[11796480]{0:T(1024)(128)(4,1)}), s8[4194304]{0:T(1024)(128)(4,1)S(1)}, s32[]{:S(2)}) async-start(s8[11796480]{0:T(1024)(128)(4,1)} %bitcast), calls=%async_computation.1 | async-start | bytes 8388608
  17.0 7.7 %slice-start.2 = ((s8[11796480]{0:T(1024)(128)(4,1)}), s8[3407872]{0:T(1024)(128)(4,1)S(1)}, s32[]{:S(2)}) async-start(s8[11796480]{0:T(1024)(128)(4,1)} %bitcast), calls=%async_computation.2 | async-start | bytes 6815744
  17.1 3.7 %collective-permute-start.4 = (f32[232,384]{1,0:T(8,128)S(1)}, f32[232,384]{1,0:T(8,128)S(1)}, u32[]{:S(2)}, u32[]{:S(2)}) collective-permute-start(f32[232,384]{1,0:T(8,128)S(1)} %get-tuple-element.85), channel_id=1, source_target_pairs={{0,1},{1,0},{2,3},{3,2},{4,5},{5,4},{6,7},{7,6},{8,9},{9,8},{10,11... | collective-permute-start | bytes 1069064 | tf_op jit(solution)/shard_map/ppermute | solution.py:55
  20.2 5.8 %collective-permute-start.5 = (f32[296,384]{1,0:T(8,128)S(1)}, f32[296,384]{1,0:T(8,128)S(1)}, u32[]{:S(2)}, u32[]{:S(2)}) collective-permute-start(f32[296,384]{1,0:T(8,128)S(1)} %get-tuple-element.97), channel_id=1, source_target_pairs={{0,1},{1,0},{2,3},{3,2},{4,5},{5,4},{6,7},{7,6},{8,9},{9,8},{10,11... | collective-permute-start | bytes 1363976 | tf_op jit(solution)/shard_map/ppermute | solution.py:55
  20.8 11.3 %collective-permute-start.8 = (f32[232,384]{1,0:T(8,128)S(1)}, f32[232,384]{1,0:T(8,128)S(1)}, u32[]{:S(2)}, u32[]{:S(2)}) collective-permute-start(f32[232,384]{1,0:T(8,128)S(1)} %added.7), channel_id=1, source_target_pairs={{0,2},{1,3},{2,0},{3,1},{4,6},{5,7},{6,4},{7,5},{8,10},{9,11},{10,... | collective-permute-start | bytes 1069064 | tf_op jit(solution)/shard_map/ppermute | solution.py:55
  24.7 7.5 %collective-permute-start.9 = (f32[232,384]{1,0:T(8,128)S(1)}, f32[232,384]{1,0:T(8,128)S(1)}, u32[]{:S(2)}, u32[]{:S(2)}) collective-permute-start(f32[232,384]{1,0:T(8,128)S(1)} %get-tuple-element.107), channel_id=1, source_target_pairs={{0,1},{1,0},{2,3},{3,2},{4,5},{5,4},{6,7},{7,6},{8,9},{9,8},{10,11... | collective-permute-start | bytes 1069064 | tf_op jit(solution)/shard_map/ppermute | solution.py:55
  28.2 1.7 %collective-permute-start.6 = (f32[144,384]{1,0:T(8,128)S(1)}, f32[144,384]{1,0:T(8,128)S(1)}, u32[]{:S(2)}, u32[]{:S(2)}) collective-permute-start(f32[144,384]{1,0:T(8,128)S(1)} %get-tuple-element.101), channel_id=1, source_target_pairs={{0,1},{1,0},{2,3},{3,2},{4,5},{5,4},{6,7},{7,6},{8,9},{9,8},{10,11... | collective-permute-start | bytes 663560 | tf_op jit(solution)/shard_map/ppermute | solution.py:55
  29.9 8.3 %collective-permute-start.7 = (f32[144,384]{1,0:T(8,128)S(1)}, f32[144,384]{1,0:T(8,128)S(1)}, u32[]{:S(2)}, u32[]{:S(2)}) collective-permute-start(f32[144,384]{1,0:T(8,128)S(1)} %added.8), channel_id=1, source_target_pairs={{0,2},{1,3},{2,0},{3,1},{4,6},{5,7},{6,4},{7,5},{8,10},{9,11},{10,... | collective-permute-start | bytes 663560 | tf_op jit(solution)/shard_map/ppermute | solution.py:55
  34.4 2.2 %collective-permute-start.11 = (f32[120,384]{1,0:T(8,128)S(1)}, f32[120,384]{1,0:T(8,128)S(1)}, u32[]{:S(2)}, u32[]{:S(2)}) collective-permute-start(f32[120,384]{1,0:T(8,128)S(1)} %get-tuple-element.111), channel_id=1, source_target_pairs={{0,1},{1,0},{2,3},{3,2},{4,5},{5,4},{6,7},{7,6},{8,9},{9,8},{10,11... | collective-permute-start | bytes 552968 | tf_op jit(solution)/shard_map/ppermute | solution.py:55
  36.0 3.6 %collective-permute-start.10 = (f32[144,384]{1,0:T(8,128)S(1)}, f32[144,384]{1,0:T(8,128)S(1)}, u32[]{:S(2)}, u32[]{:S(2)}) collective-permute-start(f32[144,384]{1,0:T(8,128)S(1)} %get-tuple-element.115), channel_id=1, source_target_pairs={{0,1},{1,0},{2,3},{3,2},{4,5},{5,4},{6,7},{7,6},{8,9},{9,8},{10,11... | collective-permute-start | bytes 663560 | tf_op jit(solution)/shard_map/ppermute | solution.py:55
  36.6 6.6 %collective-permute-start.12 = (f32[120,384]{1,0:T(8,128)S(1)}, f32[120,384]{1,0:T(8,128)S(1)}, u32[]{:S(2)}, u32[]{:S(2)}) collective-permute-start(f32[120,384]{1,0:T(8,128)S(1)} %added.10), channel_id=1, source_target_pairs={{0,2},{1,3},{2,0},{3,1},{4,6},{5,7},{6,4},{7,5},{8,10},{9,11},{10,... | collective-permute-start | bytes 552968 | tf_op jit(solution)/shard_map/ppermute | solution.py:55
  39.6 3.7 %collective-permute-start.13 = (f32[120,384]{1,0:T(8,128)S(1)}, f32[120,384]{1,0:T(8,128)S(1)}, u32[]{:S(2)}, u32[]{:S(2)}) collective-permute-start(f32[120,384]{1,0:T(8,128)S(1)} %get-tuple-element.121), channel_id=1, source_target_pairs={{0,1},{1,0},{2,3},{3,2},{4,5},{5,4},{6,7},{7,6},{8,9},{9,8},{10,11... | collective-permute-start | bytes 552968 | tf_op jit(solution)/shard_map/ppermute | solution.py:55
  43.5 6.1 %collective-permute-start.14 = (f32[96,128]{1,0:T(8,128)S(1)}, f32[96,128]{1,0:T(8,128)S(1)}, u32[]{:S(2)}, u32[]{:S(2)}) collective-permute-start(f32[96,128]{1,0:T(8,128)S(1)} %get-tuple-element.124), channel_id=1, source_target_pairs={{0,4},{4,0},{8,12},{12,8},{16,20},{20,16},{24,28},{28,24},{1,5},{5... | collective-permute-start | bytes 147464 | tf_op jit(solution)/shard_map/ppermute | solution.py:55
  47.6 4.3 %collective-permute-start.15 = (f32[96,128]{1,0:T(8,128)S(1)}, f32[96,128]{1,0:T(8,128)S(1)}, u32[]{:S(2)}, u32[]{:S(2)}) collective-permute-start(f32[96,128]{1,0:T(8,128)S(1)} %get-tuple-element.125), channel_id=1, source_target_pairs={{0,8},{4,12},{8,0},{12,4},{16,24},{20,28},{24,16},{28,20},{1,9},{5... | collective-permute-start | bytes 147464 | tf_op jit(solution)/shard_map/ppermute | solution.py:55
  49.2 5.0 %collective-permute-start.16 = (f32[96,128]{1,0:T(8,128)S(1)}, f32[96,128]{1,0:T(8,128)S(1)}, u32[]{:S(2)}, u32[]{:S(2)}) collective-permute-start(f32[96,128]{1,0:T(8,128)S(1)} %get-tuple-element.126), channel_id=1, source_target_pairs={{0,12},{4,8},{8,4},{12,0},{16,28},{20,24},{24,20},{28,16},{1,13},{... | collective-permute-start | bytes 147464 | tf_op jit(solution)/shard_map/ppermute | solution.py:55
  (2 other events, 2.7 us)
